TPU v7x, 32 devices: a whole 2x2x4 slice. The times are simulated.
32 devices in a mesh: gx: 8 (over z, x), gy: 4 (over y, core).
Axes of the slice: x: 2, y: 2, z: 4, core: 2. Of those that a mesh axis runs over, the one named last changes fastest.
Arguments:
- charges: float32 [192, 256, 128], P('gx', 'gy'), may hold values from -4 to 4
- kernel_fine: bfloat16 [15, 15, 15], replicated, may hold values from 0 to 1
- kernel_mid: bfloat16 [15, 15, 15], replicated, may hold values from 0 to 1
- kernel_top: bfloat16 [15, 15, 15], replicated, may hold values from 0 to 1
Outputs:
- potential: float32 [192, 256, 128], P('gx', 'gy')
All inputs are finite; a program needn't handle non-finite values.
Results may differ from a plain program's by a relative error of at most 0.0035.
Values may be sent and summed in bfloat16 or wider, within the bound.
No kernel may reach another device: no remote copies, remote signals or barrier semaphores. Data moves between devices by JAX's collectives and lax.ppermute only.
A program may use at most 256 MiB of HBM per device.

v0:
```python
import jax
import jax.numpy as jnp
from jax import lax
from jax.sharding import PartitionSpec as P


def from_behind(value, axis, by):
    length = lax.axis_size(axis)
    pairs = [(i, i + by) for i in range(length) if 0 <= i + by < length]
    return lax.ppermute(value, axis, pairs)


def padded(cells, sides, width):
    for axis, dim in sides:
        count = lax.axis_size(axis)
        ends = count - 1
        head = lax.slice_in_dim(cells, 0, width, axis=dim)
        tail = lax.slice_in_dim(cells, cells.shape[dim] - width, cells.shape[dim], axis=dim)
        cells = jnp.concatenate(
            [
                lax.ppermute(tail, axis, [(i, (i + 1) % count) for i in range(ends)]),
                cells,
                lax.ppermute(head, axis, [((i + 1) % count, i) for i in range(ends)]),
            ],
            axis=dim,
        )
    return cells


def restrict_axis(values, axis, count):
    left_part = lax.slice_in_dim(values, 0, 2 * count, 2, axis)
    middle_part = lax.slice_in_dim(values, 1, 2 * count, 2, axis)
    right_part = lax.slice_in_dim(values, 2, 2 * count + 1, 2, axis)
    return 0.5 * left_part + middle_part + 0.5 * right_part


def restrict(extended, start, count_x, count_y):
    layer_count = extended.shape[2]
    values = extended[start : start + 2 * count_x + 1, start : start + 2 * count_y + 1, :].astype(
        jnp.float32
    )
    values = jnp.pad(values, ((0, 0), (0, 0), (1, 0)))
    values = restrict_axis(values, 0, count_x)
    values = restrict_axis(values, 1, count_y)
    return restrict_axis(values, 2, layer_count // 2)


def prolong_axis(values, axis, count):
    first_part = lax.slice_in_dim(values, 0, count, 1, axis)
    second_part = lax.slice_in_dim(values, 1, count + 1, 1, axis)
    middle_part = 0.5 * (first_part + second_part)
    joined = jnp.stack((first_part, middle_part), axis=axis + 1)
    new_shape = list(values.shape)
    new_shape[axis] = 2 * count
    return joined.reshape(new_shape)


def interpolate(coarse):
    count_x, count_y, layer_count = coarse.shape
    next_row = from_behind(coarse[:1], "gx", -1)
    widened = jnp.concatenate((coarse, next_row), axis=0)
    next_column = from_behind(widened[:, :1], "gy", -1)
    widened = jnp.concatenate((widened, next_column), axis=1)
    widened = jnp.pad(widened, ((0, 0), (0, 0), (0, 1)))
    widened = prolong_axis(widened, 0, count_x)
    widened = prolong_axis(widened, 1, count_y)
    return prolong_axis(widened, 2, layer_count)


def with_margin(field):
    return padded(field, (("gx", 0), ("gy", 1)), 7)


def correlate(extended, kernel):
    row_count = extended.shape[0] - 14
    col_count = extended.shape[1] - 14
    layer_count = extended.shape[2]
    tile_width = min(max(1, 256 // layer_count), col_count)
    block_count = col_count // tile_width
    span_width = tile_width + 14
    stacked = jnp.stack(
        [
            lax.slice_in_dim(
                extended, column, column + tile_width * (block_count - 1) + 1, tile_width, 1
            )
            for column in range(span_width)
        ],
        axis=2,
    )
    stacked = stacked.reshape(row_count + 14, block_count, span_width * layer_count)
    offsets = jnp.arange(15)
    pick_y = (
        jnp.arange(span_width)[None, :, None] - jnp.arange(tile_width)[None, None, :]
        == offsets[:, None, None]
    ).astype(jnp.bfloat16)
    pick_z = (
        jnp.arange(layer_count)[None, :, None] - jnp.arange(layer_count)[None, None, :] + 7
        == offsets[:, None, None]
    ).astype(jnp.bfloat16)
    partial_z = jnp.einsum("abc,cwz->abwz", kernel, pick_z)
    weights_all = jnp.einsum("abwz,bji->ajwiz", partial_z, pick_y)
    weights_all = weights_all.reshape(15, span_width * layer_count, tile_width * layer_count)

    def accumulate(offset_x, total):
        weights = lax.dynamic_index_in_dim(weights_all, offset_x, 0, keepdims=False)
        window = lax.dynamic_slice_in_dim(stacked, offset_x, row_count, 0)
        window = window.reshape(row_count * block_count, span_width * layer_count)
        return total + jnp.dot(window, weights, preferred_element_type=jnp.float32)

    initial = jnp.zeros((row_count * block_count, tile_width * layer_count), jnp.float32)
    total = lax.fori_loop(0, 15, accumulate, initial)
    return total.reshape(row_count, block_count, tile_width, layer_count).reshape(
        row_count, col_count, layer_count
    )


def nearby_coarse(top_cells, quarter_x):
    side_ext = padded(top_cells, (("gy", 1),), 7)
    reach = (quarter_x + 6) // quarter_x
    distances = list(range(reach, 0, -1)) + list(range(-1, -reach - 1, -1))
    pieces = {}
    for distance in distances:
        pieces[distance] = from_behind(side_ext, "gx", distance)
    ordered = (
        [pieces[distance] for distance in range(reach, 0, -1)]
        + [side_ext]
        + [pieces[distance] for distance in range(-1, -reach - 1, -1)]
    )
    joined = jnp.concatenate(ordered, axis=0)
    return joined[reach * quarter_x - 7 : (reach + 1) * quarter_x + 7]


def shards(charges, kernel_fine, kernel_mid, kernel_top):
    size_x, size_y, layer_count = charges.shape
    half_x, half_y = (size_x // 2, size_y // 2)
    quarter_x, quarter_y = (size_x // 4, size_y // 4)
    fine_cells = charges.astype(jnp.bfloat16)
    fine_ext = with_margin(fine_cells)
    mid_cells = restrict(fine_ext, 6, half_x, half_y).astype(jnp.bfloat16)
    mid_ext = with_margin(mid_cells)
    top_cells = restrict(mid_ext, 6, quarter_x, quarter_y).astype(jnp.bfloat16)
    top_ext = nearby_coarse(top_cells, quarter_x)
    fine_pot = correlate(fine_ext, kernel_fine)
    mid_pot = correlate(mid_ext, kernel_mid)
    top_pot = correlate(top_ext, kernel_top)
    mid_total = mid_pot + interpolate(top_pot)
    return fine_pot + interpolate(mid_total)


def solution(mesh):
    placed = (P("gx", "gy", None), P(), P(), P())
    return jax.shard_map(
        shards, mesh=mesh, in_specs=placed, out_specs=P("gx", "gy", None), check_vma=False
    )
```

profile of v0, /device:TPU:8, one launch (start us, length us, event | category | flops | bytes accessed | tf_op | source)
XLA Modules:
  0.0 431.6 jit_solution(14956045009997581033)
XLA Ops:
  1.2 3.4 collective-permute-start
  4.6 3.3 collective-permute-start.1
  8.1 12.0 %convolution_bitcast_fusion.2 = bf16[15,18,64,4,64]{4,1,2,0,3:T(8,128)(2,1)} fusion(s32[64,64]{1,0:T(8,128)S(1)} %subtract_add_fusion.1, bf16[15,15,15]{2,1,0:T(8,128)(2,1)} %param.12, s32[18,4]{0,1:T(4,128)S(1)} %iota_subtract_fusion.1), kind=kOutput, calls=%fused_computation.18 | convolution fusion | flops 160420928 | bytes 8870782 | tf_op jit(solution)/shard_map/abwz,bji->ajwiz/dot_general | solution.py:101
  20.1 10.6 %convolution_bitcast_fusion.1 = bf16[15,22,32,8,32]{4,1,2,0,3:T(8,128)(2,1)} fusion(s32[32,32]{1,0:T(8,128)S(1)} %subtract_add_fusion.2, bf16[15,15,15]{2,1,0:T(8,128)(2,1)S(1)} %copy-done.10, s32[22,8]{0,1:T(8,128)S(1)} %iota_subtract_fusion), kind=kOutput, calls=%fused_computation.17 | convolution fusion | flops 88030800 | bytes 5418270 | tf_op jit(solution)/shard_map/abwz,bji->ajwiz/dot_general | solution.py:101
  33.7 9.1 %convolution_bitcast_fusion = bf16[15,16,128,2,128]{4,1,2,0,3:T(8,128)(2,1)} fusion(s32[128,128]{1,0:T(8,128)S(1)} %subtract_add_fusion, bf16[15,15,15]{2,1,0:T(8,128)(2,1)S(1)} %copy-done, s32[16,2]{0,1:T(2,128)S(1)} %iota_subtract_fusion.2), kind=kOutput, calls=%fused_computation.16 | convolution fusion | flops 346767840 | bytes 15801054 | tf_op jit(solution)/shard_map/abwz,bji->ajwiz/dot_general | solution.py:101
  42.7 29.2 %copy.51 = bf16[15,16,128,2,128]{4,3,2,1,0:T(2,128)(2,1)} copy(bf16[15,16,128,2,128]{4,1,2,0,3:T(8,128)(2,1)} %convolution_bitcast_fusion) | data formatting | bytes 31457280
  72.0 25.3 %reshape.181 = bf16[15,2048,256]{2,1,0:T(8,128)(2,1)} reshape(bf16[15,16,128,2,128]{4,3,2,1,0:T(2,128)(2,1)} %copy.51) | data formatting | bytes 31457280
  97.3 17.8 %copy.30 = bf16[15,18,64,4,64]{4,3,2,1,0:T(4,128)(2,1)} copy(bf16[15,18,64,4,64]{4,1,2,0,3:T(8,128)(2,1)} %convolution_bitcast_fusion.2) | data formatting | bytes 17694720 | tf_op jit(solution)/shard_map/abwz,bji->ajwiz/transpose | solution.py:101
  115.0 25.5 %reshape.157 = bf16[15,1152,256]{2,1,0:T(8,128)(2,1)} reshape(bf16[15,18,64,4,64]{4,3,2,1,0:T(4,128)(2,1)} %copy.30) | data formatting | bytes 17694720 | tf_op jit(solution)/shard_map/reshape | solution.py:102
  140.6 23.8 %copy.32 = bf16[15,22,32,8,32]{4,3,2,1,0:T(8,128)(2,1)} copy(bf16[15,22,32,8,32]{4,1,2,0,3:T(8,128)(2,1)} %convolution_bitcast_fusion.1) | data formatting | bytes 10813440 | tf_op jit(solution)/shard_map/abwz,bji->ajwiz/transpose | solution.py:101
  164.4 25.8 %reshape.159 = bf16[15,704,256]{2,1,0:T(8,128)(2,1)} reshape(bf16[15,22,32,8,32]{4,3,2,1,0:T(8,128)(2,1)} %copy.32) | data formatting | bytes 10813440 | tf_op jit(solution)/shard_map/reshape | solution.py:102
  223.3 3.7 slice.343
  227.0 3.5 slice.342
  230.4 4.0 slice.341
  235.5 2.5 collective-permute-start.4
  238.1 4.2 collective-permute-start.5
  261.2 4.2 collective-permute-start.6
  272.7 4.7 %collective-permute-start.8 = (bf16[6,7,32]{2,1,0:T(8,128)(2,1)S(1)}, bf16[6,7,32]{2,1,0:T(8,128)(2,1)S(1)}, u32[]{:S(2)}, u32[]{:S(2)}) collective-permute-start(bf16[6,7,32]{2,1,0:T(8,128)(2,1)S(1)} %get-tuple-element.342), channel_id=1, source_target_pairs={{0,1},{1,2},{2,3},{4,5},{5,6},{6,7},{8,9},{9,10},{10,11},{12,13},{... | collective-permute-start | bytes 8072 | tf_op jit(solution)/shard_map/ppermute | solution.py:21
  280.5 3.5 collective-permute-start.10
  288.4 3.9 collective-permute-start.11
  292.3 3.0 collective-permute-done.11
  297.3 18.2 %while.44 = (s32[]{:T(128)}, f32[12,256]{1,0:T(8,128)S(1)}, bf16[20,2,704]{2,1,0:T(2,128)(2,1)S(1)}, bf16[15,704,256]{2,1,0:T(8,128)(2,1)}, s32[]{:T(128)}, /*index=5*/s32[]{:T(128)}) while((s32[]{:T(128)}, f32[12,256]{1,0:T(8,128)S(1)}, bf16[20,2,704]{2,1,0:T(2,128)(2,1)S(1)}, bf16[15,704,256]{2,1,0:T(8,128)(2,1)}, s32[]{:T(128)}, ...), condition=%wide.region_5.6_spmd.clone, body=%wide.region_4.5_spmd.clone.sunk | while | flops 4331523 | bytes 469599 | solution.py:111
  318.6 2.6 collective-permute-done.14
  322.5 20.4 %while.43 = (s32[]{:T(128)}, f32[96,256]{1,0:T(8,128)S(1)}, bf16[26,8,1152]{2,1,0:T(8,128)(2,1)S(1)}, bf16[15,1152,256]{2,1,0:T(8,128)(2,1)}, s32[]{:T(128)}, /*index=5*/s32[]{:T(128)}) while((s32[]{:T(128)}, f32[96,256]{1,0:T(8,128)S(1)}, bf16[26,8,1152]{2,1,0:T(8,128)(2,1)S(1)}, bf16[15,1152,256]{2,1,0:T(8,128)(2,1)}, s32[]{:T(128)}, ...), condition=%wide.region_3.4_spmd.clone, body=%wide.region_2.3_spmd.clone.sunk | while | flops 56672256 | bytes 1009238 | solution.py:111
  344.2 3.0 collective-permute-start.16
  347.1 5.4 %copy_bitcast_fusion = bf16[38,32,2048]{2,1,0:T(8,128)(2,1)} fusion(bf16[38,32,16,128]{3,1,0,2:T(8,128)(2,1)} %bitcast_dynamic-update-slice_fusion), kind=kLoop, calls=%fused_computation.20 | loop fusion | bytes 9961472 | tf_op jit(solution)/shard_map/reshape | solution.py:90
  353.9 72.2 %while.42 = (s32[]{:T(128)}, f32[768,256]{1,0:T(8,128)S(1)}, bf16[38,32,2048]{2,1,0:T(8,128)(2,1)}, bf16[15,2048,256]{2,1,0:T(8,128)(2,1)}, s32[]{:T(128)}, /*index=5*/s32[]{:T(128)}) while((s32[]{:T(128)}, f32[768,256]{1,0:T(8,128)S(1)}, bf16[38,32,2048]{2,1,0:T(8,128)(2,1)}, bf16[15,2048,256]{2,1,0:T(8,128)(2,1)}, s32[]{:T(128)}, ...), condition=%wide.region_1.2_spmd.clone, body=%wide.region_0.1_spmd.clone.sunk | while | flops 805699584 | bytes 12058719 | solution.py:111
  356.2 2.5 convolution_add_fusion.6
  361.0 2.5 convolution_add_fusion.6
  375.4 2.5 convolution_add_fusion.6
  385.1 2.5 convolution_add_fusion.6
  394.7 2.5 convolution_add_fusion.6
  (326 shorter events, 182.6 us)
Async XLA Ops:
  0.0 33.6 %copy-start = (bf16[15,15,15]{2,1,0:T(8,128)(2,1)S(1)}, bf16[15,15,15]{2,1,0:T(8,128)(2,1)}, u32[]{:S(2)}) copy-start(bf16[15,15,15]{2,1,0:T(8,128)(2,1)} %param.11) | copy-start | bytes 20254
  1.2 29.5 %collective-permute-start = (bf16[7,64,128]{2,1,0:T(8,128)(2,1)S(1)}, bf16[7,64,128]{2,1,0:T(8,128)(2,1)S(1)}, u32[]{:S(2)}, u32[]{:S(2)}) collective-permute-start(bf16[7,64,128]{2,1,0:T(8,128)(2,1)S(1)} %get-tuple-element.328), channel_id=1, source_target_pairs={{0,4},{4,8},{8,12},{12,16},{16,20},{20,24},{24,28},{1,5},{5,9},{9,... | collective-permute-start | bytes 344072 | tf_op jit(solution)/shard_map/ppermute | solution.py:21
  4.6 26.1 %collective-permute-start.1 = (bf16[7,64,128]{2,1,0:T(8,128)(2,1)S(1)}, bf16[7,64,128]{2,1,0:T(8,128)(2,1)S(1)}, u32[]{:S(2)}, u32[]{:S(2)}) collective-permute-start(bf16[7,64,128]{2,1,0:T(8,128)(2,1)S(1)} %get-tuple-element.329), channel_id=1, source_target_pairs={{4,0},{8,4},{12,8},{16,12},{20,16},{24,20},{28,24},{5,1},{9,5},{13... | collective-permute-start | bytes 344072 | tf_op jit(solution)/shard_map/ppermute | solution.py:23
  8.0 12.0 %copy-start.10 = (bf16[15,15,15]{2,1,0:T(8,128)(2,1)S(1)}, bf16[15,15,15]{2,1,0:T(8,128)(2,1)}, u32[]{:S(2)}) copy-start(bf16[15,15,15]{2,1,0:T(8,128)(2,1)} %param.13) | copy-start | bytes 20254
  30.9 163.8 %collective-permute-start.2 = (bf16[38,7,128]{2,1,0:T(8,128)(2,1)S(1)}, bf16[38,7,128]{2,1,0:T(8,128)(2,1)S(1)}, u32[]{:S(2)}, u32[]{:S(2)}) collective-permute-start(bf16[38,7,128]{2,1,0:T(8,128)(2,1)S(1)} %get-tuple-element.324), channel_id=1, source_target_pairs={{0,1},{1,2},{2,3},{4,5},{5,6},{6,7},{8,9},{9,10},{10,11},{12,13},{... | collective-permute-start | bytes 204296 | tf_op jit(solution)/shard_map/ppermute | solution.py:21
  32.2 162.5 %collective-permute-start.3 = (bf16[38,7,128]{2,1,0:T(8,128)(2,1)S(1)}, bf16[38,7,128]{2,1,0:T(8,128)(2,1)S(1)}, u32[]{:S(2)}, u32[]{:S(2)}) collective-permute-start(bf16[38,7,128]{2,1,0:T(8,128)(2,1)S(1)} %get-tuple-element.325), channel_id=1, source_target_pairs={{1,0},{2,1},{3,2},{5,4},{6,5},{7,6},{9,8},{10,9},{11,10},{13,12},{... | collective-permute-start | bytes 204296 | tf_op jit(solution)/shard_map/ppermute | solution.py:23
  223.2 31.1 %copy-start.5 = (bf16[38,32,128]{2,1,0:T(8,128)(2,1)S(1)}, bf16[38,32,128]{2,1,0:T(8,128)(2,1)}, u32[]{:S(2)}) copy-start(bf16[38,32,128]{2,1,0:T(8,128)(2,1)} %slice.325) | copy-start | bytes 933892
  223.3 31.8 %copy-start.3 = (bf16[38,32,128]{2,1,0:T(8,128)(2,1)S(1)}, bf16[38,32,128]{2,1,0:T(8,128)(2,1)}, u32[]{:S(2)}) copy-start(bf16[38,32,128]{2,1,0:T(8,128)(2,1)} %slice.326) | copy-start | bytes 933892
  223.3 34.8 %copy-start.4 = (bf16[38,32,128]{2,1,0:T(8,128)(2,1)S(1)}, bf16[38,32,128]{2,1,0:T(8,128)(2,1)}, u32[]{:S(2)}) copy-start(bf16[38,32,128]{2,1,0:T(8,128)(2,1)} %slice.330) | copy-start | bytes 933892
  227.0 31.9 %copy-start.2 = (bf16[38,32,128]{2,1,0:T(8,128)(2,1)S(1)}, bf16[38,32,128]{2,1,0:T(8,128)(2,1)}, u32[]{:S(2)}) copy-start(bf16[38,32,128]{2,1,0:T(8,128)(2,1)} %slice.331) | copy-start | bytes 933892
  234.5 21.4 %copy-start.8 = (bf16[38,32,128]{2,1,0:T(8,128)(2,1)S(1)}, bf16[38,32,128]{2,1,0:T(8,128)(2,1)}, u32[]{:S(2)}) copy-start(bf16[38,32,128]{2,1,0:T(8,128)(2,1)} %slice.327) | copy-start | bytes 933892
  234.5 22.1 %copy-start.7 = (bf16[38,32,128]{2,1,0:T(8,128)(2,1)S(1)}, bf16[38,32,128]{2,1,0:T(8,128)(2,1)}, u32[]{:S(2)}) copy-start(bf16[38,32,128]{2,1,0:T(8,128)(2,1)} %slice.328) | copy-start | bytes 933892
  234.5 22.9 %copy-start.6 = (bf16[38,32,128]{2,1,0:T(8,128)(2,1)S(1)}, bf16[38,32,128]{2,1,0:T(8,128)(2,1)}, u32[]{:S(2)}) copy-start(bf16[38,32,128]{2,1,0:T(8,128)(2,1)} %slice.329) | copy-start | bytes 933892
  235.5 25.5 %collective-permute-start.4 = (bf16[7,32,64]{2,1,0:T(8,128)(2,1)S(1)}, bf16[7,32,64]{2,1,0:T(8,128)(2,1)S(1)}, u32[]{:S(2)}, u32[]{:S(2)}) collective-permute-start(bf16[7,32,64]{2,1,0:T(8,128)(2,1)S(1)} %get-tuple-element.338), channel_id=1, source_target_pairs={{0,4},{4,8},{8,12},{12,16},{16,20},{20,24},{24,28},{1,5},{5,9},{9,... | collective-permute-start | bytes 86024 | tf_op jit(solution)/shard_map/ppermute | solution.py:21
  238.1 23.0 %collective-permute-start.5 = (bf16[7,32,64]{2,1,0:T(8,128)(2,1)S(1)}, bf16[7,32,64]{2,1,0:T(8,128)(2,1)S(1)}, u32[]{:S(2)}, u32[]{:S(2)}) collective-permute-start(bf16[7,32,64]{2,1,0:T(8,128)(2,1)S(1)} %get-tuple-element.339), channel_id=1, source_target_pairs={{4,0},{8,4},{12,8},{16,12},{20,16},{24,20},{28,24},{5,1},{9,5},{13... | collective-permute-start | bytes 86024 | tf_op jit(solution)/shard_map/ppermute | solution.py:23
  261.2 6.6 %collective-permute-start.6 = (bf16[26,7,64]{2,1,0:T(8,128)(2,1)S(1)}, bf16[26,7,64]{2,1,0:T(8,128)(2,1)S(1)}, u32[]{:S(2)}, u32[]{:S(2)}) collective-permute-start(bf16[26,7,64]{2,1,0:T(8,128)(2,1)S(1)} %get-tuple-element.332), channel_id=1, source_target_pairs={{0,1},{1,2},{2,3},{4,5},{5,6},{6,7},{8,9},{9,10},{10,11},{12,13},{... | collective-permute-start | bytes 69896 | tf_op jit(solution)/shard_map/ppermute | solution.py:21
  266.5 4.9 %collective-permute-start.7 = (bf16[26,7,64]{2,1,0:T(8,128)(2,1)S(1)}, bf16[26,7,64]{2,1,0:T(8,128)(2,1)S(1)}, u32[]{:S(2)}, u32[]{:S(2)}) collective-permute-start(bf16[26,7,64]{2,1,0:T(8,128)(2,1)S(1)} %get-tuple-element.333), channel_id=1, source_target_pairs={{1,0},{2,1},{3,2},{5,4},{6,5},{7,6},{9,8},{10,9},{11,10},{13,12},{... | collective-permute-start | bytes 69896 | tf_op jit(solution)/shard_map/ppermute | solution.py:23
  272.7 6.4 %collective-permute-start.8 = (bf16[6,7,32]{2,1,0:T(8,128)(2,1)S(1)}, bf16[6,7,32]{2,1,0:T(8,128)(2,1)S(1)}, u32[]{:S(2)}, u32[]{:S(2)}) collective-permute-start(bf16[6,7,32]{2,1,0:T(8,128)(2,1)S(1)} %get-tuple-element.342), channel_id=1, source_target_pairs={{0,1},{1,2},{2,3},{4,5},{5,6},{6,7},{8,9},{9,10},{10,11},{12,13},{... | collective-permute-start | bytes 8072 | tf_op jit(solution)/shard_map/ppermute | solution.py:21
  277.4 3.1 collective-permute-start.9
  280.5 11.8 %collective-permute-start.10 = (bf16[6,30,32]{2,1,0:T(8,128)(2,1)S(1)}, bf16[6,30,32]{2,1,0:T(8,128)(2,1)S(1)}, u32[]{:S(2)}, u32[]{:S(2)}) collective-permute-start(bf16[6,30,32]{2,1,0:T(8,128)(2,1)S(1)} %pad_maximum_fusion.10), channel_id=1, source_target_pairs={{0,8},{4,12},{8,16},{12,20},{16,24},{20,28},{1,9},{5,13},{9,17},{1... | collective-permute-start | bytes 34568 | tf_op jit(solution)/shard_map/ppermute | solution.py:10
  284.1 11.4 %collective-permute-start.13 = (bf16[6,30,32]{2,1,0:T(8,128)(2,1)S(1)}, bf16[6,30,32]{2,1,0:T(8,128)(2,1)S(1)}, u32[]{:S(2)}, u32[]{:S(2)}) collective-permute-start(bf16[6,30,32]{2,1,0:T(8,128)(2,1)S(1)} %pad_maximum_fusion.10), channel_id=1, source_target_pairs={{8,0},{12,4},{16,8},{20,12},{24,16},{28,20},{9,1},{13,5},{17,9},{2... | collective-permute-start | bytes 34568 | tf_op jit(solution)/shard_map/ppermute | solution.py:10
  286.5 9.0 %collective-permute-start.12 = (bf16[6,30,32]{2,1,0:T(8,128)(2,1)S(1)}, bf16[6,30,32]{2,1,0:T(8,128)(2,1)S(1)}, u32[]{:S(2)}, u32[]{:S(2)}) collective-permute-start(bf16[6,30,32]{2,1,0:T(8,128)(2,1)S(1)} %pad_maximum_fusion.10), channel_id=1, source_target_pairs={{4,0},{8,4},{12,8},{16,12},{20,16},{24,20},{28,24},{5,1},{9,5},{13... | collective-permute-start | bytes 34568 | tf_op jit(solution)/shard_map/ppermute | solution.py:10
  288.4 7.0 %collective-permute-start.11 = (bf16[6,30,32]{2,1,0:T(8,128)(2,1)S(1)}, bf16[6,30,32]{2,1,0:T(8,128)(2,1)S(1)}, u32[]{:S(2)}, u32[]{:S(2)}) collective-permute-start(bf16[6,30,32]{2,1,0:T(8,128)(2,1)S(1)} %pad_maximum_fusion.10), channel_id=1, source_target_pairs={{0,4},{4,8},{8,12},{12,16},{16,20},{20,24},{24,28},{1,5},{5,9},{9,... | collective-permute-start | bytes 34568 | tf_op jit(solution)/shard_map/ppermute | solution.py:10
  315.6 5.5 %collective-permute-start.14 = (f32[1,16,32]{2,0,1:T(1,128)S(1)}, f32[1,16,32]{2,0,1:T(1,128)S(1)}, u32[]{:S(2)}, u32[]{:S(2)}) collective-permute-start(f32[1,16,32]{2,0,1:T(1,128)S(1)} %bitcast.252), channel_id=1, source_target_pairs={{4,0},{8,4},{12,8},{16,12},{20,16},{24,20},{28,24},{5,1},{9,5},{13... | collective-permute-start | bytes 6152 | tf_op jit(solution)/shard_map/ppermute | solution.py:10
  321.2 21.8 %collective-permute-start.15 = (f32[7,1,32]{2,0,1:T(8,128)S(1)}, f32[7,1,32]{2,0,1:T(8,128)S(1)}, u32[]{:S(2)}, u32[]{:S(2)}) collective-permute-start(f32[7,1,32]{2,0,1:T(8,128)S(1)} %pad_maximum_fusion.12), channel_id=1, source_target_pairs={{1,0},{2,1},{3,2},{5,4},{6,5},{7,6},{9,8},{10,9},{11,10},{13,12},{... | collective-permute-start | bytes 2696 | tf_op jit(solution)/shard_map/ppermute | solution.py:10
  344.2 9.7 %copy-start.9 = (f32[768,256]{1,0:T(8,128)S(1)}, f32[768,256]{1,0:T(8,128)}, u32[]{:S(2)}) copy-start(f32[768,256]{1,0:T(8,128)} %custom-call) | copy-start | bytes 2359300
  344.2 8.4 %collective-permute-start.16 = (f32[1,32,64]{2,1,0:T(8,128)S(1)}, f32[1,32,64]{2,1,0:T(8,128)S(1)}, u32[]{:S(2)}, u32[]{:S(2)}) collective-permute-start(f32[1,32,64]{2,1,0:T(8,128)S(1)} %slice.435), channel_id=1, source_target_pairs={{4,0},{8,4},{12,8},{16,12},{20,16},{24,20},{28,24},{5,1},{9,5},{13... | collective-permute-start | bytes 24584 | tf_op jit(solution)/shard_map/ppermute | solution.py:10
  352.6 74.4 %collective-permute-start.17 = (f32[13,1,64]{2,1,0:T(1,128)S(1)}, f32[13,1,64]{2,1,0:T(1,128)S(1)}, u32[]{:S(2)}, u32[]{:S(2)}) collective-permute-start(f32[13,1,64]{2,1,0:T(1,128)S(1)} %pad_maximum_fusion.11), channel_id=1, source_target_pairs={{1,0},{2,1},{3,2},{5,4},{6,5},{7,6},{9,8},{10,9},{11,10},{13,12},{... | collective-permute-start | bytes 9992 | tf_op jit(solution)/shard_map/ppermute | solution.py:10
  427.9 3.7 copy-start.1
where the time goes:
time: 440 us; the launch traced here: 432 us
  local copies, waits for them, and re-layouts  260 us (59%)
  matrix products  106 us (24%)
  starting transfers between devices  46.9 us (11%)
  waiting for transfers between devices  8.94 us (2%)
  other arithmetic  7.13 us (2%)
    dot_general x45, matrix products, accumulate(): return total + jnp.dot(window, weights, preferred_element_type=jnp.float32)  74 us
    unnamed x80, local copies, waits for them, and re-layouts  73.2 us
    reshape x2, local copies, waits for them, and re-layouts, correlate(): weights_all.reshape(15, span_width * layer_count, tile_width * layer_count)  51.4 us
    transpose x2, local copies, waits for them, and re-layouts, correlate(): weights_all = jnp.einsum('abwz,bji->ajwiz', partial_z, pick_y)  41.6 us
    dynamic_slice x30, local copies, waits for them, and re-layouts, accumulate(): window = lax.dynamic_slice_in_dim(stacked, offset_x, row_count, 0)  35.1 us
    slice x56, local copies, waits for them, and re-layouts, correlate(): lax.slice_in_dim(extended, column, column + tile_width * (block_count - 1...  34.3 us
    dot_general x3, matrix products, correlate(): weights_all = jnp.einsum('abwz,bji->ajwiz', partial_z, pick_y)  31.7 us
    ppermute x8, starting transfers between devices, from_behind(): return lax.ppermute(value, axis, pairs)  19.1 us
  transfers between devices with their start and end apart: 18, of which 4 were waited for; matrix products, arithmetic and copies ran while one was open for 71% of the time, Pallas kernels for 0%

commit v1 on v0

v1 whole, which is shorter than its diff:
```python
import functools

import jax
import jax.numpy as jnp
import numpy as np
from jax import lax
from jax.experimental import pallas as pl
from jax.experimental.pallas import tpu as pltpu
from jax.sharding import PartitionSpec as P

BF = jnp.bfloat16
F32 = jnp.float32
LANES = 128


def two(matrix):
    high = np.asarray(matrix, np.float64).astype(BF)
    low = (matrix - high.astype(np.float64)).astype(BF)
    return high, low


def beside(real, imag):
    out = np.zeros((real.shape[0], 2 * LANES))
    out[:, : real.shape[1]] = real
    out[:, LANES : LANES + imag.shape[1]] = imag
    return out


def three_terms(matrix):
    high, low = two(matrix)
    return np.concatenate([high, high, low], 1)


def up(count):
    out = np.zeros((2 * count, count + 1))
    for i in range(count):
        out[2 * i, i] = 1.0
        out[2 * i + 1, i] = out[2 * i + 1, i + 1] = 0.5
    return out


def up_closed(count):
    return up(count)[:, :count]


class Level:
    def __init__(self, taps, out_x, out_y, shift, period_y, size_z, rows_y, rows_y_end, cols_z):
        half = taps // 2
        self.taps, self.out_x, self.in_x = taps, out_x, out_x + taps - 1
        self.period_y, self.size_z = period_y, size_z
        period_z = size_z + half + (size_z + half) % 2
        assert period_y >= shift + out_y + half and shift >= half and period_y % 16 == 0
        freq_z = np.arange(period_z // 2 + 1)
        assert len(freq_z) <= LANES
        freq_y = np.arange(period_y)
        turn_z, turn_y = 2 * np.pi / period_z, 2 * np.pi / period_y
        angle = turn_z * np.outer(np.arange(size_z), freq_z)
        self.to_z = np.concatenate(two(beside(np.cos(angle), -np.sin(angle))), 0)
        angle = turn_y * np.outer(freq_y, np.arange(period_y))
        self.to_y = three_terms(np.concatenate([np.cos(angle), np.sin(angle)], 0))
        offsets = np.arange(taps) - half
        angle = turn_z * np.outer(offsets, freq_z)
        table = np.zeros((LANES, 2 * LANES))
        table[:taps] = beside(np.cos(angle), np.sin(angle))
        self.kernel_z = np.concatenate(two(table), 0)
        angle = turn_y * np.outer(freq_y, np.pad(offsets, (0, 1)))
        self.kernel_y = three_terms(np.concatenate([np.cos(angle), np.sin(angle)], 0))
        angle = turn_y * np.outer(np.arange(out_y) + shift, freq_y)
        self.from_y = [
            three_terms(
                np.concatenate([rows @ np.cos(angle), rows @ np.sin(angle)], 0) / period_y
            )
            for rows in (rows_y, rows_y_end)
        ]
        weight = np.where((freq_z == 0) | (2 * freq_z == period_z), 1.0, 2.0)[:, None] / period_z
        angle = turn_z * np.outer(freq_z, np.arange(size_z))
        table = np.zeros((2 * LANES, cols_z.shape[0]))
        table[: len(freq_z)] = (weight * np.cos(angle)) @ cols_z.T
        table[LANES : LANES + len(freq_z)] = (-weight * np.sin(angle)) @ cols_z.T
        high, low = two(table)
        self.from_z = np.concatenate([high, high, low], 0)


def down(count, first, length):
    out = np.zeros((count, length))
    for j in range(count):
        for a, w in ((-1, 0.5), (0, 1.0), (1, 0.5)):
            if 0 <= first + 2 * j + a < length:
                out[j, first + 2 * j + a] = w
    return out


def dot(a, b):
    return jnp.dot(a, b, preferred_element_type=F32)


def split(value, terms):
    out = []
    for _ in range(terms - 1):
        out.append(value.astype(BF))
        value = value - out[-1].astype(F32)
    return out + [value.astype(BF)]


def stacked(value):
    high, low = split(value, 2)
    return jnp.concatenate([high, low, high], 0)


def z_transform(cells, table):
    size_z = cells.shape[1]
    if size_z % LANES == 0:
        return dot(jnp.concatenate([cells, cells], 1), table[...])
    return dot(cells, table[:size_z]) + dot(cells, table[size_z:])


def forward(cells, to_z, to_y, real, imag, x):
    period = real.shape[1]
    spread = dot(to_y[...], stacked(z_transform(cells, to_z)))
    real[x] = spread[:period, :LANES] + spread[period:, LANES:]
    imag[x] = spread[:period, LANES:] - spread[period:, :LANES]


def backward(real, imag, from_y, from_z):
    count = from_y.shape[0] // 2
    spread = dot(from_y[...], stacked(jnp.concatenate([real, imag], 1)))
    real = spread[:count, :LANES] - spread[count:, LANES:]
    imag = spread[:count, LANES:] + spread[count:, :LANES]
    high, low = split(jnp.concatenate([real, imag], 1), 2)
    return dot(jnp.concatenate([high, low, high], 1), from_z[...])


def along_x(real, imag, spectrum, out_real, out_imag, block):
    kernel_r, kernel_d, kernel_s = spectrum
    taps, period = kernel_r.shape[:2]
    out_x = out_real.shape[0]

    def body(part, _):
        rows = pl.ds(pl.multiple_of(8 * part, 8), 8)
        for start in range(0, out_x, block):
            count = min(block, out_x - start)
            sums = [[None] * 3 for _ in range(count)]
            seen = {}
            for a in range(taps):
                weights = kernel_r[a, rows, :], kernel_d[a, rows, :], kernel_s[a, rows, :]
                for i in range(count):
                    x = start + i + a
                    if x not in seen:
                        r, m = real[x, rows, :], imag[x, rows, :]
                        seen[x] = r + m, r, m
                    for k in range(3):
                        term = weights[k] * seen[x][k]
                        sums[i][k] = term if a == 0 else sums[i][k] + term
            for i in range(count):
                out_real[start + i, rows, :] = sums[i][0] - sums[i][2]
                out_imag[start + i, rows, :] = sums[i][0] + sums[i][1]
        return 0

    lax.fori_loop(0, period // 8, body, 0)


def rows_loop(count, step, body):
    def trip(i, _):
        for k in range(step):
            body(i * step + k)
        return 0

    lax.fori_loop(0, count // step, trip, 0)
    for x in range(count - count % step, count):
        body(x)


def restrict_row(low, middle, high, down_y, down_z):
    total = 0.5 * low.astype(F32) + middle.astype(F32) + 0.5 * high.astype(F32)
    total = dot(down_y[...], jnp.concatenate(split(total, 3), 0))
    parts = split(total, 3)
    return sum(dot(part, down_z[...]) for part in reversed(parts))


def spectra_kernel(taps, kernels, *refs):
    levels = kernels.shape[0]
    tables, outs, mid = refs[: 2 * levels], refs[2 * levels : -1], refs[-1]
    for level in range(levels):
        kernel_z, kernel_y = tables[2 * level : 2 * level + 2]
        out_r, out_d, out_s = outs[3 * level : 3 * level + 3]
        period = out_r.shape[1]
        cells = kernels[level]
        mid[...] = dot(jnp.concatenate([cells, cells], 1), kernel_z[...])

        def body(a, kernel_y=kernel_y, out_r=out_r, out_d=out_d, out_s=out_s, period=period):
            rows = mid[pl.ds(pl.multiple_of(16 * a, 16), 16), :]
            spread = dot(kernel_y[...], stacked(rows))
            real = spread[:period, :LANES] - spread[period:, LANES:]
            imag = spread[:period, LANES:] + spread[period:, :LANES]
            out_r[a] = real
            out_d[a] = imag - real
            out_s[a] = imag + real

        rows_loop(taps, 3, body)


def restrict_kernel(valid, fine, down_y, down_z, out):
    def body(t):
        row = restrict_row(fine[2 * t], fine[2 * t + 1], fine[2 * t + 2], down_y, down_z)
        out[t] = jnp.where(t < valid[0], row, 0.0).astype(BF)

    rows_loop(out.shape[0], 1, body)


def fine_kernel(fine, kr, kd, ks, to_z, to_y, from_y, from_z, out, real, imag, er, ei):
    rows_loop(real.shape[0], 2, lambda x: forward(fine[x], to_z, to_y, real, imag, x))
    along_x(real, imag, (kr, kd, ks), er, ei, 8)

    def body(x):
        out[x] = backward(er[x], ei[x], from_y, from_z)

    rows_loop(out.shape[0], 2, body)


def coarse_kernel(
    valid,
    inside,
    mid,
    fine_e,
    down_y,
    down_z,
    mr,
    md,
    ms,
    m_to_z,
    m_to_y,
    m_from_y,
    m_from_z,
    tr,
    td,
    ts,
    t_to_z,
    t_to_y,
    t_from_y,
    t_from_z,
    out,
    m_real,
    m_imag,
    m_er,
    m_ei,
    m_out,
    t_real,
    t_imag,
    t_er,
    t_ei,
    t_out,
):
    skip = (mid.shape[0] - m_real.shape[0]) // 2
    cols = (mid.shape[1] - m_real.shape[1]) // 2

    def mid_body(x):
        cells = mid[x + skip, cols : cols + m_real.shape[1], :]
        forward(cells, m_to_z, m_to_y, m_real, m_imag, x)

    rows_loop(m_real.shape[0], 1, mid_body)

    def top_body(t):
        row = restrict_row(mid[2 * t], mid[2 * t + 1], mid[2 * t + 2], down_y, down_z)
        row = jnp.where(t < valid[0], row, 0.0).astype(BF)
        forward(row, t_to_z, t_to_y, t_real, t_imag, t)

    rows_loop(t_real.shape[0], 1, top_body)
    along_x(m_real, m_imag, (mr, md, ms), m_er, m_ei, 7)
    along_x(t_real, t_imag, (tr, td, ts), t_er, t_ei, 7)

    def top_out(x):
        t_out[x] = backward(t_er[x], t_ei[x], t_from_y, t_from_z)

    rows_loop(t_out.shape[0], 1, top_out)
    last = t_out.shape[0] - 1
    t_out[last] = t_out[last] * inside[0]

    def mid_out(x):
        m_out[x] = backward(m_er[x], m_ei[x], m_from_y, m_from_z)

    rows_loop(m_out.shape[0], 1, mid_out)
    for i in range(last):
        m_out[2 * i] += t_out[i]
        m_out[2 * i + 1] += 0.5 * (t_out[i] + t_out[i + 1])
    m_out[2 * last] = (m_out[2 * last] + t_out[last]) * inside[0]

    def finish(i):
        out[2 * i] = fine_e[2 * i] + m_out[i]
        out[2 * i + 1] = fine_e[2 * i + 1] + 0.5 * (m_out[i] + m_out[i + 1])

    rows_loop(out.shape[0] // 2, 1, finish)


def call(kernel, outs, scratch, scalars, args):
    vmem = pl.BlockSpec(memory_space=pltpu.VMEM)
    smem = pl.BlockSpec(memory_space=pltpu.SMEM)
    return pl.pallas_call(
        kernel,
        out_shape=outs,
        in_specs=[smem] * len(scalars) + [vmem] * len(args),
        out_specs=jax.tree.map(lambda _: vmem, outs),
        scratch_shapes=[pltpu.VMEM(shape, F32) for shape in scratch],
        compiler_params=pltpu.CompilerParams(vmem_limit_bytes=60 << 20),
    )(*scalars, *args)


def shifted(value, axis, by):
    length = lax.axis_size(axis)
    return lax.ppermute(
        value, axis, [(i, i + by) for i in range(length) if 0 <= i + by < length]
    )


def shards(charges, kernel_fine, kernel_mid, kernel_top):
    nx, ny, nz = charges.shape
    taps = kernel_fine.shape[0]
    half = taps // 2
    gx, gy = lax.axis_index("gx"), lax.axis_index("gy")
    left_x = lax.axis_size("gx") - gx
    end_y = gy == lax.axis_size("gy") - 1
    wide = half + 1

    ident = np.eye(ny)
    fine = Level(taps, nx, ny, wide, ny + 2 * wide, nz, ident, ident, np.eye(nz))
    my, mz = ny // 2, nz // 2
    to_fine = up(my)
    ended = np.diag([1.0] * my + [0.0])
    mid = Level(
        taps, nx // 2 + 1, my + 1, wide, my + 2 * wide, mz, to_fine, to_fine @ ended, up_closed(mz)
    )
    ty, tz = my // 2, mz // 2
    to_mid = np.concatenate([up(ty), np.eye(ty + 1)[-1:]], 0)
    top_ended = np.diag([1.0] * ty + [0.0])
    top = Level(
        taps,
        nx // 4 + 1,
        ty + 1,
        wide,
        ty + 2 * wide,
        tz,
        to_fine @ to_mid,
        to_fine @ to_mid @ top_ended,
        up_closed(mz) @ up_closed(tz),
    )

    cells = jnp.stack([kernel_fine, kernel_mid, kernel_top])
    cells = jnp.pad(cells, ((0, 0), (0, 0), (0, 1), (0, LANES - taps)))
    cells = cells.reshape(3, taps * 16, LANES)
    levels = (fine, mid, top)
    outs = [
        jax.ShapeDtypeStruct((taps, level.period_y, LANES), F32)
        for level in levels
        for _ in range(3)
    ]
    tables = [table for level in levels for table in (level.kernel_z, level.kernel_y)]
    spectra = call(
        functools.partial(spectra_kernel, taps),
        outs,
        [(taps * 16, 2 * LANES)],
        [],
        [cells, *tables],
    )

    fine_q = charges.astype(BF)
    fine_x = jnp.concatenate(
        [shifted(fine_q[-half:], "gx", 1), fine_q, shifted(fine_q[:wide], "gx", -1)], 0
    )
    fine_ext = jnp.concatenate(
        [shifted(fine_x[:, -wide:], "gy", 1), fine_x, shifted(fine_x[:, :wide], "gy", -1)], 1
    )

    lead = (half - 1) // 2
    rows = lead + nx // 2 + wide // 2
    down_y = np.tile(down(my, wide, ny + 2 * wide), (1, 3)).astype(BF)
    down_z = down(mz, 0, nz).T.astype(BF)
    valid = jnp.where(left_x == 1, lead + nx // 2, rows)[None].astype(jnp.int32)
    mid_q = call(
        restrict_kernel,
        jax.ShapeDtypeStruct((rows, my, mz), BF),
        [],
        [valid],
        [fine_ext, down_y, down_z],
    )
    mx = nx // 2
    reach = 2 * half + 1
    assert lead + mx >= reach and my >= 2 * wide
    mid_x = jnp.concatenate(
        [
            shifted(mid_q[lead + mx - reach : mx], "gx", 1),
            mid_q,
            shifted(mid_q[rows - mx :], "gx", -1),
        ],
        0,
    )
    mid_ext = jnp.concatenate(
        [
            shifted(mid_x[:, -2 * wide :], "gy", 1),
            mid_x,
            shifted(mid_x[:, : 2 * wide], "gy", -1),
        ],
        1,
    )

    fine_e = call(
        fine_kernel,
        jax.ShapeDtypeStruct((nx, ny, nz), F32),
        [(fine.in_x, fine.period_y, LANES)] * 2 + [(nx, fine.period_y, LANES)] * 2,
        [],
        [
            fine_ext,
            *spectra[:3],
            fine.to_z,
            fine.to_y,
            fine.from_y[0],
            fine.from_z,
        ],
    )

    tx = nx // 4
    down_y = down(ty + 2 * wide, 0, my + 4 * wide)
    keep = jnp.arange(ty + 2 * wide)[:, None] < jnp.where(end_y, wide + ty, ty + 2 * wide)
    down_y = jnp.where(keep, np.tile(down_y, (1, 3)).astype(BF), 0)
    down_z = down(tz, 0, mz).T.astype(BF)
    valid = jnp.minimum(left_x * tx + half, top.in_x)[None].astype(jnp.int32)
    inside = jnp.where(left_x == 1, 0.0, 1.0)[None].astype(F32)

    def pick(pair):
        return jnp.where(end_y, pair[1], pair[0])

    return call(
        coarse_kernel,
        jax.ShapeDtypeStruct((nx, ny, nz), F32),
        [(mid.in_x, mid.period_y, LANES)] * 2
        + [(mid.out_x, mid.period_y, LANES)] * 2
        + [(mid.out_x, ny, nz)]
        + [(top.in_x, top.period_y, LANES)] * 2
        + [(top.out_x, top.period_y, LANES)] * 2
        + [(top.out_x, ny, nz)],
        [valid, inside],
        [
            mid_ext,
            fine_e,
            down_y,
            down_z,
            *spectra[3:6],
            mid.to_z,
            mid.to_y,
            pick(mid.from_y),
            mid.from_z,
            *spectra[6:9],
            top.to_z,
            top.to_y,
            pick(top.from_y),
            top.from_z,
        ],
    )


def solution(mesh):
    placed = (P("gx", "gy", None), P(), P(), P())
    return jax.shard_map(
        shards, mesh=mesh, in_specs=placed, out_specs=P("gx", "gy", None), check_vma=False
    )
```

time: 440 us -> 105 us (0.24)
  the two profiles are of different devices: /device:TPU:8 before, /device:TPU:11 now
where the time goes in v1:
time: 105 us
  Pallas kernels  63.3 us (60%)
  starting transfers between devices  22.5 us (21%)
  waiting for transfers between devices  10.6 us (10%)
  other arithmetic  6.96 us (7%)
  local copies, waits for them, and re-layouts  1.07 us (1%)
    pallas_call x4, Pallas kernels, call(): pl.pallas_call(kernel, out_shape=outs, in_specs=[smem] * len(scalars) + [...  63.3 us
    ppermute x8, starting transfers between devices, shifted(): lax.ppermute(value, axis, [(i, i + by) for i in range(length) if 0 <= i +...  22.5 us
    ppermute x8, waiting for transfers between devices, shifted(): lax.ppermute(value, axis, [(i, i + by) for i in range(length) if 0 <= i +...  10.6 us
  transfers between devices with their start and end apart: 8, of which 3 were waited for; matrix products, arithmetic and copies ran while one was open for 3% of the time, Pallas kernels for 23%

profile of v1, /device:TPU:11, one launch (start us, length us, event | category | flops | bytes accessed | tf_op | source)
XLA Modules:
  0.0 104.6 jit_solution(9743740917139334792)
XLA Ops:
  0.0 0.0 copy-start.7
  0.0 1.2 %convert_element_type.7 = bf16[24,64,128]{2,1,0:T(8,128)(2,1)S(1)} convert(f32[24,64,128]{2,1,0:T(8,128)} %param.28) | non-fusion elementwise | flops 196608 | bytes 1179648 | tf_op jit(solution)/shard_map/convert_element_type | solution.py:364
  1.3 2.2 %collective-permute-start.1 = (bf16[8,64,128]{2,1,0:T(8,128)(2,1)S(1)}, bf16[8,64,128]{2,1,0:T(8,128)(2,1)S(1)}, u32[]{:S(2)}, u32[]{:S(2)}) collective-permute-start(bf16[8,64,128]{2,1,0:T(8,128)(2,1)S(1)} %slice.33), channel_id=1, source_target_pairs={{4,0},{8,4},{12,8},{16,12},{20,16},{24,20},{28,24},{5,1},{9,5},{13... | collective-permute-start | bytes 393224 | tf_op jit(solution)/shard_map/ppermute | solution.py:309
  3.5 4.0 %collective-permute-start = (bf16[7,64,128]{2,1,0:T(8,128)(2,1)S(1)}, bf16[7,64,128]{2,1,0:T(8,128)(2,1)S(1)}, u32[]{:S(2)}, u32[]{:S(2)}) collective-permute-start(bf16[7,64,128]{2,1,0:T(8,128)(2,1)S(1)} %slice.32), channel_id=1, source_target_pairs={{0,4},{4,8},{8,12},{12,16},{16,20},{20,24},{24,28},{1,5},{5,9},{9,... | collective-permute-start | bytes 344072 | tf_op jit(solution)/shard_map/ppermute | solution.py:309
  7.5 0.6 broadcast_select_fusion.m_from_y
  8.2 0.6 broadcast_select_fusion.1.t_from_y
  8.8 3.2 %collective-permute-done = bf16[7,64,128]{2,1,0:T(8,128)(2,1)S(1)} collective-permute-done((bf16[7,64,128]{2,1,0:T(8,128)(2,1)S(1)}, bf16[7,64,128]{2,1,0:T(8,128)(2,1)S(1)}, u32[]{:S(2)}, u32[]{:S(2)}) %collective-permute-start) | collective-permute-done | bytes 114720 | tf_op jit(solution)/shard_map/ppermute | solution.py:309
  11.9 0.0 collective-permute-done.1
  12.0 3.5 %collective-permute-start.2 = (bf16[39,8,128]{2,1,0:T(8,128)(2,1)S(1)}, bf16[39,8,128]{2,1,0:T(8,128)(2,1)S(1)}, u32[]{:S(2)}, u32[]{:S(2)}) collective-permute-start(bf16[39,8,128]{2,1,0:T(8,128)(2,1)S(1)} %get-tuple-element.23), channel_id=1, source_target_pairs={{0,1},{1,2},{2,3},{4,5},{5,6},{6,7},{8,9},{9,10},{10,11},{12,13},{... | collective-permute-start | bytes 239624 | tf_op jit(solution)/shard_map/ppermute | solution.py:309
  15.5 1.9 %collective-permute-start.3 = (bf16[39,8,128]{2,1,0:T(8,128)(2,1)S(1)}, bf16[39,8,128]{2,1,0:T(8,128)(2,1)S(1)}, u32[]{:S(2)}, u32[]{:S(2)}) collective-permute-start(bf16[39,8,128]{2,1,0:T(8,128)(2,1)S(1)} %get-tuple-element.24), channel_id=1, source_target_pairs={{1,0},{2,1},{3,2},{5,4},{6,5},{7,6},{9,8},{10,9},{11,10},{13,12},{... | collective-permute-start | bytes 239624 | tf_op jit(solution)/shard_map/ppermute | solution.py:309
  17.5 0.0 collective-permute-done.2
  17.5 3.8 %collective-permute-done.3 = bf16[39,8,128]{2,1,0:T(8,128)(2,1)S(1)} collective-permute-done((bf16[39,8,128]{2,1,0:T(8,128)(2,1)S(1)}, bf16[39,8,128]{2,1,0:T(8,128)(2,1)S(1)}, u32[]{:S(2)}, u32[]{:S(2)}) %collective-permute-start.3) | collective-permute-done | bytes 79904 | tf_op jit(solution)/shard_map/ppermute | solution.py:309
  21.2 1.0 pad_maximum_fusion.fine
  22.2 7.5 %shard_map.262 = bf16[19,32,64]{2,1,0:T(8,128)(2,1)} custom-call(s32[1]{0:T(128)} %bitcast.2.valid, bf16[39,80,128]{2,1,0:T(8,128)(2,1)} %pad_maximum_fusion.fine, bf16[32,240]{1,0:T(8,128)(2,1)} %constant.90.clone.down_y, bf16[128,64]{1,0:T(8,128)(2,1)} %constant.91.clone.down_z), custom_call_target="tpu_custom_call" | custom-call | tf_op jit(solution)/shard_map/pallas_call | solution.py:297
  29.7 1.0 fusion.10
  30.7 0.0 copy-start.3
  30.7 0.0 copy-start.4
  30.7 0.0 copy-start.5
  30.7 3.7 %collective-permute-start.4 = (bf16[12,32,64]{2,1,0:T(8,128)(2,1)S(1)}, bf16[12,32,64]{2,1,0:T(8,128)(2,1)S(1)}, u32[]{:S(2)}, u32[]{:S(2)}) collective-permute-start(bf16[12,32,64]{2,1,0:T(8,128)(2,1)S(1)} %get-tuple-element.27), channel_id=1, source_target_pairs={{0,4},{4,8},{8,12},{12,16},{16,20},{20,24},{24,28},{1,5},{5,9},{9,... | collective-permute-start | bytes 147464 | tf_op jit(solution)/shard_map/ppermute | solution.py:309
  34.5 1.9 %collective-permute-start.5 = (bf16[12,32,64]{2,1,0:T(8,128)(2,1)S(1)}, bf16[12,32,64]{2,1,0:T(8,128)(2,1)S(1)}, u32[]{:S(2)}, u32[]{:S(2)}) collective-permute-start(bf16[12,32,64]{2,1,0:T(8,128)(2,1)S(1)} %get-tuple-element.28), channel_id=1, source_target_pairs={{4,0},{8,4},{12,8},{16,12},{20,16},{24,20},{28,24},{5,1},{9,5},{13... | collective-permute-start | bytes 147464 | tf_op jit(solution)/shard_map/ppermute | solution.py:309
  36.4 0.7 broadcast_select_fusion.2.down_y
  37.1 0.0 collective-permute-done.4
  37.1 3.6 %collective-permute-done.5 = bf16[12,32,64]{2,1,0:T(8,128)(2,1)S(1)} collective-permute-done((bf16[12,32,64]{2,1,0:T(8,128)(2,1)S(1)}, bf16[12,32,64]{2,1,0:T(8,128)(2,1)S(1)}, u32[]{:S(2)}, u32[]{:S(2)}) %collective-permute-start.5) | collective-permute-done | bytes 49184 | tf_op jit(solution)/shard_map/ppermute | solution.py:309
  40.7 1.0 pad_maximum_fusion.2
  41.8 3.3 %collective-permute-start.6 = (bf16[43,16,64]{2,1,0:T(8,128)(2,1)S(1)}, bf16[43,16,64]{2,1,0:T(8,128)(2,1)S(1)}, u32[]{:S(2)}, u32[]{:S(2)}) collective-permute-start(bf16[43,16,64]{2,1,0:T(8,128)(2,1)S(1)} %get-tuple-element.25), channel_id=1, source_target_pairs={{0,1},{1,2},{2,3},{4,5},{5,6},{6,7},{8,9},{9,10},{10,11},{12,13},{... | collective-permute-start | bytes 264200 | tf_op jit(solution)/shard_map/ppermute | solution.py:309
  45.0 1.9 %collective-permute-start.7 = (bf16[43,16,64]{2,1,0:T(8,128)(2,1)S(1)}, bf16[43,16,64]{2,1,0:T(8,128)(2,1)S(1)}, u32[]{:S(2)}, u32[]{:S(2)}) collective-permute-start(bf16[43,16,64]{2,1,0:T(8,128)(2,1)S(1)} %get-tuple-element.26), channel_id=1, source_target_pairs={{1,0},{2,1},{3,2},{5,4},{6,5},{7,6},{9,8},{10,9},{11,10},{13,12},{... | collective-permute-start | bytes 264200 | tf_op jit(solution)/shard_map/ppermute | solution.py:309
  47.0 0.8 fusion.8
  47.8 6.1 %shard_map.263 = (f32[15,80,128]{2,1,0:T(8,128)}, f32[15,80,128]{2,1,0:T(8,128)}, f32[15,80,128]{2,1,0:T(8,128)}, f32[15,48,128]{2,1,0:T(8,128)}, f32[15,48,128]...) custom-call(bf16[3,240,128]{2,1,0:T(8,128)(2,1)} %bitcast.7, ...), custom_call_target="tpu_custom_call" | custom-call | tf_op jit(solution)/shard_map/pallas_call | solution.py:297
  53.8 18.4 %shard_map.264.fine_e = f32[24,64,128]{2,1,0:T(8,128)} custom-call(bf16[39,80,128]{2,1,0:T(8,128)(2,1)} %pad_maximum_fusion.fine, f32[15,80,128]{2,1,0:T(8,128)} %get-tuple-element.14.kr, f32[15,80,128]{2,1,0:T(8,128)} %get-tuple-element.15.kd, f32[15,80,128]{2,1,0:T(8,128)} %get-tuple-element.16.ks, bf16[256,256]{1,0:T(8,128)(2,1)} %constant.92.clone.to_z, ...), custom_call_target="tpu_custom_call" | custom-call | tf_op jit(solution)/shard_map/pallas_call | solution.py:297
  72.2 0.0 collective-permute-done.6
  72.2 1.1 %pad_maximum_fusion.1.mid = bf16[43,64,64]{2,1,0:T(8,128)(2,1)} fusion(bf16[43,16,64]{2,1,0:T(8,128)(2,1)S(1)} %collective-permute-done.7, bf16[12,32,64]{2,1,0:T(8,128)(2,1)S(1)} %collective-permute-done.5, bf16[19,32,64]{2,1,0:T(8,128)(2,1)S(1)} %copy-done, bf16[12,32,64]{2,1,0:T(8,128)(2,1)S(1)} %collective-permute-done.4, ...), kind=kLoop, calls=%fused_computation.1 | loop fusion | flops 1761280 | bytes 704512 | tf_op jit(solution)/shard_map/concatenate | solution.py:395
  73.3 31.3 %shard_map.265 = f32[24,64,128]{2,1,0:T(8,128)} custom-call(s32[1]{0:T(128)} %bitcast.valid, f32[1]{0:T(128)} %bitcast.1.inside, bf16[43,64,64]{2,1,0:T(8,128)(2,1)} %pad_maximum_fusion.1.mid, f32[24,64,128]{2,1,0:T(8,128)} %shard_map.264.fine_e, bf16[32,192]{1,0:T(8,128)(2,1)} %broadcast_select_fusion.2.down_y, bf16[64,32]{1,0:T(8,128)(2,1)} %constant.101.clone.down_z, ...), custom_call_target="tpu_custom_call" | custom-call | tf_op jit(solution)/shard_map/pallas_call | solution.py:297
  (20 shorter events, 0.1 us)
Async XLA Ops:
  0.0 7.5 %copy-start.1 = (bf16[128,144]{1,0:T(8,128)(2,1)S(1)}, bf16[128,144]{1,0:T(8,128)(2,1)}, u32[]{:S(2)}) copy-start(bf16[128,144]{1,0:T(8,128)(2,1)} %constant.97.clone) | copy-start | bytes 110596
  0.0 7.5 %copy-start.2 = (bf16[128,144]{1,0:T(8,128)(2,1)S(1)}, bf16[128,144]{1,0:T(8,128)(2,1)}, u32[]{:S(2)}) copy-start(bf16[128,144]{1,0:T(8,128)(2,1)} %constant.98.clone) | copy-start | bytes 110596
  0.0 8.1 %copy-start.6 = (bf16[128,96]{1,0:T(8,128)(2,1)S(1)}, bf16[128,96]{1,0:T(8,128)(2,1)}, u32[]{:S(2)}) copy-start(bf16[128,96]{1,0:T(8,128)(2,1)} %constant.100.clone) | copy-start | bytes 73732
  0.0 8.1 %copy-start.7 = (bf16[128,96]{1,0:T(8,128)(2,1)S(1)}, bf16[128,96]{1,0:T(8,128)(2,1)}, u32[]{:S(2)}) copy-start(bf16[128,96]{1,0:T(8,128)(2,1)} %constant.99.clone) | copy-start | bytes 73732
  1.3 10.7 %collective-permute-start.1 = (bf16[8,64,128]{2,1,0:T(8,128)(2,1)S(1)}, bf16[8,64,128]{2,1,0:T(8,128)(2,1)S(1)}, u32[]{:S(2)}, u32[]{:S(2)}) collective-permute-start(bf16[8,64,128]{2,1,0:T(8,128)(2,1)S(1)} %slice.33), channel_id=1, source_target_pairs={{4,0},{8,4},{12,8},{16,12},{20,16},{24,20},{28,24},{5,1},{9,5},{13... | collective-permute-start | bytes 393224 | tf_op jit(solution)/shard_map/ppermute | solution.py:309
  3.5 8.5 %collective-permute-start = (bf16[7,64,128]{2,1,0:T(8,128)(2,1)S(1)}, bf16[7,64,128]{2,1,0:T(8,128)(2,1)S(1)}, u32[]{:S(2)}, u32[]{:S(2)}) collective-permute-start(bf16[7,64,128]{2,1,0:T(8,128)(2,1)S(1)} %slice.32), channel_id=1, source_target_pairs={{0,4},{4,8},{8,12},{12,16},{16,20},{20,24},{24,28},{1,5},{5,9},{9,... | collective-permute-start | bytes 344072 | tf_op jit(solution)/shard_map/ppermute | solution.py:309
  12.0 5.5 %collective-permute-start.2 = (bf16[39,8,128]{2,1,0:T(8,128)(2,1)S(1)}, bf16[39,8,128]{2,1,0:T(8,128)(2,1)S(1)}, u32[]{:S(2)}, u32[]{:S(2)}) collective-permute-start(bf16[39,8,128]{2,1,0:T(8,128)(2,1)S(1)} %get-tuple-element.23), channel_id=1, source_target_pairs={{0,1},{1,2},{2,3},{4,5},{5,6},{6,7},{8,9},{9,10},{10,11},{12,13},{... | collective-permute-start | bytes 239624 | tf_op jit(solution)/shard_map/ppermute | solution.py:309
  15.5 5.7 %collective-permute-start.3 = (bf16[39,8,128]{2,1,0:T(8,128)(2,1)S(1)}, bf16[39,8,128]{2,1,0:T(8,128)(2,1)S(1)}, u32[]{:S(2)}, u32[]{:S(2)}) collective-permute-start(bf16[39,8,128]{2,1,0:T(8,128)(2,1)S(1)} %get-tuple-element.24), channel_id=1, source_target_pairs={{1,0},{2,1},{3,2},{5,4},{6,5},{7,6},{9,8},{10,9},{11,10},{13,12},{... | collective-permute-start | bytes 239624 | tf_op jit(solution)/shard_map/ppermute | solution.py:309
  22.2 14.2 %copy-start.8 = (bf16[32,192]{1,0:T(8,128)(2,1)S(1)}, bf16[32,192]{1,0:T(8,128)(2,1)}, u32[]{:S(2)}) copy-start(bf16[32,192]{1,0:T(8,128)(2,1)} %constant.96.clone) | copy-start | bytes 36868
  30.7 16.3 %copy-start.3 = (bf16[15,15,15]{2,1,0:T(8,128)(2,1)S(1)}, bf16[15,15,15]{2,1,0:T(8,128)(2,1)}, u32[]{:S(2)}) copy-start(bf16[15,15,15]{2,1,0:T(8,128)(2,1)} %param.31) | copy-start | bytes 20254
  30.7 16.3 %copy-start.4 = (bf16[15,15,15]{2,1,0:T(8,128)(2,1)S(1)}, bf16[15,15,15]{2,1,0:T(8,128)(2,1)}, u32[]{:S(2)}) copy-start(bf16[15,15,15]{2,1,0:T(8,128)(2,1)} %param.30) | copy-start | bytes 20254
  30.7 16.3 %copy-start.5 = (bf16[15,15,15]{2,1,0:T(8,128)(2,1)S(1)}, bf16[15,15,15]{2,1,0:T(8,128)(2,1)}, u32[]{:S(2)}) copy-start(bf16[15,15,15]{2,1,0:T(8,128)(2,1)} %param.29) | copy-start | bytes 20254
  30.7 6.3 %collective-permute-start.4 = (bf16[12,32,64]{2,1,0:T(8,128)(2,1)S(1)}, bf16[12,32,64]{2,1,0:T(8,128)(2,1)S(1)}, u32[]{:S(2)}, u32[]{:S(2)}) collective-permute-start(bf16[12,32,64]{2,1,0:T(8,128)(2,1)S(1)} %get-tuple-element.27), channel_id=1, source_target_pairs={{0,4},{4,8},{8,12},{12,16},{16,20},{20,24},{24,28},{1,5},{5,9},{9,... | collective-permute-start | bytes 147464 | tf_op jit(solution)/shard_map/ppermute | solution.py:309
  34.5 6.3 %collective-permute-start.5 = (bf16[12,32,64]{2,1,0:T(8,128)(2,1)S(1)}, bf16[12,32,64]{2,1,0:T(8,128)(2,1)S(1)}, u32[]{:S(2)}, u32[]{:S(2)}) collective-permute-start(bf16[12,32,64]{2,1,0:T(8,128)(2,1)S(1)} %get-tuple-element.28), channel_id=1, source_target_pairs={{4,0},{8,4},{12,8},{16,12},{20,16},{24,20},{28,24},{5,1},{9,5},{13... | collective-permute-start | bytes 147464 | tf_op jit(solution)/shard_map/ppermute | solution.py:309
  41.8 30.4 %collective-permute-start.6 = (bf16[43,16,64]{2,1,0:T(8,128)(2,1)S(1)}, bf16[43,16,64]{2,1,0:T(8,128)(2,1)S(1)}, u32[]{:S(2)}, u32[]{:S(2)}) collective-permute-start(bf16[43,16,64]{2,1,0:T(8,128)(2,1)S(1)} %get-tuple-element.25), channel_id=1, source_target_pairs={{0,1},{1,2},{2,3},{4,5},{5,6},{6,7},{8,9},{9,10},{10,11},{12,13},{... | collective-permute-start | bytes 264200 | tf_op jit(solution)/shard_map/ppermute | solution.py:309
  45.0 27.1 %collective-permute-start.7 = (bf16[43,16,64]{2,1,0:T(8,128)(2,1)S(1)}, bf16[43,16,64]{2,1,0:T(8,128)(2,1)S(1)}, u32[]{:S(2)}, u32[]{:S(2)}) collective-permute-start(bf16[43,16,64]{2,1,0:T(8,128)(2,1)S(1)} %get-tuple-element.26), channel_id=1, source_target_pairs={{1,0},{2,1},{3,2},{5,4},{6,5},{7,6},{9,8},{10,9},{11,10},{13,12},{... | collective-permute-start | bytes 264200 | tf_op jit(solution)/shard_map/ppermute | solution.py:309
  53.8 18.4 %copy-start = (bf16[19,32,64]{2,1,0:T(8,128)(2,1)S(1)}, bf16[19,32,64]{2,1,0:T(8,128)(2,1)}, u32[]{:S(2)}) copy-start(bf16[19,32,64]{2,1,0:T(8,128)(2,1)} %shard_map.262) | copy-start | bytes 233476

commit v2 on v1

--- a/solution.py
+++ b/solution.py
@@ -107,27 +107,87 @@
     return jnp.concatenate([high, low, high], 0)
 
 
-def z_transform(cells, table):
-    size_z = cells.shape[1]
-    if size_z % LANES == 0:
-        return dot(jnp.concatenate([cells, cells], 1), table[...])
-    return dot(cells, table[:size_z]) + dot(cells, table[size_z:])
-
-
-def forward(cells, to_z, to_y, real, imag, x):
-    period = real.shape[1]
-    spread = dot(to_y[...], stacked(z_transform(cells, to_z)))
-    real[x] = spread[:period, :LANES] + spread[period:, LANES:]
-    imag[x] = spread[:period, LANES:] - spread[period:, :LANES]
-
-
-def backward(real, imag, from_y, from_z):
-    count = from_y.shape[0] // 2
-    spread = dot(from_y[...], stacked(jnp.concatenate([real, imag], 1)))
-    real = spread[:count, :LANES] - spread[count:, LANES:]
-    imag = spread[:count, LANES:] + spread[count:, :LANES]
-    high, low = split(jnp.concatenate([real, imag], 1), 2)
-    return dot(jnp.concatenate([high, low, high], 1), from_z[...])
+def batches(count, size, body):
+    def trip(i, _):
+        first = i * size
+        body([first + k for k in range(size)], first)
+        return 0
+
+    whole = count // size
+    if whole > 1:
+        lax.fori_loop(0, whole, trip, 0)
+    else:
+        whole = 0
+    for first in range(whole * size, count, size):
+        body(list(range(first, min(count, first + size))), first)
+
+
+def rows_at(first, period, count):
+    return pl.ds(first * period if isinstance(first, int) else pl.multiple_of(first * period, 16), count * period)
+
+
+def to_frequencies_z(read, count, size, table, terms):
+    period = terms.shape[1] // count
+
+    def body(xs, first):
+        cells = jnp.concatenate([read(x) for x in xs], 0)
+        size_z = cells.shape[1]
+        if size_z % LANES == 0:
+            value = dot(jnp.concatenate([cells, cells], 1), table[...])
+        else:
+            value = dot(cells, table[:size_z]) + dot(cells, table[size_z:])
+        high, low = split(value, 2)
+        terms[0, rows_at(first, period, len(xs)), :] = high
+        terms[1, rows_at(first, period, len(xs)), :] = low
+
+    batches(count, size, body)
+
+
+def to_frequencies_y(terms, size, to_y, real, imag):
+    count, period = real.shape[:2]
+
+    def body(xs, first):
+        spreads = []
+        for x in xs:
+            rows = rows_at(x, period, 1)
+            high, low = terms[0, rows, :], terms[1, rows, :]
+            spreads.append(dot(to_y[...], jnp.concatenate([high, low, high], 0)))
+        for x, spread in zip(xs, spreads):
+            real[x] = spread[:period, :LANES] + spread[period:, LANES:]
+            imag[x] = spread[:period, LANES:] - spread[period:, :LANES]
+
+    batches(count, size, body)
+
+
+def from_frequencies_y(real, imag, size, from_y, terms):
+    count = real.shape[0]
+    rows = from_y.shape[0] // 2
+
+    def body(xs, first):
+        spreads = [
+            dot(from_y[...], stacked(jnp.concatenate([real[x], imag[x]], 1))) for x in xs
+        ]
+        for x, spread in zip(xs, spreads):
+            r = spread[:rows, :LANES] - spread[rows:, LANES:]
+            i = spread[rows:, :LANES] + spread[:rows, LANES:]
+            high, low = split(jnp.concatenate([r, i], 1), 2)
+            terms[0, rows_at(x, rows, 1), :] = high
+            terms[1, rows_at(x, rows, 1), :] = low
+
+    batches(count, size, body)
+
+
+def from_frequencies_z(terms, count, size, from_z, write):
+    rows = terms.shape[1] // count
+
+    def body(xs, first):
+        span = rows_at(first, rows, len(xs))
+        high, low = terms[0, span, :], terms[1, span, :]
+        value = dot(jnp.concatenate([high, low, high], 1), from_z[...])
+        for k, x in enumerate(xs):
+            write(x, value[k * rows : (k + 1) * rows])
+
+    batches(count, size, body)
 
 
 def along_x(real, imag, spectrum, out_real, out_imag, block):
@@ -170,11 +230,16 @@
         body(x)
 
 
-def restrict_row(low, middle, high, down_y, down_z):
-    total = 0.5 * low.astype(F32) + middle.astype(F32) + 0.5 * high.astype(F32)
-    total = dot(down_y[...], jnp.concatenate(split(total, 3), 0))
-    parts = split(total, 3)
-    return sum(dot(part, down_z[...]) for part in reversed(parts))
+def restrict_rows(read, down_y, down_z, xs):
+    rows = down_y.shape[0]
+    totals = [
+        0.5 * read(2 * x).astype(F32) + read(2 * x + 1).astype(F32) + 0.5 * read(2 * x + 2).astype(F32)
+        for x in xs
+    ]
+    totals = [dot(down_y[...], jnp.concatenate(split(total, 3), 0)) for total in totals]
+    parts = split(jnp.concatenate(totals, 0), 3)
+    value = sum(dot(part, down_z[...]) for part in reversed(parts))
+    return [value[k * rows : (k + 1) * rows] for k in range(len(xs))]
 
 
 def spectra_kernel(taps, kernels, *refs):
@@ -187,34 +252,36 @@
         cells = kernels[level]
         mid[...] = dot(jnp.concatenate([cells, cells], 1), kernel_z[...])
 
-        def body(a, kernel_y=kernel_y, out_r=out_r, out_d=out_d, out_s=out_s, period=period):
-            rows = mid[pl.ds(pl.multiple_of(16 * a, 16), 16), :]
-            spread = dot(kernel_y[...], stacked(rows))
-            real = spread[:period, :LANES] - spread[period:, LANES:]
-            imag = spread[:period, LANES:] + spread[period:, :LANES]
-            out_r[a] = real
-            out_d[a] = imag - real
-            out_s[a] = imag + real
-
-        rows_loop(taps, 3, body)
+        def body(xs, first, kernel_y=kernel_y, outs=(out_r, out_d, out_s), period=period):
+            spreads = [dot(kernel_y[...], stacked(mid[rows_at(a, 16, 1), :])) for a in xs]
+            for a, spread in zip(xs, spreads):
+                real = spread[:period, :LANES] - spread[period:, LANES:]
+                imag = spread[:period, LANES:] + spread[period:, :LANES]
+                outs[0][a] = real
+                outs[1][a] = imag - real
+                outs[2][a] = imag + real
+
+        batches(taps, 5, body)
 
 
 def restrict_kernel(valid, fine, down_y, down_z, out):
-    def body(t):
-        row = restrict_row(fine[2 * t], fine[2 * t + 1], fine[2 * t + 2], down_y, down_z)
-        out[t] = jnp.where(t < valid[0], row, 0.0).astype(BF)
-
-    rows_loop(out.shape[0], 1, body)
-
-
-def fine_kernel(fine, kr, kd, ks, to_z, to_y, from_y, from_z, out, real, imag, er, ei):
-    rows_loop(real.shape[0], 2, lambda x: forward(fine[x], to_z, to_y, real, imag, x))
+    def body(xs, first):
+        for t, row in zip(xs, restrict_rows(lambda x: fine[x], down_y, down_z, xs)):
+            out[t] = jnp.where(t < valid[0], row, 0.0).astype(BF)
+
+    batches(out.shape[0], 10, body)
+
+
+def fine_kernel(fine, kr, kd, ks, to_z, to_y, from_y, from_z, out, real, imag, er, ei, ahead, back):
+    to_frequencies_z(lambda x: fine[x], real.shape[0], 4, to_z, ahead)
+    to_frequencies_y(ahead, 4, to_y, real, imag)
     along_x(real, imag, (kr, kd, ks), er, ei, 8)
-
-    def body(x):
-        out[x] = backward(er[x], ei[x], from_y, from_z)
-
-    rows_loop(out.shape[0], 2, body)
+    from_frequencies_y(er, ei, 4, from_y, back)
+
+    def write(x, value):
+        out[x] = value
+
+    from_frequencies_z(back, out.shape[0], 4, from_z, write)
 
 
 def coarse_kernel(
@@ -249,36 +316,43 @@
     t_er,
     t_ei,
     t_out,
+    m_ahead,
+    m_back,
+    t_cells,
+    t_ahead,
+    t_back,
 ):
     skip = (mid.shape[0] - m_real.shape[0]) // 2
     cols = (mid.shape[1] - m_real.shape[1]) // 2
 
-    def mid_body(x):
-        cells = mid[x + skip, cols : cols + m_real.shape[1], :]
-        forward(cells, m_to_z, m_to_y, m_real, m_imag, x)
-
-    rows_loop(m_real.shape[0], 1, mid_body)
-
-    def top_body(t):
-        row = restrict_row(mid[2 * t], mid[2 * t + 1], mid[2 * t + 2], down_y, down_z)
-        row = jnp.where(t < valid[0], row, 0.0).astype(BF)
-        forward(row, t_to_z, t_to_y, t_real, t_imag, t)
-
-    rows_loop(t_real.shape[0], 1, top_body)
+    def mid_cells(x):
+        return mid[x + skip, cols : cols + m_real.shape[1], :]
+
+    to_frequencies_z(mid_cells, m_real.shape[0], 9, m_to_z, m_ahead)
+    to_frequencies_y(m_ahead, 9, m_to_y, m_real, m_imag)
+
+    def restrict_body(xs, first):
+        for t, row in zip(xs, restrict_rows(lambda x: mid[x], down_y, down_z, xs)):
+            t_cells[t] = jnp.where(t < valid[0], row, 0.0).astype(BF)
+
+    batches(t_real.shape[0], 7, restrict_body)
+    to_frequencies_z(lambda x: t_cells[x], t_real.shape[0], 7, t_to_z, t_ahead)
+    to_frequencies_y(t_ahead, 7, t_to_y, t_real, t_imag)
     along_x(m_real, m_imag, (mr, md, ms), m_er, m_ei, 7)
     along_x(t_real, t_imag, (tr, td, ts), t_er, t_ei, 7)
 
-    def top_out(x):
-        t_out[x] = backward(t_er[x], t_ei[x], t_from_y, t_from_z)
-
-    rows_loop(t_out.shape[0], 1, top_out)
+    def top_write(x, value):
+        t_out[x] = value
+
+    def mid_write(x, value):
+        m_out[x] = value
+
+    from_frequencies_y(t_er, t_ei, 7, t_from_y, t_back)
+    from_frequencies_y(m_er, m_ei, 7, m_from_y, m_back)
+    from_frequencies_z(t_back, t_out.shape[0], 7, t_from_z, top_write)
+    from_frequencies_z(m_back, m_out.shape[0], 7, m_from_z, mid_write)
     last = t_out.shape[0] - 1
     t_out[last] = t_out[last] * inside[0]
-
-    def mid_out(x):
-        m_out[x] = backward(m_er[x], m_ei[x], m_from_y, m_from_z)
-
-    rows_loop(m_out.shape[0], 1, mid_out)
     for i in range(last):
         m_out[2 * i] += t_out[i]
         m_out[2 * i + 1] += 0.5 * (t_out[i] + t_out[i + 1])
@@ -288,7 +362,7 @@
         out[2 * i] = fine_e[2 * i] + m_out[i]
         out[2 * i + 1] = fine_e[2 * i + 1] + 0.5 * (m_out[i] + m_out[i + 1])
 
-    rows_loop(out.shape[0] // 2, 1, finish)
+    rows_loop(out.shape[0] // 2, 2, finish)
 
 
 def call(kernel, outs, scratch, scalars, args):
@@ -299,9 +373,23 @@
         out_shape=outs,
         in_specs=[smem] * len(scalars) + [vmem] * len(args),
         out_specs=jax.tree.map(lambda _: vmem, outs),
-        scratch_shapes=[pltpu.VMEM(shape, F32) for shape in scratch],
+        scratch_shapes=[pltpu.VMEM(shape, dtype) for dtype, shape in scratch],
         compiler_params=pltpu.CompilerParams(vmem_limit_bytes=60 << 20),
     )(*scalars, *args)
+
+
+def spectrum_scratch(level):
+    return [
+        (F32, (rows, level.period_y, LANES))
+        for rows in (level.in_x, level.in_x, level.out_x, level.out_x)
+    ]
+
+
+def terms_scratch(level, out_rows):
+    return [
+        (BF, (2, level.in_x * level.period_y, 2 * LANES)),
+        (BF, (2, level.out_x * out_rows, 2 * LANES)),
+    ]
 
 
 def shifted(value, axis, by):
@@ -356,7 +444,7 @@
     spectra = call(
         functools.partial(spectra_kernel, taps),
         outs,
-        [(taps * 16, 2 * LANES)],
+        [(F32, (taps * 16, 2 * LANES))],
         [],
         [cells, *tables],
     )
@@ -404,7 +492,7 @@
     fine_e = call(
         fine_kernel,
         jax.ShapeDtypeStruct((nx, ny, nz), F32),
-        [(fine.in_x, fine.period_y, LANES)] * 2 + [(nx, fine.period_y, LANES)] * 2,
+        spectrum_scratch(fine) + terms_scratch(fine, ny),
         [],
         [
             fine_ext,
@@ -430,12 +518,13 @@
     return call(
         coarse_kernel,
         jax.ShapeDtypeStruct((nx, ny, nz), F32),
-        [(mid.in_x, mid.period_y, LANES)] * 2
-        + [(mid.out_x, mid.period_y, LANES)] * 2
-        + [(mid.out_x, ny, nz)]
-        + [(top.in_x, top.period_y, LANES)] * 2
-        + [(top.out_x, top.period_y, LANES)] * 2
-        + [(top.out_x, ny, nz)],
+        spectrum_scratch(mid)
+        + [(F32, (mid.out_x, ny, nz))]
+        + spectrum_scratch(top)
+        + [(F32, (top.out_x, ny, nz))]
+        + terms_scratch(mid, ny)
+        + [(BF, (top.in_x, top.period_y, tz))]
+        + terms_scratch(top, ny),
         [valid, inside],
         [
             mid_ext,

time: 105 us -> 73.6 us (0.70)
  the two profiles are of different devices: /device:TPU:11 before, /device:TPU:19 now
where the time goes in v2:
time: 73.6 us; the launch traced here: 73.1 us
  Pallas kernels  31.7 us (43%)
  starting transfers between devices  22.5 us (31%)
  waiting for transfers between devices  10.6 us (14%)
  other arithmetic  6.96 us (9%)
  local copies, waits for them, and re-layouts  1.07 us (1%)
    pallas_call x4, Pallas kernels, call(): pl.pallas_call(kernel, out_shape=outs, in_specs=[smem] * len(scalars) + [...  31.7 us
    ppermute x8, starting transfers between devices, shifted(): lax.ppermute(value, axis, [(i, i + by) for i in range(length) if 0 <= i +...  22.5 us
    ppermute x8, waiting for transfers between devices, shifted(): lax.ppermute(value, axis, [(i, i + by) for i in range(length) if 0 <= i +...  10.6 us
  transfers between devices with their start and end apart: 8, of which 3 were waited for; matrix products, arithmetic and copies ran while one was open for 4% of the time, Pallas kernels for 26%

profile of v2, /device:TPU:19, one launch (start us, length us, event | category | flops | bytes accessed | tf_op | source)
XLA Modules:
  0.0 73.1 jit_solution(1831464105100602662)
XLA Ops:
  0.0 0.0 copy-start.7
  0.0 1.2 %convert_element_type.7 = bf16[24,64,128]{2,1,0:T(8,128)(2,1)S(1)} convert(f32[24,64,128]{2,1,0:T(8,128)} %param.28) | non-fusion elementwise | flops 196608 | bytes 1179648 | tf_op jit(solution)/shard_map/convert_element_type | solution.py:452
  1.3 2.2 %collective-permute-start.1 = (bf16[8,64,128]{2,1,0:T(8,128)(2,1)S(1)}, bf16[8,64,128]{2,1,0:T(8,128)(2,1)S(1)}, u32[]{:S(2)}, u32[]{:S(2)}) collective-permute-start(bf16[8,64,128]{2,1,0:T(8,128)(2,1)S(1)} %slice.33), channel_id=1, source_target_pairs={{4,0},{8,4},{12,8},{16,12},{20,16},{24,20},{28,24},{5,1},{9,5},{13... | collective-permute-start | bytes 393224 | tf_op jit(solution)/shard_map/ppermute | solution.py:397
  3.5 4.0 %collective-permute-start = (bf16[7,64,128]{2,1,0:T(8,128)(2,1)S(1)}, bf16[7,64,128]{2,1,0:T(8,128)(2,1)S(1)}, u32[]{:S(2)}, u32[]{:S(2)}) collective-permute-start(bf16[7,64,128]{2,1,0:T(8,128)(2,1)S(1)} %slice.32), channel_id=1, source_target_pairs={{0,4},{4,8},{8,12},{12,16},{16,20},{20,24},{24,28},{1,5},{5,9},{9,... | collective-permute-start | bytes 344072 | tf_op jit(solution)/shard_map/ppermute | solution.py:397
  7.5 0.6 broadcast_select_fusion.m_from_y
  8.2 0.6 broadcast_select_fusion.1.t_from_y
  8.8 3.2 %collective-permute-done = bf16[7,64,128]{2,1,0:T(8,128)(2,1)S(1)} collective-permute-done((bf16[7,64,128]{2,1,0:T(8,128)(2,1)S(1)}, bf16[7,64,128]{2,1,0:T(8,128)(2,1)S(1)}, u32[]{:S(2)}, u32[]{:S(2)}) %collective-permute-start) | collective-permute-done | bytes 114720 | tf_op jit(solution)/shard_map/ppermute | solution.py:397
  11.9 0.0 collective-permute-done.1
  12.0 3.5 %collective-permute-start.2 = (bf16[39,8,128]{2,1,0:T(8,128)(2,1)S(1)}, bf16[39,8,128]{2,1,0:T(8,128)(2,1)S(1)}, u32[]{:S(2)}, u32[]{:S(2)}) collective-permute-start(bf16[39,8,128]{2,1,0:T(8,128)(2,1)S(1)} %get-tuple-element.23), channel_id=1, source_target_pairs={{0,1},{1,2},{2,3},{4,5},{5,6},{6,7},{8,9},{9,10},{10,11},{12,13},{... | collective-permute-start | bytes 239624 | tf_op jit(solution)/shard_map/ppermute | solution.py:397
  15.5 1.9 %collective-permute-start.3 = (bf16[39,8,128]{2,1,0:T(8,128)(2,1)S(1)}, bf16[39,8,128]{2,1,0:T(8,128)(2,1)S(1)}, u32[]{:S(2)}, u32[]{:S(2)}) collective-permute-start(bf16[39,8,128]{2,1,0:T(8,128)(2,1)S(1)} %get-tuple-element.24), channel_id=1, source_target_pairs={{1,0},{2,1},{3,2},{5,4},{6,5},{7,6},{9,8},{10,9},{11,10},{13,12},{... | collective-permute-start | bytes 239624 | tf_op jit(solution)/shard_map/ppermute | solution.py:397
  17.5 0.0 collective-permute-done.2
  17.5 3.8 %collective-permute-done.3 = bf16[39,8,128]{2,1,0:T(8,128)(2,1)S(1)} collective-permute-done((bf16[39,8,128]{2,1,0:T(8,128)(2,1)S(1)}, bf16[39,8,128]{2,1,0:T(8,128)(2,1)S(1)}, u32[]{:S(2)}, u32[]{:S(2)}) %collective-permute-start.3) | collective-permute-done | bytes 79904 | tf_op jit(solution)/shard_map/ppermute | solution.py:397
  21.2 1.0 %pad_maximum_fusion.fine = bf16[39,80,128]{2,1,0:T(8,128)(2,1)} fusion(bf16[39,8,128]{2,1,0:T(8,128)(2,1)S(1)} %collective-permute-done.3, bf16[8,64,128]{2,1,0:T(8,128)(2,1)S(1)} %collective-permute-done.1, bf16[24,64,128]{2,1,0:T(8,128)(2,1)S(1)} %convert_element_type.7, bf16[7,64,128]{2,1,0:T(8,128)(2,1)S(1)} %collective-permute-done, ...), kind=kLoop, calls=%fused_computation | loop fusion | flops 3993600 | bytes 1597440 | tf_op jit(solution)/shard_map/concatenate | solution.py:456
  22.2 2.6 %shard_map.262 = bf16[19,32,64]{2,1,0:T(8,128)(2,1)} custom-call(s32[1]{0:T(128)} %bitcast.2.valid, bf16[39,80,128]{2,1,0:T(8,128)(2,1)} %pad_maximum_fusion.fine, bf16[32,240]{1,0:T(8,128)(2,1)} %constant.90.clone.down_y, bf16[128,64]{1,0:T(8,128)(2,1)} %constant.91.clone.down_z), custom_call_target="tpu_custom_call" | custom-call | tf_op jit(solution)/shard_map/pallas_call | solution.py:371
  24.8 1.0 %fusion.10 = (bf16[12,32,64]{2,1,0:T(8,128)(2,1)S(1)}, bf16[12,32,64]{2,1,0:T(8,128)(2,1)S(1)}) fusion(bf16[19,32,64]{2,1,0:T(8,128)(2,1)} %shard_map.262), kind=kLoop, calls=%fused_computation.22 | loop fusion | bytes 196608 | tf_op jit(solution)/shard_map/slice | solution.py:477
  25.8 0.0 copy-start.3
  25.8 0.0 copy-start.4
  25.8 0.0 copy-start.5
  25.9 3.7 %collective-permute-start.4 = (bf16[12,32,64]{2,1,0:T(8,128)(2,1)S(1)}, bf16[12,32,64]{2,1,0:T(8,128)(2,1)S(1)}, u32[]{:S(2)}, u32[]{:S(2)}) collective-permute-start(bf16[12,32,64]{2,1,0:T(8,128)(2,1)S(1)} %get-tuple-element.27), channel_id=1, source_target_pairs={{0,4},{4,8},{8,12},{12,16},{16,20},{20,24},{24,28},{1,5},{5,9},{9,... | collective-permute-start | bytes 147464 | tf_op jit(solution)/shard_map/ppermute | solution.py:397
  29.6 1.9 %collective-permute-start.5 = (bf16[12,32,64]{2,1,0:T(8,128)(2,1)S(1)}, bf16[12,32,64]{2,1,0:T(8,128)(2,1)S(1)}, u32[]{:S(2)}, u32[]{:S(2)}) collective-permute-start(bf16[12,32,64]{2,1,0:T(8,128)(2,1)S(1)} %get-tuple-element.28), channel_id=1, source_target_pairs={{4,0},{8,4},{12,8},{16,12},{20,16},{24,20},{28,24},{5,1},{9,5},{13... | collective-permute-start | bytes 147464 | tf_op jit(solution)/shard_map/ppermute | solution.py:397
  31.5 0.7 broadcast_select_fusion.2.down_y
  32.2 3.6 %collective-permute-done.5 = bf16[12,32,64]{2,1,0:T(8,128)(2,1)S(1)} collective-permute-done((bf16[12,32,64]{2,1,0:T(8,128)(2,1)S(1)}, bf16[12,32,64]{2,1,0:T(8,128)(2,1)S(1)}, u32[]{:S(2)}, u32[]{:S(2)}) %collective-permute-start.5) | collective-permute-done | bytes 49184 | tf_op jit(solution)/shard_map/ppermute | solution.py:397
  35.8 1.0 %pad_maximum_fusion.2 = bf16[43,32,64]{2,1,0:T(8,128)(2,1)S(1)} fusion(bf16[12,32,64]{2,1,0:T(8,128)(2,1)S(1)} %collective-permute-done.5, bf16[19,32,64]{2,1,0:T(8,128)(2,1)} %shard_map.262, bf16[12,32,64]{2,1,0:T(8,128)(2,1)S(1)} %collective-permute-done.4), kind=kLoop, calls=%fused_computation.8 | loop fusion | flops 176128 | bytes 352256 | tf_op jit(solution)/shard_map/concatenate | solution.py:475
  36.9 3.3 %collective-permute-start.6 = (bf16[43,16,64]{2,1,0:T(8,128)(2,1)S(1)}, bf16[43,16,64]{2,1,0:T(8,128)(2,1)S(1)}, u32[]{:S(2)}, u32[]{:S(2)}) collective-permute-start(bf16[43,16,64]{2,1,0:T(8,128)(2,1)S(1)} %get-tuple-element.25), channel_id=1, source_target_pairs={{0,1},{1,2},{2,3},{4,5},{5,6},{6,7},{8,9},{9,10},{10,11},{12,13},{... | collective-permute-start | bytes 264200 | tf_op jit(solution)/shard_map/ppermute | solution.py:397
  40.2 1.9 %collective-permute-start.7 = (bf16[43,16,64]{2,1,0:T(8,128)(2,1)S(1)}, bf16[43,16,64]{2,1,0:T(8,128)(2,1)S(1)}, u32[]{:S(2)}, u32[]{:S(2)}) collective-permute-start(bf16[43,16,64]{2,1,0:T(8,128)(2,1)S(1)} %get-tuple-element.26), channel_id=1, source_target_pairs={{1,0},{2,1},{3,2},{5,4},{6,5},{7,6},{9,8},{10,9},{11,10},{13,12},{... | collective-permute-start | bytes 264200 | tf_op jit(solution)/shard_map/ppermute | solution.py:397
  42.1 0.8 %fusion.8 = bf16[3,15,16,128]{3,2,1,0:T(8,128)(2,1)} fusion(bf16[1,15,15,15]{3,2,1,0:T(8,128)(2,1)S(1)} %bitcast.8, bf16[1,15,15,15]{3,2,1,0:T(8,128)(2,1)S(1)} %bitcast.9, bf16[1,15,15,15]{3,2,1,0:T(8,128)(2,1)S(1)} %bitcast.10), kind=kLoop, calls=%fused_computation.13 | loop fusion | flops 1382400 | bytes 204570 | tf_op jit(solution)/shard_map/stack | solution.py:434
  42.9 5.2 %shard_map.263 = (f32[15,80,128]{2,1,0:T(8,128)}, f32[15,80,128]{2,1,0:T(8,128)}, f32[15,80,128]{2,1,0:T(8,128)}, f32[15,48,128]{2,1,0:T(8,128)}, f32[15,48,128]...) custom-call(bf16[3,240,128]{2,1,0:T(8,128)(2,1)} %bitcast.7, ...), custom_call_target="tpu_custom_call" | custom-call | tf_op jit(solution)/shard_map/pallas_call | solution.py:371
  48.1 14.0 %shard_map.264.fine_e = f32[24,64,128]{2,1,0:T(8,128)} custom-call(bf16[39,80,128]{2,1,0:T(8,128)(2,1)} %pad_maximum_fusion.fine, f32[15,80,128]{2,1,0:T(8,128)} %get-tuple-element.14.kr, f32[15,80,128]{2,1,0:T(8,128)} %get-tuple-element.15.kd, f32[15,80,128]{2,1,0:T(8,128)} %get-tuple-element.16.ks, bf16[256,256]{1,0:T(8,128)(2,1)} %constant.92.clone.to_z, ...), custom_call_target="tpu_custom_call" | custom-call | tf_op jit(solution)/shard_map/pallas_call | solution.py:371
  62.1 0.0 collective-permute-done.6
  62.1 0.0 collective-permute-done.7
  62.1 1.1 %pad_maximum_fusion.1.mid = bf16[43,64,64]{2,1,0:T(8,128)(2,1)} fusion(bf16[43,16,64]{2,1,0:T(8,128)(2,1)S(1)} %collective-permute-done.7, bf16[12,32,64]{2,1,0:T(8,128)(2,1)S(1)} %collective-permute-done.5, bf16[19,32,64]{2,1,0:T(8,128)(2,1)S(1)} %copy-done, bf16[12,32,64]{2,1,0:T(8,128)(2,1)S(1)} %collective-permute-done.4, ...), kind=kLoop, calls=%fused_computation.1 | loop fusion | flops 1761280 | bytes 704512 | tf_op jit(solution)/shard_map/concatenate | solution.py:483
  63.2 9.9 %shard_map.265 = f32[24,64,128]{2,1,0:T(8,128)} custom-call(s32[1]{0:T(128)} %bitcast.valid, f32[1]{0:T(128)} %bitcast.1.inside, bf16[43,64,64]{2,1,0:T(8,128)(2,1)} %pad_maximum_fusion.1.mid, f32[24,64,128]{2,1,0:T(8,128)} %shard_map.264.fine_e, bf16[32,192]{1,0:T(8,128)(2,1)} %broadcast_select_fusion.2.down_y, bf16[64,32]{1,0:T(8,128)(2,1)} %constant.101.clone.down_z, ...), custom_call_target="tpu_custom_call" | custom-call | tf_op jit(solution)/shard_map/pallas_call | solution.py:371
  (20 shorter events, 0.1 us)
Async XLA Ops:
  0.0 7.5 %copy-start.1 = (bf16[128,144]{1,0:T(8,128)(2,1)S(1)}, bf16[128,144]{1,0:T(8,128)(2,1)}, u32[]{:S(2)}) copy-start(bf16[128,144]{1,0:T(8,128)(2,1)} %constant.97.clone) | copy-start | bytes 110596
  0.0 7.5 %copy-start.2 = (bf16[128,144]{1,0:T(8,128)(2,1)S(1)}, bf16[128,144]{1,0:T(8,128)(2,1)}, u32[]{:S(2)}) copy-start(bf16[128,144]{1,0:T(8,128)(2,1)} %constant.98.clone) | copy-start | bytes 110596
  0.0 8.1 %copy-start.6 = (bf16[128,96]{1,0:T(8,128)(2,1)S(1)}, bf16[128,96]{1,0:T(8,128)(2,1)}, u32[]{:S(2)}) copy-start(bf16[128,96]{1,0:T(8,128)(2,1)} %constant.100.clone) | copy-start | bytes 73732
  0.0 8.1 %copy-start.7 = (bf16[128,96]{1,0:T(8,128)(2,1)S(1)}, bf16[128,96]{1,0:T(8,128)(2,1)}, u32[]{:S(2)}) copy-start(bf16[128,96]{1,0:T(8,128)(2,1)} %constant.99.clone) | copy-start | bytes 73732
  1.3 10.7 %collective-permute-start.1 = (bf16[8,64,128]{2,1,0:T(8,128)(2,1)S(1)}, bf16[8,64,128]{2,1,0:T(8,128)(2,1)S(1)}, u32[]{:S(2)}, u32[]{:S(2)}) collective-permute-start(bf16[8,64,128]{2,1,0:T(8,128)(2,1)S(1)} %slice.33), channel_id=1, source_target_pairs={{4,0},{8,4},{12,8},{16,12},{20,16},{24,20},{28,24},{5,1},{9,5},{13... | collective-permute-start | bytes 393224 | tf_op jit(solution)/shard_map/ppermute | solution.py:397
  3.5 8.5 %collective-permute-start = (bf16[7,64,128]{2,1,0:T(8,128)(2,1)S(1)}, bf16[7,64,128]{2,1,0:T(8,128)(2,1)S(1)}, u32[]{:S(2)}, u32[]{:S(2)}) collective-permute-start(bf16[7,64,128]{2,1,0:T(8,128)(2,1)S(1)} %slice.32), channel_id=1, source_target_pairs={{0,4},{4,8},{8,12},{12,16},{16,20},{20,24},{24,28},{1,5},{5,9},{9,... | collective-permute-start | bytes 344072 | tf_op jit(solution)/shard_map/ppermute | solution.py:397
  12.0 5.5 %collective-permute-start.2 = (bf16[39,8,128]{2,1,0:T(8,128)(2,1)S(1)}, bf16[39,8,128]{2,1,0:T(8,128)(2,1)S(1)}, u32[]{:S(2)}, u32[]{:S(2)}) collective-permute-start(bf16[39,8,128]{2,1,0:T(8,128)(2,1)S(1)} %get-tuple-element.23), channel_id=1, source_target_pairs={{0,1},{1,2},{2,3},{4,5},{5,6},{6,7},{8,9},{9,10},{10,11},{12,13},{... | collective-permute-start | bytes 239624 | tf_op jit(solution)/shard_map/ppermute | solution.py:397
  15.5 5.7 %collective-permute-start.3 = (bf16[39,8,128]{2,1,0:T(8,128)(2,1)S(1)}, bf16[39,8,128]{2,1,0:T(8,128)(2,1)S(1)}, u32[]{:S(2)}, u32[]{:S(2)}) collective-permute-start(bf16[39,8,128]{2,1,0:T(8,128)(2,1)S(1)} %get-tuple-element.24), channel_id=1, source_target_pairs={{1,0},{2,1},{3,2},{5,4},{6,5},{7,6},{9,8},{10,9},{11,10},{13,12},{... | collective-permute-start | bytes 239624 | tf_op jit(solution)/shard_map/ppermute | solution.py:397
  22.2 9.3 %copy-start.8 = (bf16[32,192]{1,0:T(8,128)(2,1)S(1)}, bf16[32,192]{1,0:T(8,128)(2,1)}, u32[]{:S(2)}) copy-start(bf16[32,192]{1,0:T(8,128)(2,1)} %constant.96.clone) | copy-start | bytes 36868
  25.8 16.3 %copy-start.3 = (bf16[15,15,15]{2,1,0:T(8,128)(2,1)S(1)}, bf16[15,15,15]{2,1,0:T(8,128)(2,1)}, u32[]{:S(2)}) copy-start(bf16[15,15,15]{2,1,0:T(8,128)(2,1)} %param.31) | copy-start | bytes 20254
  25.8 16.3 %copy-start.4 = (bf16[15,15,15]{2,1,0:T(8,128)(2,1)S(1)}, bf16[15,15,15]{2,1,0:T(8,128)(2,1)}, u32[]{:S(2)}) copy-start(bf16[15,15,15]{2,1,0:T(8,128)(2,1)} %param.30) | copy-start | bytes 20254
  25.8 16.3 %copy-start.5 = (bf16[15,15,15]{2,1,0:T(8,128)(2,1)S(1)}, bf16[15,15,15]{2,1,0:T(8,128)(2,1)}, u32[]{:S(2)}) copy-start(bf16[15,15,15]{2,1,0:T(8,128)(2,1)} %param.29) | copy-start | bytes 20254
  25.9 6.3 %collective-permute-start.4 = (bf16[12,32,64]{2,1,0:T(8,128)(2,1)S(1)}, bf16[12,32,64]{2,1,0:T(8,128)(2,1)S(1)}, u32[]{:S(2)}, u32[]{:S(2)}) collective-permute-start(bf16[12,32,64]{2,1,0:T(8,128)(2,1)S(1)} %get-tuple-element.27), channel_id=1, source_target_pairs={{0,4},{4,8},{8,12},{12,16},{16,20},{20,24},{24,28},{1,5},{5,9},{9,... | collective-permute-start | bytes 147464 | tf_op jit(solution)/shard_map/ppermute | solution.py:397
  29.6 6.3 %collective-permute-start.5 = (bf16[12,32,64]{2,1,0:T(8,128)(2,1)S(1)}, bf16[12,32,64]{2,1,0:T(8,128)(2,1)S(1)}, u32[]{:S(2)}, u32[]{:S(2)}) collective-permute-start(bf16[12,32,64]{2,1,0:T(8,128)(2,1)S(1)} %get-tuple-element.28), channel_id=1, source_target_pairs={{4,0},{8,4},{12,8},{16,12},{20,16},{24,20},{28,24},{5,1},{9,5},{13... | collective-permute-start | bytes 147464 | tf_op jit(solution)/shard_map/ppermute | solution.py:397
  36.9 25.2 %collective-permute-start.6 = (bf16[43,16,64]{2,1,0:T(8,128)(2,1)S(1)}, bf16[43,16,64]{2,1,0:T(8,128)(2,1)S(1)}, u32[]{:S(2)}, u32[]{:S(2)}) collective-permute-start(bf16[43,16,64]{2,1,0:T(8,128)(2,1)S(1)} %get-tuple-element.25), channel_id=1, source_target_pairs={{0,1},{1,2},{2,3},{4,5},{5,6},{6,7},{8,9},{9,10},{10,11},{12,13},{... | collective-permute-start | bytes 264200 | tf_op jit(solution)/shard_map/ppermute | solution.py:397
  40.2 21.9 %collective-permute-start.7 = (bf16[43,16,64]{2,1,0:T(8,128)(2,1)S(1)}, bf16[43,16,64]{2,1,0:T(8,128)(2,1)S(1)}, u32[]{:S(2)}, u32[]{:S(2)}) collective-permute-start(bf16[43,16,64]{2,1,0:T(8,128)(2,1)S(1)} %get-tuple-element.26), channel_id=1, source_target_pairs={{1,0},{2,1},{3,2},{5,4},{6,5},{7,6},{9,8},{10,9},{11,10},{13,12},{... | collective-permute-start | bytes 264200 | tf_op jit(solution)/shard_map/ppermute | solution.py:397
  48.1 14.0 %copy-start = (bf16[19,32,64]{2,1,0:T(8,128)(2,1)S(1)}, bf16[19,32,64]{2,1,0:T(8,128)(2,1)}, u32[]{:S(2)}) copy-start(bf16[19,32,64]{2,1,0:T(8,128)(2,1)} %shard_map.262) | copy-start | bytes 233476

commit v3 on v2

--- a/solution.py
+++ b/solution.py
@@ -41,6 +41,11 @@
 
 def up_closed(count):
     return up(count)[:, :count]
+
+
+def both_sides(table):
+    size = table.shape[0]
+    return [np.pad(table, ((at, LANES - size - at), (0, 0))) for at in (0, LANES - size)]
 
 
 class Level:
@@ -55,7 +60,9 @@
         freq_y = np.arange(period_y)
         turn_z, turn_y = 2 * np.pi / period_z, 2 * np.pi / period_y
         angle = turn_z * np.outer(np.arange(size_z), freq_z)
-        self.to_z = np.concatenate(two(beside(np.cos(angle), -np.sin(angle))), 0)
+        table = beside(np.cos(angle), -np.sin(angle))
+        self.to_z = np.concatenate(two(table), 0)
+        self.to_z_packed = [np.concatenate(two(side), 0) for side in both_sides(table)]
         angle = turn_y * np.outer(freq_y, np.arange(period_y))
         self.to_y = three_terms(np.concatenate([np.cos(angle), np.sin(angle)], 0))
         offsets = np.arange(taps) - half
@@ -206,7 +213,7 @@
                 for i in range(count):
                     x = start + i + a
                     if x not in seen:
-                        r, m = real[x, rows, :], imag[x, rows, :]
+                        r, m = real(x, rows), imag(x, rows)
                         seen[x] = r + m, r, m
                     for k in range(3):
                         term = weights[k] * seen[x][k]
@@ -230,29 +237,24 @@
         body(x)
 
 
-def restrict_rows(read, down_y, down_z, xs):
-    rows = down_y.shape[0]
-    totals = [
-        0.5 * read(2 * x).astype(F32) + read(2 * x + 1).astype(F32) + 0.5 * read(2 * x + 2).astype(F32)
-        for x in xs
-    ]
-    totals = [dot(down_y[...], jnp.concatenate(split(total, 3), 0)) for total in totals]
-    parts = split(jnp.concatenate(totals, 0), 3)
-    value = sum(dot(part, down_z[...]) for part in reversed(parts))
-    return [value[k * rows : (k + 1) * rows] for k in range(len(xs))]
-
-
-def spectra_kernel(taps, kernels, *refs):
-    levels = kernels.shape[0]
-    tables, outs, mid = refs[: 2 * levels], refs[2 * levels : -1], refs[-1]
+def all_terms(value):
+    return jnp.concatenate(split(value, 3), 0)
+
+
+def spectra_kernel(levels, *refs):
+    kernels, refs = refs[:levels], refs[levels:]
+    tables, outs, (padded, mid) = refs[: 2 * levels], refs[2 * levels : -2], refs[-2:]
+    taps = kernels[0].shape[0]
+    padded[...] = jnp.zeros(padded.shape, padded.dtype)
     for level in range(levels):
         kernel_z, kernel_y = tables[2 * level : 2 * level + 2]
-        out_r, out_d, out_s = outs[3 * level : 3 * level + 3]
-        period = out_r.shape[1]
-        cells = kernels[level]
+        outs_here = outs[3 * level : 3 * level + 3]
+        period = outs_here[0].shape[1]
+        padded[:, :taps, :taps] = kernels[level][...].astype(F32)
+        cells = padded[...].astype(BF).reshape(taps * padded.shape[1], LANES)
         mid[...] = dot(jnp.concatenate([cells, cells], 1), kernel_z[...])
 
-        def body(xs, first, kernel_y=kernel_y, outs=(out_r, out_d, out_s), period=period):
+        def body(xs, first, kernel_y=kernel_y, outs=outs_here, period=period):
             spreads = [dot(kernel_y[...], stacked(mid[rows_at(a, 16, 1), :])) for a in xs]
             for a, spread in zip(xs, spreads):
                 real = spread[:period, :LANES] - spread[period:, LANES:]
@@ -264,82 +266,240 @@
         batches(taps, 5, body)
 
 
-def restrict_kernel(valid, fine, down_y, down_z, out):
+def pack_kernel(
+    ended, own, left, right, down_z, down_y, ordered, near, coarse, to_right, to_left, far_right, far_left, part
+):
+    count, size = own.shape[:2]
+    side = left.shape[1]
+    width = near.shape[1]
+    start = side - (width - size) // 2
+    window = part.shape[1]
+
     def body(xs, first):
-        for t, row in zip(xs, restrict_rows(lambda x: fine[x], down_y, down_z, xs)):
-            out[t] = jnp.where(t < valid[0], row, 0.0).astype(BF)
-
-    batches(out.shape[0], 10, body)
-
-
-def fine_kernel(fine, kr, kd, ks, to_z, to_y, from_y, from_z, out, real, imag, er, ei, ahead, back):
-    to_frequencies_z(lambda x: fine[x], real.shape[0], 4, to_z, ahead)
+        rows = []
+        for x in xs:
+            l, o, r = left[x], own[x], right[x]
+            near[x] = jnp.concatenate([l[start:], o, r[: side - start]], 0)
+            low = jnp.concatenate([l, o[: window - side]], 0)
+            high = jnp.concatenate([o[size + side - window :], r], 0)
+            rows.append(jnp.concatenate([low, high], 1))
+        value = dot(jnp.concatenate(rows, 0), down_z[...])
+        for k, x in enumerate(xs):
+            part[x] = value[k * window : (k + 1) * window]
+
+    batches(count, 4, body)
+    half = down_y.shape[0] // 2
+    shape = (half, LANES)
+    high_lanes = lax.broadcasted_iota(jnp.int32, shape, 1) >= LANES // 2
+    outside = high_lanes & (lax.broadcasted_iota(jnp.int32, shape, 0) >= half // 2)
+    outside = outside & (ended[0] == 1)
+    last = count // 2
+    totals = []
+    for i in range(last + 1):
+        if i == 0:
+            total = part[0] + 0.5 * part[1]
+        elif i == last:
+            total = 0.5 * part[count - 1]
+        else:
+            total = 0.5 * part[2 * i - 1] + part[2 * i] + 0.5 * part[2 * i + 1]
+        totals.append(dot(down_y[...], all_terms(total)))
+    for i, total in enumerate(totals):
+        row = jnp.where(high_lanes, total[half:], total[:half])
+        row = jnp.where(outside, 0.0, row)
+        if i == 0:
+            for k, term in enumerate(split(row, 3)):
+                coarse[k] = term
+        elif i == last:
+            for k, term in enumerate(split(row, 3)):
+                coarse[last + 2 + k] = term
+        else:
+            coarse[i + 2] = row.astype(BF)
+    for out, rows in ((to_right, to_right.shape[0]), (to_left, to_left.shape[0])):
+        lines = rows - coarse.shape[0] * half
+        first = count - lines // width if out is to_right else 0
+        for x in range(lines // width):
+            out[x * width : (x + 1) * width, :] = near[first + x]
+        for k in range(coarse.shape[0]):
+            out[lines + k * half : lines + (k + 1) * half, :] = coarse[k]
+    shift = coarse.shape[0] - far_right.shape[0]
+    for k in range(far_right.shape[0]):
+        far_right[k] = coarse[shift + k]
+        far_left[k] = coarse[k]
+
+
+def own_kernel(near, to_z, to_y, real, imag, ahead):
+    to_frequencies_z(lambda x: near[x], real.shape[0], 4, to_z, ahead)
     to_frequencies_y(ahead, 4, to_y, real, imag)
-    along_x(real, imag, (kr, kd, ks), er, ei, 8)
-    from_frequencies_y(er, ei, 4, from_y, back)
-
-    def write(x, value):
-        out[x] = value
-
-    from_frequencies_z(back, out.shape[0], 4, from_z, write)
-
-
-def coarse_kernel(
-    valid,
-    inside,
-    mid,
-    fine_e,
-    down_y,
-    down_z,
+
+
+def final_kernel(
+    limits,
+    own_real,
+    own_imag,
+    from_left,
+    from_right,
+    far_left,
+    far_right,
+    coarse,
+    kr,
+    kd,
+    ks,
+    to_z,
+    to_y,
+    from_y,
+    from_z,
     mr,
     md,
     ms,
-    m_to_z,
+    m_low,
+    m_high,
     m_to_y,
     m_from_y,
     m_from_z,
     tr,
     td,
     ts,
+    t_down_y,
+    t_down_z,
     t_to_z,
     t_to_y,
     t_from_y,
     t_from_z,
     out,
+    side_real,
+    side_imag,
+    er,
+    ei,
+    ahead,
+    back,
+    mid,
     m_real,
     m_imag,
     m_er,
     m_ei,
+    m_ahead,
+    m_back,
     m_out,
     t_real,
     t_imag,
     t_er,
     t_ei,
-    t_out,
-    m_ahead,
-    m_back,
     t_cells,
     t_ahead,
     t_back,
+    t_out,
 ):
+    top_rows, ended_x, close_x, ended_y = limits[0], limits[1], limits[2], limits[3]
+    count, width = own_real.shape[:2]
+    reach = side_real.shape[0] // 2
+
+    def side_cells(x):
+        ref, first = (from_left, x) if x < reach else (from_right, x - reach)
+        return ref[first * width : (first + 1) * width, :]
+
+    period = width
+    for first in range(0, 2 * reach, 4):
+        xs = list(range(first, min(2 * reach, first + 4)))
+        cells = jnp.concatenate([side_cells(x) for x in xs], 0)
+        value = dot(jnp.concatenate([cells, cells], 1), to_z[...])
+        high, low = split(value, 2)
+        ahead[0, rows_at(first, period, len(xs)), :] = high
+        ahead[1, rows_at(first, period, len(xs)), :] = low
+    to_frequencies_y(ahead, 7, to_y, side_real, side_imag)
+
+    def source(own, side):
+        def read(x, rows):
+            if x < reach:
+                return side[x, rows, :]
+            if x < reach + count:
+                return own[x - reach, rows, :]
+            return side[x - count, rows, :]
+
+        return read
+
+    along_x(source(own_real, side_real), source(own_imag, side_imag), (kr, kd, ks), er, ei, 8)
+    from_frequencies_y(er, ei, 4, from_y, back)
+
+    def fine_write(x, value):
+        out[x] = value
+
+    from_frequencies_z(back, count, 4, from_z, fine_write)
+
+    half = mid.shape[1]
+    last = count // 2
+    skip_left = from_left.shape[0] - coarse.shape[0] * half
+    skip_right = from_right.shape[0] - coarse.shape[0] * half
+
+    def left_row(k):
+        return from_left[skip_left + k * half : skip_left + (k + 1) * half, :]
+
+    def right_row(k):
+        return from_right[skip_right + k * half : skip_right + (k + 1) * half, :]
+
+    def added(first, second, dropped=None):
+        value = sum(first(2 - k).astype(F32) for k in range(3))
+        value = value + sum(second(last + 4 - k).astype(F32) for k in range(3))
+        if dropped is not None:
+            value = jnp.where(dropped == 1, 0.0, value)
+        return value.astype(BF)
+
+    spare = far_left.shape[0] - 3
+    far_first = coarse.shape[0] - far_left.shape[0]
+    rows = [far_left[k] for k in range(spare)]
+    rows += [added(left_row, lambda k: far_left[k - far_first])]
+    rows += [left_row(k) for k in range(3, last + 2)]
+    rows += [added(lambda k: coarse[k], left_row)]
+    rows += [coarse[k] for k in range(3, last + 2)]
+    rows += [added(right_row, lambda k: coarse[k], ended_x)]
+    rows += [right_row(k) for k in range(3, last + 2)]
+    rows += [added(lambda k: far_right[k], right_row, close_x)]
+    rows += [far_right[k] for k in range(3, 3 + spare)]
+    for k, row in enumerate(rows):
+        mid[k] = row
+
     skip = (mid.shape[0] - m_real.shape[0]) // 2
-    cols = (mid.shape[1] - m_real.shape[1]) // 2
-
-    def mid_cells(x):
-        return mid[x + skip, cols : cols + m_real.shape[1], :]
-
-    to_frequencies_z(mid_cells, m_real.shape[0], 9, m_to_z, m_ahead)
+    m_width = m_real.shape[1]
+    cut = half - m_width // 2
+
+    def mid_z(xs, first):
+        cells = jnp.concatenate([mid[x + skip] for x in xs], 0)
+        cells = jnp.concatenate([cells, cells], 1)
+        low, high = dot(cells, m_low[...]), dot(cells, m_high[...])
+        parts = []
+        for k in range(len(xs)):
+            parts += [low[k * half + cut : (k + 1) * half], high[k * half : (k + 1) * half - cut]]
+        high, low = split(jnp.concatenate(parts, 0), 2)
+        m_ahead[0, rows_at(first, m_width, len(xs)), :] = high
+        m_ahead[1, rows_at(first, m_width, len(xs)), :] = low
+
+    batches(m_real.shape[0], 9, mid_z)
     to_frequencies_y(m_ahead, 9, m_to_y, m_real, m_imag)
 
-    def restrict_body(xs, first):
-        for t, row in zip(xs, restrict_rows(lambda x: mid[x], down_y, down_z, xs)):
-            t_cells[t] = jnp.where(t < valid[0], row, 0.0).astype(BF)
-
-    batches(t_real.shape[0], 7, restrict_body)
+    t_width = t_real.shape[1]
+    inside = lax.broadcasted_iota(jnp.int32, (t_width, t_cells.shape[2]), 0)
+    inside = inside < jnp.where(ended_y == 1, t_width - (t_width - last_columns(t_width, m_width)) // 2, t_width)
+
+    def top_cells(xs, first):
+        spreads = []
+        for t in xs:
+            total = 0.5 * mid[2 * t].astype(F32) + mid[2 * t + 1].astype(F32) + 0.5 * mid[2 * t + 2].astype(F32)
+            spreads.append(dot(t_down_y[...], all_terms(total)))
+        low = jnp.concatenate([spread[:t_width] for spread in spreads], 0)
+        high = jnp.concatenate([spread[t_width:] for spread in spreads], 0)
+        value = dot(jnp.concatenate(split(low, 3) + split(high, 3), 1), t_down_z[...])
+        for k, t in enumerate(xs):
+            row = jnp.where(inside, value[k * t_width : (k + 1) * t_width], 0.0)
+            t_cells[t] = jnp.where(t < top_rows, row, 0.0).astype(BF)
+
+    batches(t_real.shape[0], 7, top_cells)
     to_frequencies_z(lambda x: t_cells[x], t_real.shape[0], 7, t_to_z, t_ahead)
     to_frequencies_y(t_ahead, 7, t_to_y, t_real, t_imag)
-    along_x(m_real, m_imag, (mr, md, ms), m_er, m_ei, 7)
-    along_x(t_real, t_imag, (tr, td, ts), t_er, t_ei, 7)
+
+    def plain(ref):
+        return lambda x, rows: ref[x, rows, :]
+
+    along_x(plain(m_real), plain(m_imag), (mr, md, ms), m_er, m_ei, 7)
+    along_x(plain(t_real), plain(t_imag), (tr, td, ts), t_er, t_ei, 7)
 
     def top_write(x, value):
         t_out[x] = value
@@ -347,49 +507,55 @@
     def mid_write(x, value):
         m_out[x] = value
 
-    from_frequencies_y(t_er, t_ei, 7, t_from_y, t_back)
-    from_frequencies_y(m_er, m_ei, 7, m_from_y, m_back)
+    from_frequencies_y(t_er, t_ei, 7, t_from_y.at[ended_y], t_back)
+    from_frequencies_y(m_er, m_ei, 7, m_from_y.at[ended_y], m_back)
     from_frequencies_z(t_back, t_out.shape[0], 7, t_from_z, top_write)
     from_frequencies_z(m_back, m_out.shape[0], 7, m_from_z, mid_write)
-    last = t_out.shape[0] - 1
-    t_out[last] = t_out[last] * inside[0]
-    for i in range(last):
+    keep = jnp.where(ended_x == 1, 0.0, 1.0)
+    top = t_out.shape[0] - 1
+    t_out[top] = t_out[top] * keep
+    for i in range(top):
         m_out[2 * i] += t_out[i]
         m_out[2 * i + 1] += 0.5 * (t_out[i] + t_out[i + 1])
-    m_out[2 * last] = (m_out[2 * last] + t_out[last]) * inside[0]
+    m_out[2 * top] = (m_out[2 * top] + t_out[top]) * keep
 
     def finish(i):
-        out[2 * i] = fine_e[2 * i] + m_out[i]
-        out[2 * i + 1] = fine_e[2 * i + 1] + 0.5 * (m_out[i] + m_out[i + 1])
-
-    rows_loop(out.shape[0] // 2, 2, finish)
-
-
-def call(kernel, outs, scratch, scalars, args):
+        out[2 * i] += m_out[i]
+        out[2 * i + 1] += 0.5 * (m_out[i] + m_out[i + 1])
+
+    rows_loop(count // 2, 2, finish)
+
+
+def last_columns(t_width, m_width):
+    return m_width - t_width
+
+
+def call(kernel, outs, scratch, scalars, args, loose=()):
     vmem = pl.BlockSpec(memory_space=pltpu.VMEM)
     smem = pl.BlockSpec(memory_space=pltpu.SMEM)
     return pl.pallas_call(
         kernel,
         out_shape=outs,
-        in_specs=[smem] * len(scalars) + [vmem] * len(args),
+        in_specs=[
+            smem if i < len(scalars) else pl.BlockSpec(memory_space=pl.ANY) if i in loose else vmem
+            for i in range(len(scalars) + len(args))
+        ],
         out_specs=jax.tree.map(lambda _: vmem, outs),
         scratch_shapes=[pltpu.VMEM(shape, dtype) for dtype, shape in scratch],
         compiler_params=pltpu.CompilerParams(vmem_limit_bytes=60 << 20),
     )(*scalars, *args)
 
 
-def spectrum_scratch(level):
-    return [
-        (F32, (rows, level.period_y, LANES))
-        for rows in (level.in_x, level.in_x, level.out_x, level.out_x)
+def level_scratch(level, ny, nz, extra=()):
+    rows = [
+        (F32, (count, level.period_y, LANES))
+        for count in (level.in_x, level.in_x, level.out_x, level.out_x)
     ]
-
-
-def terms_scratch(level, out_rows):
-    return [
+    terms = [
         (BF, (2, level.in_x * level.period_y, 2 * LANES)),
-        (BF, (2, level.out_x * out_rows, 2 * LANES)),
+        (BF, (2, level.out_x * ny, 2 * LANES)),
     ]
+    return [*rows, *extra, *terms, (F32, (level.out_x, ny, nz))]
 
 
 def shifted(value, axis, by):
@@ -431,9 +597,6 @@
         up_closed(mz) @ up_closed(tz),
     )
 
-    cells = jnp.stack([kernel_fine, kernel_mid, kernel_top])
-    cells = jnp.pad(cells, ((0, 0), (0, 0), (0, 1), (0, LANES - taps)))
-    cells = cells.reshape(3, taps * 16, LANES)
     levels = (fine, mid, top)
     outs = [
         jax.ShapeDtypeStruct((taps, level.period_y, LANES), F32)
@@ -442,104 +605,117 @@
     ]
     tables = [table for level in levels for table in (level.kernel_z, level.kernel_y)]
     spectra = call(
-        functools.partial(spectra_kernel, taps),
+        functools.partial(spectra_kernel, 3),
         outs,
-        [(F32, (taps * 16, 2 * LANES))],
+        [(F32, (taps, 16, LANES)), (F32, (taps * 16, 2 * LANES))],
         [],
-        [cells, *tables],
+        [kernel_fine, kernel_mid, kernel_top, *tables],
     )
 
     fine_q = charges.astype(BF)
-    fine_x = jnp.concatenate(
-        [shifted(fine_q[-half:], "gx", 1), fine_q, shifted(fine_q[:wide], "gx", -1)], 0
-    )
-    fine_ext = jnp.concatenate(
-        [shifted(fine_x[:, -wide:], "gy", 1), fine_x, shifted(fine_x[:, :wide], "gy", -1)], 1
-    )
-
-    lead = (half - 1) // 2
-    rows = lead + nx // 2 + wide // 2
-    down_y = np.tile(down(my, wide, ny + 2 * wide), (1, 3)).astype(BF)
-    down_z = down(mz, 0, nz).T.astype(BF)
-    valid = jnp.where(left_x == 1, lead + nx // 2, rows)[None].astype(jnp.int32)
-    mid_q = call(
-        restrict_kernel,
-        jax.ShapeDtypeStruct((rows, my, mz), BF),
+    side = ny // 2
+    from_below = shifted(fine_q[:, ny - side :], "gy", 1)
+    from_above = shifted(fine_q[:, :side], "gy", -1)
+
+    window = side + ny // 2 + 16
+    packed = ny // 2
+    down_z = np.concatenate([np.pad(down(mz, 0, nz).T, ((0, 0), (at, mz - at))) for at in (0, mz)], 0)
+    shift = ny + 2 * side - window
+    down_y = np.concatenate([down(packed, 0, window), down(packed, 2 * packed - shift, window)], 0)
+    mx = nx // 2
+    lines = mx - 1 + 6
+    reach = 2 * half + 1 - mx
+    assert 0 < reach <= mx - 1 and 2 * mz == LANES == nz
+    ended = end_y.astype(jnp.int32)
+    shapes = [
+        (nx, fine.period_y, LANES),
+        (lines, packed, LANES),
+        (half * fine.period_y + lines * packed, LANES),
+        (half * fine.period_y + lines * packed, LANES),
+        (reach + 3, packed, LANES),
+        (reach + 3, packed, LANES),
+    ]
+    near, coarse, to_right, to_left, far_right, far_left = call(
+        pack_kernel,
+        [jax.ShapeDtypeStruct(shape, BF) for shape in shapes],
+        [(F32, (nx, window, LANES))],
+        [ended[None]],
+        [
+            fine_q,
+            from_below,
+            from_above,
+            down_z.astype(BF),
+            np.tile(down_y, (1, 3)).astype(BF),
+            spectra[0],
+        ],
+        loose=(6,),
+    )
+    from_left = shifted(to_right, "gx", 1)
+    from_right = shifted(to_left, "gx", -1)
+    from_far_left = shifted(far_right, "gx", 2)
+    from_far_right = shifted(far_left, "gx", -2)
+
+    own = call(
+        own_kernel,
+        [jax.ShapeDtypeStruct((nx, fine.period_y, LANES), F32)] * 2,
+        [(BF, (2, nx * fine.period_y, 2 * LANES))],
         [],
-        [valid],
-        [fine_ext, down_y, down_z],
-    )
-    mx = nx // 2
-    reach = 2 * half + 1
-    assert lead + mx >= reach and my >= 2 * wide
-    mid_x = jnp.concatenate(
+        [near, fine.to_z, fine.to_y],
+    )
+
+    tx = nx // 4
+    wide_top = ty + 2 * wide
+    t_down_y = down(wide_top, 0, 2 * packed)
+    t_down_y = np.concatenate([t_down_y[:, :packed], t_down_y[:, packed:]], 0)
+    t_down_z = np.concatenate(
+        [np.tile(table, (3, 1)) for table in both_sides(down(tz, 0, mz).T)], 0
+    )
+    limits = jnp.stack(
         [
-            shifted(mid_q[lead + mx - reach : mx], "gx", 1),
-            mid_q,
-            shifted(mid_q[rows - mx :], "gx", -1),
+            jnp.minimum(left_x * tx + half, top.in_x),
+            (left_x == 1).astype(jnp.int32),
+            (left_x <= 2).astype(jnp.int32),
+            ended,
+        ]
+    ).astype(jnp.int32)
+    return call(
+        final_kernel,
+        jax.ShapeDtypeStruct((nx, ny, nz), F32),
+        [
+            (F32, (2 * half, fine.period_y, LANES)),
+            (F32, (2 * half, fine.period_y, LANES)),
+            (F32, (nx, fine.period_y, LANES)),
+            (F32, (nx, fine.period_y, LANES)),
+            (BF, (2, 2 * half * fine.period_y, 2 * LANES)),
+            (BF, (2, nx * ny, 2 * LANES)),
+            (BF, (3 * mx + 1 + 2 * reach, packed, LANES)),
+            *level_scratch(mid, ny, nz),
+            *level_scratch(top, ny, nz, [(BF, (top.in_x, top.period_y, tz))]),
         ],
-        0,
-    )
-    mid_ext = jnp.concatenate(
+        [limits],
         [
-            shifted(mid_x[:, -2 * wide :], "gy", 1),
-            mid_x,
-            shifted(mid_x[:, : 2 * wide], "gy", -1),
-        ],
-        1,
-    )
-
-    fine_e = call(
-        fine_kernel,
-        jax.ShapeDtypeStruct((nx, ny, nz), F32),
-        spectrum_scratch(fine) + terms_scratch(fine, ny),
-        [],
-        [
-            fine_ext,
+            *own,
+            from_left,
+            from_right,
+            from_far_left,
+            from_far_right,
+            coarse,
             *spectra[:3],
             fine.to_z,
             fine.to_y,
             fine.from_y[0],
             fine.from_z,
-        ],
-    )
-
-    tx = nx // 4
-    down_y = down(ty + 2 * wide, 0, my + 4 * wide)
-    keep = jnp.arange(ty + 2 * wide)[:, None] < jnp.where(end_y, wide + ty, ty + 2 * wide)
-    down_y = jnp.where(keep, np.tile(down_y, (1, 3)).astype(BF), 0)
-    down_z = down(tz, 0, mz).T.astype(BF)
-    valid = jnp.minimum(left_x * tx + half, top.in_x)[None].astype(jnp.int32)
-    inside = jnp.where(left_x == 1, 0.0, 1.0)[None].astype(F32)
-
-    def pick(pair):
-        return jnp.where(end_y, pair[1], pair[0])
-
-    return call(
-        coarse_kernel,
-        jax.ShapeDtypeStruct((nx, ny, nz), F32),
-        spectrum_scratch(mid)
-        + [(F32, (mid.out_x, ny, nz))]
-        + spectrum_scratch(top)
-        + [(F32, (top.out_x, ny, nz))]
-        + terms_scratch(mid, ny)
-        + [(BF, (top.in_x, top.period_y, tz))]
-        + terms_scratch(top, ny),
-        [valid, inside],
-        [
-            mid_ext,
-            fine_e,
-            down_y,
-            down_z,
             *spectra[3:6],
-            mid.to_z,
+            *mid.to_z_packed,
             mid.to_y,
-            pick(mid.from_y),
+            np.stack(mid.from_y),
             mid.from_z,
-            *spectra[6:9],
+            *spectra[6:],
+            np.tile(t_down_y, (1, 3)).astype(BF),
+            t_down_z.astype(BF),
             top.to_z,
             top.to_y,
-            pick(top.from_y),
+            np.stack(top.from_y),
             top.from_z,
         ],
     )

time: 73.6 us -> 55 us (0.75)
  the two profiles are of different devices: /device:TPU:19 before, /device:TPU:8 now
where the time goes in v3:
time: 55 us; the launch traced here: 54.2 us
  Pallas kernels  33 us (60%)
  starting transfers between devices  16.9 us (31%)
  local copies, waits for them, and re-layouts  2.21 us (4%)
  other arithmetic  1.87 us (3%)
    pallas_call x4, Pallas kernels, call(): pl.pallas_call(kernel, out_shape=outs, in_specs=[smem if i < len(scalars)...  33 us
    ppermute x6, starting transfers between devices, shifted(): lax.ppermute(value, axis, [(i, i + by) for i in range(length) if 0 <= i +...  16.9 us
    unnamed x14, local copies, waits for them, and re-layouts  2.18 us
    convert_element_type x1, other arithmetic, shards(): fine_q = charges.astype(BF)  1.19 us
  transfers between devices with their start and end apart: 6, of which 1 were waited for; matrix products, arithmetic and copies ran while one was open for 1% of the time, Pallas kernels for 19%

profile of v3, /device:TPU:8, one launch (start us, length us, event | category | flops | bytes accessed | tf_op | source)
XLA Modules:
  0.0 54.2 jit_solution(13673845142987647177)
XLA Ops:
  0.0 1.2 %convert_element_type.2.own = bf16[24,64,128]{2,1,0:T(8,128)(2,1)S(1)} convert(f32[24,64,128]{2,1,0:T(8,128)} %param.27) | non-fusion elementwise | flops 196608 | bytes 1179648 | tf_op jit(solution)/shard_map/convert_element_type | solution.py:615
  1.2 0.0 copy-start
  1.2 0.7 %copy-done = bf16[24,64,128]{2,1,0:T(8,128)(2,1)} copy-done((bf16[24,64,128]{2,1,0:T(8,128)(2,1)}, bf16[24,64,128]{2,1,0:T(8,128)(2,1)S(1)}, u32[]{:S(2)}) %copy-start) | copy-done | bytes 393240
  2.0 1.3 %collective-permute-start.1 = (bf16[24,32,128]{2,1,0:T(8,128)(2,1)S(1)}, bf16[24,32,128]{2,1,0:T(8,128)(2,1)S(1)}, u32[]{:S(2)}, u32[]{:S(2)}) collective-permute-start(bf16[24,32,128]{2,1,0:T(8,128)(2,1)S(1)} %get-tuple-element.39), channel_id=1, source_target_pairs={{1,0},{2,1},{3,2},{5,4},{6,5},{7,6},{9,8},{10,9},{11,10},{13,12},{... | collective-permute-start | bytes 589832 | tf_op jit(solution)/shard_map/ppermute | solution.py:563
  3.3 3.0 %collective-permute-start = (bf16[24,32,128]{2,1,0:T(8,128)(2,1)S(1)}, bf16[24,32,128]{2,1,0:T(8,128)(2,1)S(1)}, u32[]{:S(2)}, u32[]{:S(2)}) collective-permute-start(bf16[24,32,128]{2,1,0:T(8,128)(2,1)S(1)} %get-tuple-element.40), channel_id=1, source_target_pairs={{0,1},{1,2},{2,3},{4,5},{5,6},{6,7},{8,9},{9,10},{10,11},{12,13},{... | collective-permute-start | bytes 589832 | tf_op jit(solution)/shard_map/ppermute | solution.py:563
  6.3 5.3 %shard_map.253 = (f32[15,80,128]{2,1,0:T(8,128)}, f32[15,80,128]{2,1,0:T(8,128)}, f32[15,80,128]{2,1,0:T(8,128)}, f32[15,48,128]{2,1,0:T(8,128)}, f32[15,48,128]...) custom-call(bf16[15,15,15]{2,1,0:T(8,128)(2,1)} %refs_0_.1, ...), custom_call_target="tpu_custom_call" | custom-call | tf_op jit(solution)/shard_map/pallas_call | solution.py:536
  11.6 0.0 collective-permute-done.1.right
  11.6 0.0 copy-start.3
  11.6 0.0 collective-permute-done.left
  11.6 0.0 copy-start.4
  11.7 0.7 %copy-done.3 = bf16[24,32,128]{2,1,0:T(8,128)(2,1)} copy-done((bf16[24,32,128]{2,1,0:T(8,128)(2,1)}, bf16[24,32,128]{2,1,0:T(8,128)(2,1)S(1)}, u32[]{:S(2)}) %copy-start.3) | copy-done | bytes 196632
  12.3 0.1 copy-done.4
  12.4 3.7 %shard_map.254 = (bf16[24,80,128]{2,1,0:T(8,128)(2,1)}, bf16[17,32,128]{2,1,0:T(8,128)(2,1)}, bf16[1104,128]{1,0:T(8,128)(2,1)}, bf16[1104,128]{1,0:T(8,128)(2,1...) custom-call(s32[1]{0:T(128)} %bitcast.3.ended, bf16[24,64,128]{2,1,0:T(8,128)(2,1)} %copy-done, ...), custom_call_target="tpu_custom_call" | custom-call | tf_op jit(solution)/shard_map/pallas_call | solution.py:536
  16.1 3.4 %collective-permute-start.2 = (bf16[1104,128]{1,0:T(8,128)(2,1)}, bf16[1104,128]{1,0:T(8,128)(2,1)S(1)}, u32[]{:S(2)}, u32[]{:S(2)}) collective-permute-start(bf16[1104,128]{1,0:T(8,128)(2,1)} %get-tuple-element.26), channel_id=1, source_target_pairs={{0,4},{4,8},{8,12},{12,16},{16,20},{20,24},{24,28},{1,5},{5,9},{9,... | collective-permute-start | bytes 847880 | tf_op jit(solution)/shard_map/ppermute | solution.py:563
  19.5 3.3 %collective-permute-start.3 = (bf16[1104,128]{1,0:T(8,128)(2,1)}, bf16[1104,128]{1,0:T(8,128)(2,1)S(1)}, u32[]{:S(2)}, u32[]{:S(2)}) collective-permute-start(bf16[1104,128]{1,0:T(8,128)(2,1)} %get-tuple-element.27), channel_id=1, source_target_pairs={{4,0},{8,4},{12,8},{16,12},{20,16},{24,20},{28,24},{5,1},{9,5},{13... | collective-permute-start | bytes 847880 | tf_op jit(solution)/shard_map/ppermute | solution.py:563
  22.8 3.5 %collective-permute-start.4 = (bf16[6,32,128]{2,1,0:T(8,128)(2,1)}, bf16[6,32,128]{2,1,0:T(8,128)(2,1)S(1)}, u32[]{:S(2)}, u32[]{:S(2)}) collective-permute-start(bf16[6,32,128]{2,1,0:T(8,128)(2,1)} %get-tuple-element.28), channel_id=1, source_target_pairs={{0,8},{4,12},{8,16},{12,20},{16,24},{20,28},{1,9},{5,13},{9,17},{1... | collective-permute-start | bytes 147464 | tf_op jit(solution)/shard_map/ppermute | solution.py:563
  26.3 2.4 %collective-permute-start.5 = (bf16[6,32,128]{2,1,0:T(8,128)(2,1)}, bf16[6,32,128]{2,1,0:T(8,128)(2,1)S(1)}, u32[]{:S(2)}, u32[]{:S(2)}) collective-permute-start(bf16[6,32,128]{2,1,0:T(8,128)(2,1)} %get-tuple-element.29), channel_id=1, source_target_pairs={{8,0},{12,4},{16,8},{20,12},{24,16},{28,20},{9,1},{13,5},{17,9},{2... | collective-permute-start | bytes 147464 | tf_op jit(solution)/shard_map/ppermute | solution.py:563
  28.7 0.7 %pad_add_fusion.limits = s32[4]{0:T(128)} fusion(s32[1]{0:T(128)} %bitcast.3.ended, s32[1]{0:T(128)} %bitcast.2, s32[1]{0:T(128)} %bitcast.1, s32[1]{0:T(128)} %bitcast), kind=kLoop, calls=%fused_computation | loop fusion | flops 12 | bytes 32 | tf_op jit(solution)/shard_map/stack | solution.py:673
  29.3 5.2 %shard_map.255 = (f32[24,80,128]{2,1,0:T(8,128)}, f32[24,80,128]{2,1,0:T(8,128)}) custom-call(bf16[24,80,128]{2,1,0:T(8,128)(2,1)} %get-tuple-element.23.near, bf16[256,256]{1,0:T(8,128)(2,1)} %constant.77.clone.to_z, bf16[160,240]{1,0:T(8,128)(2,1)} %constant.78.clone.to_y), custom_call_target="tpu_custom_call" | custom-call | tf_op jit(solution)/shard_map/pallas_call | solution.py:536
  34.5 0.0 collective-permute-done.4.far_left
  34.5 0.0 copy-start.5
  34.5 0.0 collective-permute-done.5.far_right
  34.5 0.0 copy-start.6
  34.6 0.0 collective-permute-done.2.from_left
  34.6 0.0 copy-start.1
  34.6 0.2 collective-permute-done.3.from_right
  34.7 0.0 copy-start.2
  34.7 0.4 copy-done.5
  35.2 0.0 copy-done.6
  35.2 0.2 copy-done.1
  35.3 0.1 copy-done.2
  35.5 18.8 %shard_map.256 = f32[24,64,128]{2,1,0:T(8,128)} custom-call(s32[4]{0:T(128)} %pad_add_fusion.limits, f32[24,80,128]{2,1,0:T(8,128)} %get-tuple-element.24.own_real, f32[24,80,128]{2,1,0:T(8,128)} %get-tuple-element.25.own_imag, bf16[1104,128]{1,0:T(8,128)(2,1)} %copy-done.1, bf16[1104,128]{1,0:T(8,128)(2,1)} %copy-done.2, bf16[6,32,128]{2,1,0:T(8,128)(2,1)} %copy-done.5, ...), custom_call_target="tpu_custom_call" | custom-call | tf_op jit(solution)/shard_map/pallas_call | solution.py:536
  (1 shorter events, 0.0 us)
Async XLA Ops:
  1.2 0.8 %copy-start = (bf16[24,64,128]{2,1,0:T(8,128)(2,1)}, bf16[24,64,128]{2,1,0:T(8,128)(2,1)S(1)}, u32[]{:S(2)}) copy-start(bf16[24,64,128]{2,1,0:T(8,128)(2,1)S(1)} %convert_element_type.2.own) | copy-start | bytes 1179652
  2.0 9.7 %collective-permute-start.1 = (bf16[24,32,128]{2,1,0:T(8,128)(2,1)S(1)}, bf16[24,32,128]{2,1,0:T(8,128)(2,1)S(1)}, u32[]{:S(2)}, u32[]{:S(2)}) collective-permute-start(bf16[24,32,128]{2,1,0:T(8,128)(2,1)S(1)} %get-tuple-element.39), channel_id=1, source_target_pairs={{1,0},{2,1},{3,2},{5,4},{6,5},{7,6},{9,8},{10,9},{11,10},{13,12},{... | collective-permute-start | bytes 589832 | tf_op jit(solution)/shard_map/ppermute | solution.py:563
  3.3 8.4 %collective-permute-start = (bf16[24,32,128]{2,1,0:T(8,128)(2,1)S(1)}, bf16[24,32,128]{2,1,0:T(8,128)(2,1)S(1)}, u32[]{:S(2)}, u32[]{:S(2)}) collective-permute-start(bf16[24,32,128]{2,1,0:T(8,128)(2,1)S(1)} %get-tuple-element.40), channel_id=1, source_target_pairs={{0,1},{1,2},{2,3},{4,5},{5,6},{6,7},{8,9},{9,10},{10,11},{12,13},{... | collective-permute-start | bytes 589832 | tf_op jit(solution)/shard_map/ppermute | solution.py:563
  11.6 0.7 %copy-start.3 = (bf16[24,32,128]{2,1,0:T(8,128)(2,1)}, bf16[24,32,128]{2,1,0:T(8,128)(2,1)S(1)}, u32[]{:S(2)}) copy-start(bf16[24,32,128]{2,1,0:T(8,128)(2,1)S(1)} %collective-permute-done.1.right) | copy-start | bytes 589828
  11.6 0.7 %copy-start.4 = (bf16[24,32,128]{2,1,0:T(8,128)(2,1)}, bf16[24,32,128]{2,1,0:T(8,128)(2,1)S(1)}, u32[]{:S(2)}) copy-start(bf16[24,32,128]{2,1,0:T(8,128)(2,1)S(1)} %collective-permute-done.left) | copy-start | bytes 589828
  16.1 18.5 %collective-permute-start.2 = (bf16[1104,128]{1,0:T(8,128)(2,1)}, bf16[1104,128]{1,0:T(8,128)(2,1)S(1)}, u32[]{:S(2)}, u32[]{:S(2)}) collective-permute-start(bf16[1104,128]{1,0:T(8,128)(2,1)} %get-tuple-element.26), channel_id=1, source_target_pairs={{0,4},{4,8},{8,12},{12,16},{16,20},{20,24},{24,28},{1,5},{5,9},{9,... | collective-permute-start | bytes 847880 | tf_op jit(solution)/shard_map/ppermute | solution.py:563
  19.5 15.3 %collective-permute-start.3 = (bf16[1104,128]{1,0:T(8,128)(2,1)}, bf16[1104,128]{1,0:T(8,128)(2,1)S(1)}, u32[]{:S(2)}, u32[]{:S(2)}) collective-permute-start(bf16[1104,128]{1,0:T(8,128)(2,1)} %get-tuple-element.27), channel_id=1, source_target_pairs={{4,0},{8,4},{12,8},{16,12},{20,16},{24,20},{28,24},{5,1},{9,5},{13... | collective-permute-start | bytes 847880 | tf_op jit(solution)/shard_map/ppermute | solution.py:563
  22.8 11.7 %collective-permute-start.4 = (bf16[6,32,128]{2,1,0:T(8,128)(2,1)}, bf16[6,32,128]{2,1,0:T(8,128)(2,1)S(1)}, u32[]{:S(2)}, u32[]{:S(2)}) collective-permute-start(bf16[6,32,128]{2,1,0:T(8,128)(2,1)} %get-tuple-element.28), channel_id=1, source_target_pairs={{0,8},{4,12},{8,16},{12,20},{16,24},{20,28},{1,9},{5,13},{9,17},{1... | collective-permute-start | bytes 147464 | tf_op jit(solution)/shard_map/ppermute | solution.py:563
  26.3 8.2 %collective-permute-start.5 = (bf16[6,32,128]{2,1,0:T(8,128)(2,1)}, bf16[6,32,128]{2,1,0:T(8,128)(2,1)S(1)}, u32[]{:S(2)}, u32[]{:S(2)}) collective-permute-start(bf16[6,32,128]{2,1,0:T(8,128)(2,1)} %get-tuple-element.29), channel_id=1, source_target_pairs={{8,0},{12,4},{16,8},{20,12},{24,16},{28,20},{9,1},{13,5},{17,9},{2... | collective-permute-start | bytes 147464 | tf_op jit(solution)/shard_map/ppermute | solution.py:563
  34.5 0.6 %copy-start.5 = (bf16[6,32,128]{2,1,0:T(8,128)(2,1)}, bf16[6,32,128]{2,1,0:T(8,128)(2,1)S(1)}, u32[]{:S(2)}) copy-start(bf16[6,32,128]{2,1,0:T(8,128)(2,1)S(1)} %collective-permute-done.4.far_left) | copy-start | bytes 147460
  34.5 0.6 %copy-start.6 = (bf16[6,32,128]{2,1,0:T(8,128)(2,1)}, bf16[6,32,128]{2,1,0:T(8,128)(2,1)S(1)}, u32[]{:S(2)}) copy-start(bf16[6,32,128]{2,1,0:T(8,128)(2,1)S(1)} %collective-permute-done.5.far_right) | copy-start | bytes 147460
  34.6 0.8 %copy-start.1 = (bf16[1104,128]{1,0:T(8,128)(2,1)}, bf16[1104,128]{1,0:T(8,128)(2,1)S(1)}, u32[]{:S(2)}) copy-start(bf16[1104,128]{1,0:T(8,128)(2,1)S(1)} %collective-permute-done.2.from_left) | copy-start | bytes 847876
  34.7 0.7 %copy-start.2 = (bf16[1104,128]{1,0:T(8,128)(2,1)}, bf16[1104,128]{1,0:T(8,128)(2,1)S(1)}, u32[]{:S(2)}) copy-start(bf16[1104,128]{1,0:T(8,128)(2,1)S(1)} %collective-permute-done.3.from_right) | copy-start | bytes 847876

commit v4 on v3

--- a/solution.py
+++ b/solution.py
@@ -266,11 +266,17 @@
         batches(taps, 5, body)
 
 
+def chosen(flag, first, second):
+    return jnp.where(flag, first, second)
+
+
 def pack_kernel(
-    ended, own, left, right, down_z, down_y, ordered, near, coarse, to_right, to_left, far_right, far_left, part
+    own, got_a, got_b, down_z, down_y, ordered, near, coarse, next_a, next_b, far_a, far_b, part
 ):
     count, size = own.shape[:2]
-    side = left.shape[1]
+    side = got_a.shape[1]
+    up_y, up_x, up_far = leads("gy", 1), leads("gx", 1), leads("gx", 2)
+    ended = lax.axis_index("gy") == lax.axis_size("gy") - 1
     width = near.shape[1]
     start = side - (width - size) // 2
     window = part.shape[1]
@@ -278,7 +284,8 @@
     def body(xs, first):
         rows = []
         for x in xs:
-            l, o, r = left[x], own[x], right[x]
+            a, b, o = got_a[x], got_b[x], own[x].astype(BF)
+            l, r = chosen(up_y, b, a), chosen(up_y, a, b)
             near[x] = jnp.concatenate([l[start:], o, r[: side - start]], 0)
             low = jnp.concatenate([l, o[: window - side]], 0)
             high = jnp.concatenate([o[size + side - window :], r], 0)
@@ -292,7 +299,7 @@
     shape = (half, LANES)
     high_lanes = lax.broadcasted_iota(jnp.int32, shape, 1) >= LANES // 2
     outside = high_lanes & (lax.broadcasted_iota(jnp.int32, shape, 0) >= half // 2)
-    outside = outside & (ended[0] == 1)
+    outside = outside & ended
     last = count // 2
     totals = []
     for i in range(last + 1):
@@ -314,17 +321,19 @@
                 coarse[last + 2 + k] = term
         else:
             coarse[i + 2] = row.astype(BF)
-    for out, rows in ((to_right, to_right.shape[0]), (to_left, to_left.shape[0])):
-        lines = rows - coarse.shape[0] * half
-        first = count - lines // width if out is to_right else 0
+    lines = next_a.shape[0] - coarse.shape[0] * half
+    tail = count - lines // width
+    far_tail = coarse.shape[0] - far_a.shape[0]
+    for out, upward in ((next_a, up_x), (next_b, jnp.logical_not(up_x))):
+        first = jnp.where(upward, tail, 0)
         for x in range(lines // width):
             out[x * width : (x + 1) * width, :] = near[first + x]
         for k in range(coarse.shape[0]):
             out[lines + k * half : lines + (k + 1) * half, :] = coarse[k]
-    shift = coarse.shape[0] - far_right.shape[0]
-    for k in range(far_right.shape[0]):
-        far_right[k] = coarse[shift + k]
-        far_left[k] = coarse[k]
+    for out, upward in ((far_a, up_far), (far_b, jnp.logical_not(up_far))):
+        first = jnp.where(upward, far_tail, 0)
+        for k in range(far_a.shape[0]):
+            out[k] = coarse[first + k]
 
 
 def own_kernel(near, to_z, to_y, real, imag, ahead):
@@ -333,13 +342,12 @@
 
 
 def final_kernel(
-    limits,
     own_real,
     own_imag,
-    from_left,
-    from_right,
-    far_left,
-    far_right,
+    next_a,
+    next_b,
+    far_a,
+    far_b,
     coarse,
     kr,
     kd,
@@ -389,13 +397,29 @@
     t_back,
     t_out,
 ):
-    top_rows, ended_x, close_x, ended_y = limits[0], limits[1], limits[2], limits[3]
+    left_x = lax.axis_size("gx") - lax.axis_index("gx")
+    ended_x, close_x = left_x == 1, left_x <= 2
+    ended_y = (lax.axis_index("gy") == lax.axis_size("gy") - 1).astype(jnp.int32)
+    up_x, up_far = leads("gx", 1), leads("gx", 2)
     count, width = own_real.shape[:2]
     reach = side_real.shape[0] // 2
+    top_rows = left_x * (count // 4) + reach
+
+    def from_left(at):
+        return chosen(up_x, next_b[at, :], next_a[at, :])
+
+    def from_right(at):
+        return chosen(up_x, next_a[at, :], next_b[at, :])
+
+    def far_left(k):
+        return chosen(up_far, far_b[k], far_a[k])
+
+    def far_right(k):
+        return chosen(up_far, far_a[k], far_b[k])
 
     def side_cells(x):
-        ref, first = (from_left, x) if x < reach else (from_right, x - reach)
-        return ref[first * width : (first + 1) * width, :]
+        read, first = (from_left, x) if x < reach else (from_right, x - reach)
+        return read(slice(first * width, (first + 1) * width))
 
     period = width
     for first in range(0, 2 * reach, 4):
@@ -427,33 +451,32 @@
 
     half = mid.shape[1]
     last = count // 2
-    skip_left = from_left.shape[0] - coarse.shape[0] * half
-    skip_right = from_right.shape[0] - coarse.shape[0] * half
+    lines = next_a.shape[0] - coarse.shape[0] * half
 
     def left_row(k):
-        return from_left[skip_left + k * half : skip_left + (k + 1) * half, :]
+        return from_left(slice(lines + k * half, lines + (k + 1) * half))
 
     def right_row(k):
-        return from_right[skip_right + k * half : skip_right + (k + 1) * half, :]
+        return from_right(slice(lines + k * half, lines + (k + 1) * half))
 
     def added(first, second, dropped=None):
         value = sum(first(2 - k).astype(F32) for k in range(3))
         value = value + sum(second(last + 4 - k).astype(F32) for k in range(3))
         if dropped is not None:
-            value = jnp.where(dropped == 1, 0.0, value)
+            value = jnp.where(dropped, 0.0, value)
         return value.astype(BF)
 
-    spare = far_left.shape[0] - 3
-    far_first = coarse.shape[0] - far_left.shape[0]
-    rows = [far_left[k] for k in range(spare)]
-    rows += [added(left_row, lambda k: far_left[k - far_first])]
+    spare = far_a.shape[0] - 3
+    far_first = coarse.shape[0] - far_a.shape[0]
+    rows = [far_left(k) for k in range(spare)]
+    rows += [added(left_row, lambda k: far_left(k - far_first))]
     rows += [left_row(k) for k in range(3, last + 2)]
     rows += [added(lambda k: coarse[k], left_row)]
     rows += [coarse[k] for k in range(3, last + 2)]
     rows += [added(right_row, lambda k: coarse[k], ended_x)]
     rows += [right_row(k) for k in range(3, last + 2)]
-    rows += [added(lambda k: far_right[k], right_row, close_x)]
-    rows += [far_right[k] for k in range(3, 3 + spare)]
+    rows += [added(far_right, right_row, close_x)]
+    rows += [far_right(k) for k in range(3, 3 + spare)]
     for k, row in enumerate(rows):
         mid[k] = row
 
@@ -511,7 +534,7 @@
     from_frequencies_y(m_er, m_ei, 7, m_from_y.at[ended_y], m_back)
     from_frequencies_z(t_back, t_out.shape[0], 7, t_from_z, top_write)
     from_frequencies_z(m_back, m_out.shape[0], 7, m_from_z, mid_write)
-    keep = jnp.where(ended_x == 1, 0.0, 1.0)
+    keep = jnp.where(ended_x, 0.0, 1.0)
     top = t_out.shape[0] - 1
     t_out[top] = t_out[top] * keep
     for i in range(top):
@@ -530,20 +553,18 @@
     return m_width - t_width
 
 
-def call(kernel, outs, scratch, scalars, args, loose=()):
+def call(kernel, outs, scratch, args, mib, loose=()):
     vmem = pl.BlockSpec(memory_space=pltpu.VMEM)
-    smem = pl.BlockSpec(memory_space=pltpu.SMEM)
     return pl.pallas_call(
         kernel,
         out_shape=outs,
         in_specs=[
-            smem if i < len(scalars) else pl.BlockSpec(memory_space=pl.ANY) if i in loose else vmem
-            for i in range(len(scalars) + len(args))
+            pl.BlockSpec(memory_space=pl.ANY) if i in loose else vmem for i in range(len(args))
         ],
         out_specs=jax.tree.map(lambda _: vmem, outs),
         scratch_shapes=[pltpu.VMEM(shape, dtype) for dtype, shape in scratch],
-        compiler_params=pltpu.CompilerParams(vmem_limit_bytes=60 << 20),
-    )(*scalars, *args)
+        compiler_params=pltpu.CompilerParams(vmem_limit_bytes=mib << 20),
+    )(*args)
 
 
 def level_scratch(level, ny, nz, extra=()):
@@ -558,20 +579,24 @@
     return [*rows, *extra, *terms, (F32, (level.out_x, ny, nz))]
 
 
-def shifted(value, axis, by):
+def leads(axis, by):
+    return lax.rem(lax.div(lax.axis_index(axis), by), 2) == 0
+
+
+def swapped(first, second, axis, by):
     length = lax.axis_size(axis)
-    return lax.ppermute(
-        value, axis, [(i, i + by) for i in range(length) if 0 <= i + by < length]
-    )
+    outs = []
+    for value, turn in ((first, 0), (second, 1)):
+        up = [i for i in range(length - by) if i // by % 2 == turn]
+        pairs = [(i, i + by) for i in up] + [(i + by, i) for i in up]
+        outs.append(lax.ppermute(value, axis, pairs))
+    return outs
 
 
 def shards(charges, kernel_fine, kernel_mid, kernel_top):
     nx, ny, nz = charges.shape
     taps = kernel_fine.shape[0]
     half = taps // 2
-    gx, gy = lax.axis_index("gx"), lax.axis_index("gy")
-    left_x = lax.axis_size("gx") - gx
-    end_y = gy == lax.axis_size("gy") - 1
     wide = half + 1
 
     ident = np.eye(ny)
@@ -608,14 +633,20 @@
         functools.partial(spectra_kernel, 3),
         outs,
         [(F32, (taps, 16, LANES)), (F32, (taps * 16, 2 * LANES))],
-        [],
         [kernel_fine, kernel_mid, kernel_top, *tables],
-    )
-
-    fine_q = charges.astype(BF)
+        8,
+    )
+
     side = ny // 2
-    from_below = shifted(fine_q[:, ny - side :], "gy", 1)
-    from_above = shifted(fine_q[:, :side], "gy", -1)
+    up_y = leads("gy", 1)
+    got_a, got_b = swapped(
+        *(
+            lax.dynamic_slice_in_dim(charges, jnp.where(flag, side, 0), side, 1).astype(BF)
+            for flag in (up_y, jnp.logical_not(up_y))
+        ),
+        "gy",
+        1,
+    )
 
     window = side + ny // 2 + 16
     packed = ny // 2
@@ -626,7 +657,6 @@
     lines = mx - 1 + 6
     reach = 2 * half + 1 - mx
     assert 0 < reach <= mx - 1 and 2 * mz == LANES == nz
-    ended = end_y.astype(jnp.int32)
     shapes = [
         (nx, fine.period_y, LANES),
         (lines, packed, LANES),
@@ -635,49 +665,38 @@
         (reach + 3, packed, LANES),
         (reach + 3, packed, LANES),
     ]
-    near, coarse, to_right, to_left, far_right, far_left = call(
+    near, coarse, next_a, next_b, far_a, far_b = call(
         pack_kernel,
         [jax.ShapeDtypeStruct(shape, BF) for shape in shapes],
         [(F32, (nx, window, LANES))],
-        [ended[None]],
         [
-            fine_q,
-            from_below,
-            from_above,
+            charges,
+            got_a,
+            got_b,
             down_z.astype(BF),
             np.tile(down_y, (1, 3)).astype(BF),
             spectra[0],
         ],
-        loose=(6,),
-    )
-    from_left = shifted(to_right, "gx", 1)
-    from_right = shifted(to_left, "gx", -1)
-    from_far_left = shifted(far_right, "gx", 2)
-    from_far_right = shifted(far_left, "gx", -2)
+        8,
+        loose=(5,),
+    )
+    next_a, next_b = swapped(next_a, next_b, "gx", 1)
+    far_a, far_b = swapped(far_a, far_b, "gx", 2)
 
     own = call(
         own_kernel,
         [jax.ShapeDtypeStruct((nx, fine.period_y, LANES), F32)] * 2,
         [(BF, (2, nx * fine.period_y, 2 * LANES))],
-        [],
         [near, fine.to_z, fine.to_y],
-    )
-
-    tx = nx // 4
+        8,
+    )
+
     wide_top = ty + 2 * wide
     t_down_y = down(wide_top, 0, 2 * packed)
     t_down_y = np.concatenate([t_down_y[:, :packed], t_down_y[:, packed:]], 0)
     t_down_z = np.concatenate(
         [np.tile(table, (3, 1)) for table in both_sides(down(tz, 0, mz).T)], 0
     )
-    limits = jnp.stack(
-        [
-            jnp.minimum(left_x * tx + half, top.in_x),
-            (left_x == 1).astype(jnp.int32),
-            (left_x <= 2).astype(jnp.int32),
-            ended,
-        ]
-    ).astype(jnp.int32)
     return call(
         final_kernel,
         jax.ShapeDtypeStruct((nx, ny, nz), F32),
@@ -692,13 +711,12 @@
             *level_scratch(mid, ny, nz),
             *level_scratch(top, ny, nz, [(BF, (top.in_x, top.period_y, tz))]),
         ],
-        [limits],
         [
             *own,
-            from_left,
-            from_right,
-            from_far_left,
-            from_far_right,
+            next_a,
+            next_b,
+            far_a,
+            far_b,
             coarse,
             *spectra[:3],
             fine.to_z,
@@ -718,6 +736,7 @@
             np.stack(top.from_y),
             top.from_z,
         ],
+        26,
     )
 
 

time: 55 us -> 44.9 us (0.82)
  Pallas kernels: 33 us -> 22.7 us
  starting transfers between devices: 16.9 us -> 12.6 us
  local copies, waits for them, and re-layouts: 2.21 us -> 5.39 us
  waiting for transfers between devices: 0.16 us -> 2.93 us
  other arithmetic: 1.87 us -> 0 us
    pallas_call x4, Pallas kernels: 33 us -> 22.7 us  [call(): pl.pallas_call(kernel, out_shape=outs, in_specs=[pl.BlockSpec(memory_spac...]
    ppermute x6, starting transfers between devices: 16.9 us -> 12.6 us  [swapped(): outs.append(lax.ppermute(value, axis, pairs))]
    ppermute x6, waiting for transfers between devices: 0.16 us -> 2.93 us  [swapped(): outs.append(lax.ppermute(value, axis, pairs))]
    unnamed x14 -> x54, local copies, waits for them, and re-layouts: 2.18 us -> 4.11 us
    convert_element_type x0 -> x1, local copies, waits for them, and re-layouts: none -> 1.28 us  [shards(): lax.dynamic_slice_in_dim(charges, jnp.where(flag, side, 0), side, 1)]
    convert_element_type x1 -> x0, other arithmetic: 1.19 us -> none  [shards(): fine_q = charges.astype(BF)]
    another operation x1 -> x0, other arithmetic: 0.67 us -> none  [shards(): jnp.stack([jnp.minimum(left_x * tx + half, top.in_x), (left_x == 1).astyp...]
  transfers between devices with their start and end apart: 6 -> 6, of which waited for: 1 -> 2; matrix products, arithmetic and copies ran while one was open for 1% -> 0% of each run, Pallas kernels for 19% -> 12%
where the time goes in v4:
time: 44.9 us; the launch traced here: 44 us
  Pallas kernels  22.7 us (51%)
  starting transfers between devices  12.6 us (28%)
  local copies, waits for them, and re-layouts  5.39 us (12%)
  waiting for transfers between devices  2.93 us (7%)
    pallas_call x4, Pallas kernels, call(): pl.pallas_call(kernel, out_shape=outs, in_specs=[pl.BlockSpec(memory_spac...  22.7 us
    ppermute x6, starting transfers between devices, swapped(): outs.append(lax.ppermute(value, axis, pairs))  12.6 us
    unnamed x54, local copies, waits for them, and re-layouts  4.11 us
    ppermute x6, waiting for transfers between devices, swapped(): outs.append(lax.ppermute(value, axis, pairs))  2.93 us
    convert_element_type x1, local copies, waits for them, and re-layouts, shards(): lax.dynamic_slice_in_dim(charges, jnp.where(flag, side, 0), side, 1)  1.28 us
  transfers between devices with their start and end apart: 6, of which 2 were waited for; matrix products, arithmetic and copies ran while one was open for 0% of the time, Pallas kernels for 12%

profile of v4, /device:TPU:8, one launch (start us, length us, event | category | flops | bytes accessed | tf_op | source)
XLA Modules:
  0.0 44.0 jit_solution(6465704073642096119)
XLA Ops:
  0.0 0.0 copy-start.12
  0.0 1.3 %dynamic-slice_convert_fusion = (bf16[24,32,128]{2,1,0:T(8,128)(2,1)S(1)}, bf16[24,32,128]{2,1,0:T(8,128)(2,1)S(1)}) fusion(f32[24,64,128]{2,1,0:T(8,128)} %own.1, s32[]{:T(128)S(6)} %select_n.10, s32[]{:T(128)S(6)} %select_n.9), kind=kLoop, calls=%fused_computation | loop fusion | bytes 786440 | tf_op jit(solution)/shard_map/convert_element_type | solution.py:644
  1.3 0.7 %collective-permute-start.1 = (bf16[24,32,128]{2,1,0:T(8,128)(2,1)S(1)}, bf16[24,32,128]{2,1,0:T(8,128)(2,1)S(1)}, u32[]{:S(2)}, u32[]{:S(2)}) collective-permute-start(bf16[24,32,128]{2,1,0:T(8,128)(2,1)S(1)} %get-tuple-element.39), channel_id=1, source_target_pairs={{1,2},{2,1},{5,6},{6,5},{9,10},{10,9},{13,14},{14,13},{17,18},{18,... | collective-permute-start | bytes 589832 | tf_op jit(solution)/shard_map/ppermute | solution.py:592
  2.0 0.0 copy-start.15
  2.0 2.9 %collective-permute-start = (bf16[24,32,128]{2,1,0:T(8,128)(2,1)S(1)}, bf16[24,32,128]{2,1,0:T(8,128)(2,1)S(1)}, u32[]{:S(2)}, u32[]{:S(2)}) collective-permute-start(bf16[24,32,128]{2,1,0:T(8,128)(2,1)S(1)} %get-tuple-element.40), channel_id=1, source_target_pairs={{0,1},{2,3},{1,0},{3,2},{4,5},{6,7},{5,4},{7,6},{8,9},{10,11},{9,8... | collective-permute-start | bytes 589832 | tf_op jit(solution)/shard_map/ppermute | solution.py:592
  5.0 0.8 %copy-done.16 = bf16[15,15,15]{2,1,0:T(8,128)(2,1)S(1)} copy-done((bf16[15,15,15]{2,1,0:T(8,128)(2,1)S(1)}, bf16[15,15,15]{2,1,0:T(8,128)(2,1)}, u32[]{:S(2)}) %copy-start.16) | copy-done | bytes 6774
  5.8 0.8 %copy-done.17 = bf16[15,15,15]{2,1,0:T(8,128)(2,1)S(1)} copy-done((bf16[15,15,15]{2,1,0:T(8,128)(2,1)S(1)}, bf16[15,15,15]{2,1,0:T(8,128)(2,1)}, u32[]{:S(2)}) %copy-start.17) | copy-done | bytes 6774
  6.6 0.8 %copy-done.18 = bf16[15,15,15]{2,1,0:T(8,128)(2,1)S(1)} copy-done((bf16[15,15,15]{2,1,0:T(8,128)(2,1)S(1)}, bf16[15,15,15]{2,1,0:T(8,128)(2,1)}, u32[]{:S(2)}) %copy-start.18) | copy-done | bytes 6774
  7.5 0.8 %copy-done.20 = bf16[160,48]{1,0:T(8,128)(2,1)S(1)} copy-done((bf16[160,48]{1,0:T(8,128)(2,1)S(1)}, bf16[160,48]{1,0:T(8,128)(2,1)}, u32[]{:S(2)}) %copy-start.20) | copy-done | bytes 15384
  8.2 0.7 %copy-done.26 = bf16[64,48]{1,0:T(8,128)(2,1)S(1)} copy-done((bf16[64,48]{1,0:T(8,128)(2,1)S(1)}, bf16[64,48]{1,0:T(8,128)(2,1)}, u32[]{:S(2)}) %copy-start.26) | copy-done | bytes 6168
  9.0 2.5 %shard_map.253 = (f32[15,80,128]{2,1,0:T(8,128)S(1)}, f32[15,80,128]{2,1,0:T(8,128)S(1)}, f32[15,80,128]{2,1,0:T(8,128)S(1)}, f32[15,48,128]{2,1,0:T(8,128)S(1)}...) custom-call(bf16[15,15,15]{2,1,0:T(8,128)(2,1)S(1)} %copy-done.16, ...), custom_call_target="tpu_custom_call" | custom-call | tf_op jit(solution)/shard_map/pallas_call | solution.py:558
  11.5 0.0 copy-start.1
  11.5 0.0 copy-start.2
  11.5 0.0 copy-start.6
  11.5 0.0 copy-start.8
  11.5 0.0 copy-start.13
  11.6 0.0 copy-start.14
  11.6 0.0 copy-start.19
  11.6 0.0 copy-start.21
  11.6 0.0 copy-start.24
  11.6 0.0 copy-start.25
  11.6 1.7 %shard_map.254 = (bf16[24,80,128]{2,1,0:T(8,128)(2,1)S(1)}, bf16[17,32,128]{2,1,0:T(8,128)(2,1)S(1)}, bf16[1104,128]{1,0:T(8,128)(2,1)S(1)}, bf16[1104,128]{1,0:...) custom-call(f32[24,64,128]{2,1,0:T(8,128)S(1)} %copy-done, ...), custom_call_target="tpu_custom_call" | custom-call | tf_op jit(solution)/shard_map/pallas_call | solution.py:558
  13.3 1.6 %collective-permute-start.2 = (bf16[1104,128]{1,0:T(8,128)(2,1)S(1)}, bf16[1104,128]{1,0:T(8,128)(2,1)S(1)}, u32[]{:S(2)}, u32[]{:S(2)}) collective-permute-start(bf16[1104,128]{1,0:T(8,128)(2,1)S(1)} %get-tuple-element.26), channel_id=1, source_target_pairs={{0,4},{8,12},{16,20},{24,28},{4,0},{12,8},{20,16},{28,24},{1,5},{9... | collective-permute-start | bytes 847880 | tf_op jit(solution)/shard_map/ppermute | solution.py:592
  14.9 2.3 %collective-permute-start.3 = (bf16[1104,128]{1,0:T(8,128)(2,1)S(1)}, bf16[1104,128]{1,0:T(8,128)(2,1)S(1)}, u32[]{:S(2)}, u32[]{:S(2)}) collective-permute-start(bf16[1104,128]{1,0:T(8,128)(2,1)S(1)} %get-tuple-element.27), channel_id=1, source_target_pairs={{4,8},{12,16},{20,24},{8,4},{16,12},{24,20},{5,9},{13,17},{21,25},... | collective-permute-start | bytes 847880 | tf_op jit(solution)/shard_map/ppermute | solution.py:592
  17.2 0.1 collective-permute-start.4
  17.3 5.0 %collective-permute-start.5 = (bf16[6,32,128]{2,1,0:T(8,128)(2,1)S(1)}, bf16[6,32,128]{2,1,0:T(8,128)(2,1)S(1)}, u32[]{:S(2)}, u32[]{:S(2)}) collective-permute-start(bf16[6,32,128]{2,1,0:T(8,128)(2,1)S(1)} %get-tuple-element.29), channel_id=1, source_target_pairs={{8,16},{12,20},{16,8},{20,12},{9,17},{13,21},{17,9},{21,13},{10,18... | collective-permute-start | bytes 147464 | tf_op jit(solution)/shard_map/ppermute | solution.py:592
  22.4 0.0 copy-start.3
  22.4 0.0 copy-start.5
  22.4 2.8 %shard_map.255 = (f32[24,80,128]{2,1,0:T(8,128)S(1)}, f32[24,80,128]{2,1,0:T(8,128)S(1)}) custom-call(bf16[24,80,128]{2,1,0:T(8,128)(2,1)S(1)} %get-tuple-element.23.near, bf16[256,256]{1,0:T(8,128)(2,1)S(1)} %copy-done.1, bf16[160,240]{1,0:T(8,128)(2,1)S(1)} %copy-done.2), custom_call_target="tpu_custom_call" | custom-call | tf_op jit(solution)/shard_map/pallas_call | solution.py:558
  25.2 1.0 %collective-permute-done.5.far_b = bf16[6,32,128]{2,1,0:T(8,128)(2,1)S(1)} collective-permute-done((bf16[6,32,128]{2,1,0:T(8,128)(2,1)S(1)}, bf16[6,32,128]{2,1,0:T(8,128)(2,1)S(1)}, u32[]{:S(2)}, u32[]{:S(2)}) %collective-permute-start.5) | collective-permute-done | bytes 49184 | tf_op jit(solution)/shard_map/ppermute | solution.py:592
  26.2 1.9 %collective-permute-done.2.next_a = bf16[1104,128]{1,0:T(8,128)(2,1)S(1)} collective-permute-done((bf16[1104,128]{1,0:T(8,128)(2,1)S(1)}, bf16[1104,128]{1,0:T(8,128)(2,1)S(1)}, u32[]{:S(2)}, u32[]{:S(2)}) %collective-permute-start.2) | collective-permute-done | bytes 282656 | tf_op jit(solution)/shard_map/ppermute | solution.py:592
  28.2 15.8 %shard_map.256 = f32[24,64,128]{2,1,0:T(8,128)} custom-call(f32[24,80,128]{2,1,0:T(8,128)S(1)} %get-tuple-element.24.own_real, f32[24,80,128]{2,1,0:T(8,128)S(1)} %get-tuple-element.25.own_imag, bf16[1104,128]{1,0:T(8,128)(2,1)S(1)} %collective-permute-done.2.next_a, bf16[1104,128]{1,0:T(8,128)(2,1)S(1)} %collective-permute-done.3.next_b, ...), custom_call_target="tpu_custom_call" | custom-call | tf_op jit(solution)/shard_map/pallas_call | solution.py:558
  (39 shorter events, 0.1 us)
Async XLA Ops:
  0.0 5.0 %copy-start.23 = (bf16[96,48]{1,0:T(8,128)(2,1)S(1)}, bf16[96,48]{1,0:T(8,128)(2,1)}, u32[]{:S(2)}) copy-start(bf16[96,48]{1,0:T(8,128)(2,1)} %constant.65.clone.refs_6_) | copy-start | bytes 27652
  0.0 5.0 %copy-start.10 = (bf16[256,256]{1,0:T(8,128)(2,1)S(1)}, bf16[256,256]{1,0:T(8,128)(2,1)}, u32[]{:S(2)}) copy-start(bf16[256,256]{1,0:T(8,128)(2,1)} %constant.66.clone.refs_7_) | copy-start | bytes 393220
  0.0 5.0 %copy-start.11 = (bf16[256,256]{1,0:T(8,128)(2,1)S(1)}, bf16[256,256]{1,0:T(8,128)(2,1)}, u32[]{:S(2)}) copy-start(bf16[256,256]{1,0:T(8,128)(2,1)} %constant.64.clone.refs_5_) | copy-start | bytes 393220
  0.0 5.0 %copy-start.12 = (bf16[256,256]{1,0:T(8,128)(2,1)S(1)}, bf16[256,256]{1,0:T(8,128)(2,1)}, u32[]{:S(2)}) copy-start(bf16[256,256]{1,0:T(8,128)(2,1)} %constant.62.clone.refs_3_) | copy-start | bytes 393220
  0.0 11.4 %copy-start = (f32[24,64,128]{2,1,0:T(8,128)S(1)}, f32[24,64,128]{2,1,0:T(8,128)}, u32[]{:S(2)}) copy-start(f32[24,64,128]{2,1,0:T(8,128)} %own.1) | copy-start | bytes 2359300
  1.3 10.1 %collective-permute-start.1 = (bf16[24,32,128]{2,1,0:T(8,128)(2,1)S(1)}, bf16[24,32,128]{2,1,0:T(8,128)(2,1)S(1)}, u32[]{:S(2)}, u32[]{:S(2)}) collective-permute-start(bf16[24,32,128]{2,1,0:T(8,128)(2,1)S(1)} %get-tuple-element.39), channel_id=1, source_target_pairs={{1,2},{2,1},{5,6},{6,5},{9,10},{10,9},{13,14},{14,13},{17,18},{18,... | collective-permute-start | bytes 589832 | tf_op jit(solution)/shard_map/ppermute | solution.py:592
  2.0 9.5 %copy-start.15 = (bf16[256,128]{1,0:T(8,128)(2,1)S(1)}, bf16[256,128]{1,0:T(8,128)(2,1)}, u32[]{:S(2)}) copy-start(bf16[256,128]{1,0:T(8,128)(2,1)} %constant.68.clone.down_z) | copy-start | bytes 196612
  2.0 9.4 %collective-permute-start = (bf16[24,32,128]{2,1,0:T(8,128)(2,1)S(1)}, bf16[24,32,128]{2,1,0:T(8,128)(2,1)S(1)}, u32[]{:S(2)}, u32[]{:S(2)}) collective-permute-start(bf16[24,32,128]{2,1,0:T(8,128)(2,1)S(1)} %get-tuple-element.40), channel_id=1, source_target_pairs={{0,1},{2,3},{1,0},{3,2},{4,5},{6,7},{5,4},{7,6},{8,9},{10,11},{9,8... | collective-permute-start | bytes 589832 | tf_op jit(solution)/shard_map/ppermute | solution.py:592
  5.0 0.8 %copy-start.16 = (bf16[15,15,15]{2,1,0:T(8,128)(2,1)S(1)}, bf16[15,15,15]{2,1,0:T(8,128)(2,1)}, u32[]{:S(2)}) copy-start(bf16[15,15,15]{2,1,0:T(8,128)(2,1)} %refs_0_.1) | copy-start | bytes 20254
  5.8 0.8 %copy-start.17 = (bf16[15,15,15]{2,1,0:T(8,128)(2,1)S(1)}, bf16[15,15,15]{2,1,0:T(8,128)(2,1)}, u32[]{:S(2)}) copy-start(bf16[15,15,15]{2,1,0:T(8,128)(2,1)} %refs_1_.1) | copy-start | bytes 20254
  6.6 0.8 %copy-start.18 = (bf16[15,15,15]{2,1,0:T(8,128)(2,1)S(1)}, bf16[15,15,15]{2,1,0:T(8,128)(2,1)}, u32[]{:S(2)}) copy-start(bf16[15,15,15]{2,1,0:T(8,128)(2,1)} %refs_2_.1) | copy-start | bytes 20254
  7.5 0.8 %copy-start.20 = (bf16[160,48]{1,0:T(8,128)(2,1)S(1)}, bf16[160,48]{1,0:T(8,128)(2,1)}, u32[]{:S(2)}) copy-start(bf16[160,48]{1,0:T(8,128)(2,1)} %constant.63.clone.refs_4_) | copy-start | bytes 46084
  9.0 2.5 %copy-start.22 = (bf16[64,240]{1,0:T(8,128)(2,1)S(1)}, bf16[64,240]{1,0:T(8,128)(2,1)}, u32[]{:S(2)}) copy-start(bf16[64,240]{1,0:T(8,128)(2,1)} %constant.69.clone.down_y) | copy-start | bytes 92164
  11.5 10.8 %copy-start.1 = (bf16[256,256]{1,0:T(8,128)(2,1)S(1)}, bf16[256,256]{1,0:T(8,128)(2,1)}, u32[]{:S(2)}) copy-start(bf16[256,256]{1,0:T(8,128)(2,1)} %constant.70.clone.to_z) | copy-start | bytes 393220
  11.5 10.8 %copy-start.2 = (bf16[160,240]{1,0:T(8,128)(2,1)S(1)}, bf16[160,240]{1,0:T(8,128)(2,1)}, u32[]{:S(2)}) copy-start(bf16[160,240]{1,0:T(8,128)(2,1)} %constant.71.clone.to_y) | copy-start | bytes 230404
  11.5 16.6 %copy-start.6 = (bf16[768,128]{1,0:T(8,128)(2,1)S(1)}, bf16[768,128]{1,0:T(8,128)(2,1)}, u32[]{:S(2)}) copy-start(bf16[768,128]{1,0:T(8,128)(2,1)} %constant.73.clone.from_z) | copy-start | bytes 589828
  11.5 16.6 %copy-start.8 = (bf16[256,256]{1,0:T(8,128)(2,1)S(1)}, bf16[256,256]{1,0:T(8,128)(2,1)}, u32[]{:S(2)}) copy-start(bf16[256,256]{1,0:T(8,128)(2,1)} %constant.75.clone.m_high) | copy-start | bytes 393220
  11.5 16.6 %copy-start.9 = (bf16[256,256]{1,0:T(8,128)(2,1)S(1)}, bf16[256,256]{1,0:T(8,128)(2,1)}, u32[]{:S(2)}) copy-start(bf16[256,256]{1,0:T(8,128)(2,1)} %constant.74.clone.m_low) | copy-start | bytes 393220
  11.5 16.6 %copy-start.13 = (bf16[2,128,96]{2,1,0:T(8,128)(2,1)S(1)}, bf16[2,128,96]{2,1,0:T(8,128)(2,1)}, u32[]{:S(2)}) copy-start(bf16[2,128,96]{2,1,0:T(8,128)(2,1)} %constant.83.clone.t_from_y) | copy-start | bytes 147460
  11.6 16.6 %copy-start.14 = (bf16[128,240]{1,0:T(8,128)(2,1)S(1)}, bf16[128,240]{1,0:T(8,128)(2,1)}, u32[]{:S(2)}) copy-start(bf16[128,240]{1,0:T(8,128)(2,1)} %constant.72.clone.from_y) | copy-start | bytes 184324
  11.6 16.6 %copy-start.19 = (bf16[96,144]{1,0:T(8,128)(2,1)S(1)}, bf16[96,144]{1,0:T(8,128)(2,1)}, u32[]{:S(2)}) copy-start(bf16[96,144]{1,0:T(8,128)(2,1)} %constant.76.clone.m_to_y) | copy-start | bytes 82948
  11.6 16.6 %copy-start.21 = (bf16[64,256]{1,0:T(8,128)(2,1)S(1)}, bf16[64,256]{1,0:T(8,128)(2,1)}, u32[]{:S(2)}) copy-start(bf16[64,256]{1,0:T(8,128)(2,1)} %constant.81.clone.t_to_z) | copy-start | bytes 98308
  11.6 16.6 %copy-start.24 = (bf16[64,96]{1,0:T(8,128)(2,1)S(1)}, bf16[64,96]{1,0:T(8,128)(2,1)}, u32[]{:S(2)}) copy-start(bf16[64,96]{1,0:T(8,128)(2,1)} %constant.82.clone.t_to_y) | copy-start | bytes 36868
  11.6 16.6 %copy-start.25 = (bf16[64,96]{1,0:T(8,128)(2,1)S(1)}, bf16[64,96]{1,0:T(8,128)(2,1)}, u32[]{:S(2)}) copy-start(bf16[64,96]{1,0:T(8,128)(2,1)} %constant.79.clone.t_down_y) | copy-start | bytes 36868
  13.3 14.8 %collective-permute-start.2 = (bf16[1104,128]{1,0:T(8,128)(2,1)S(1)}, bf16[1104,128]{1,0:T(8,128)(2,1)S(1)}, u32[]{:S(2)}, u32[]{:S(2)}) collective-permute-start(bf16[1104,128]{1,0:T(8,128)(2,1)S(1)} %get-tuple-element.26), channel_id=1, source_target_pairs={{0,4},{8,12},{16,20},{24,28},{4,0},{12,8},{20,16},{28,24},{1,5},{9... | collective-permute-start | bytes 847880 | tf_op jit(solution)/shard_map/ppermute | solution.py:592
  14.9 13.3 %collective-permute-start.3 = (bf16[1104,128]{1,0:T(8,128)(2,1)S(1)}, bf16[1104,128]{1,0:T(8,128)(2,1)S(1)}, u32[]{:S(2)}, u32[]{:S(2)}) collective-permute-start(bf16[1104,128]{1,0:T(8,128)(2,1)S(1)} %get-tuple-element.27), channel_id=1, source_target_pairs={{4,8},{12,16},{20,24},{8,4},{16,12},{24,20},{5,9},{13,17},{21,25},... | collective-permute-start | bytes 847880 | tf_op jit(solution)/shard_map/ppermute | solution.py:592
  17.2 8.0 %collective-permute-start.4 = (bf16[6,32,128]{2,1,0:T(8,128)(2,1)S(1)}, bf16[6,32,128]{2,1,0:T(8,128)(2,1)S(1)}, u32[]{:S(2)}, u32[]{:S(2)}) collective-permute-start(bf16[6,32,128]{2,1,0:T(8,128)(2,1)S(1)} %get-tuple-element.28), channel_id=1, source_target_pairs={{0,8},{4,12},{16,24},{20,28},{8,0},{12,4},{24,16},{28,20},{1,9},{5... | collective-permute-start | bytes 147464 | tf_op jit(solution)/shard_map/ppermute | solution.py:592
  17.3 8.9 %collective-permute-start.5 = (bf16[6,32,128]{2,1,0:T(8,128)(2,1)S(1)}, bf16[6,32,128]{2,1,0:T(8,128)(2,1)S(1)}, u32[]{:S(2)}, u32[]{:S(2)}) collective-permute-start(bf16[6,32,128]{2,1,0:T(8,128)(2,1)S(1)} %get-tuple-element.29), channel_id=1, source_target_pairs={{8,16},{12,20},{16,8},{20,12},{9,17},{13,21},{17,9},{21,13},{10,18... | collective-permute-start | bytes 147464 | tf_op jit(solution)/shard_map/ppermute | solution.py:592
  22.4 5.9 %copy-start.3 = (bf16[768,128]{1,0:T(8,128)(2,1)S(1)}, bf16[768,128]{1,0:T(8,128)(2,1)}, u32[]{:S(2)}) copy-start(bf16[768,128]{1,0:T(8,128)(2,1)} %constant.84.clone.t_from_z) | copy-start | bytes 589828
  22.4 5.8 %copy-start.4 = (bf16[768,32]{1,0:T(8,128)(2,1)S(1)}, bf16[768,32]{1,0:T(8,128)(2,1)}, u32[]{:S(2)}) copy-start(bf16[768,32]{1,0:T(8,128)(2,1)} %constant.80.clone.t_down_z) | copy-start | bytes 147460
  22.4 5.8 %copy-start.5 = (bf16[768,128]{1,0:T(8,128)(2,1)S(1)}, bf16[768,128]{1,0:T(8,128)(2,1)}, u32[]{:S(2)}) copy-start(bf16[768,128]{1,0:T(8,128)(2,1)} %constant.78.clone.m_from_z) | copy-start | bytes 589828
  22.4 5.8 %copy-start.7 = (bf16[2,128,144]{2,1,0:T(8,128)(2,1)S(1)}, bf16[2,128,144]{2,1,0:T(8,128)(2,1)}, u32[]{:S(2)}) copy-start(bf16[2,128,144]{2,1,0:T(8,128)(2,1)} %constant.77.clone.m_from_y) | copy-start | bytes 221188
  (1 other events, 0.7 us)

commit v5 on v4

--- a/solution.py
+++ b/solution.py
@@ -197,10 +197,11 @@
     batches(count, size, body)
 
 
-def along_x(real, imag, spectrum, out_real, out_imag, block):
+def along_x(real, imag, spectrum, out_real, out_imag, block, taken=None, before=None):
     kernel_r, kernel_d, kernel_s = spectrum
     taps, period = kernel_r.shape[:2]
     out_x = out_real.shape[0]
+    taken = taken or (lambda x: True)
 
     def body(part, _):
         rows = pl.ds(pl.multiple_of(8 * part, 8), 8)
@@ -209,18 +210,25 @@
             sums = [[None] * 3 for _ in range(count)]
             seen = {}
             for a in range(taps):
-                weights = kernel_r[a, rows, :], kernel_d[a, rows, :], kernel_s[a, rows, :]
-                for i in range(count):
+                used = [i for i in range(count) if taken(start + i + a)]
+                if used:
+                    weights = kernel_r[a, rows, :], kernel_d[a, rows, :], kernel_s[a, rows, :]
+                for i in used:
                     x = start + i + a
                     if x not in seen:
                         r, m = real(x, rows), imag(x, rows)
                         seen[x] = r + m, r, m
                     for k in range(3):
                         term = weights[k] * seen[x][k]
-                        sums[i][k] = term if a == 0 else sums[i][k] + term
+                        sums[i][k] = term if sums[i][k] is None else sums[i][k] + term
             for i in range(count):
-                out_real[start + i, rows, :] = sums[i][0] - sums[i][2]
-                out_imag[start + i, rows, :] = sums[i][0] + sums[i][1]
+                values = []
+                if sums[i][0] is not None:
+                    values.append((sums[i][0] - sums[i][2], sums[i][0] + sums[i][1]))
+                if before is not None:
+                    values.append((before[0][start + i, rows, :], before[1][start + i, rows, :]))
+                out_real[start + i, rows, :] = sum(value[0] for value in values)
+                out_imag[start + i, rows, :] = sum(value[1] for value in values)
         return 0
 
     lax.fori_loop(0, period // 8, body, 0)
@@ -243,19 +251,22 @@
 
 def spectra_kernel(levels, *refs):
     kernels, refs = refs[:levels], refs[levels:]
-    tables, outs, (padded, mid) = refs[: 2 * levels], refs[2 * levels : -2], refs[-2:]
+    table, outs, (padded, mid) = refs[0], refs[1:-2], refs[-2:]
+    at = 0
     taps = kernels[0].shape[0]
     padded[...] = jnp.zeros(padded.shape, padded.dtype)
     for level in range(levels):
-        kernel_z, kernel_y = tables[2 * level : 2 * level + 2]
         outs_here = outs[3 * level : 3 * level + 3]
         period = outs_here[0].shape[1]
+        kernel_z = table[at : at + 2 * LANES, :]
+        kernel_y = table[at + 2 * LANES : at + 2 * LANES + 2 * period, : 3 * padded.shape[1]]
+        at += 2 * LANES + 2 * period
         padded[:, :taps, :taps] = kernels[level][...].astype(F32)
         cells = padded[...].astype(BF).reshape(taps * padded.shape[1], LANES)
-        mid[...] = dot(jnp.concatenate([cells, cells], 1), kernel_z[...])
+        mid[...] = dot(jnp.concatenate([cells, cells], 1), kernel_z)
 
         def body(xs, first, kernel_y=kernel_y, outs=outs_here, period=period):
-            spreads = [dot(kernel_y[...], stacked(mid[rows_at(a, 16, 1), :])) for a in xs]
+            spreads = [dot(kernel_y, stacked(mid[rows_at(a, 16, 1), :])) for a in xs]
             for a, spread in zip(xs, spreads):
                 real = spread[:period, :LANES] - spread[period:, LANES:]
                 imag = spread[:period, LANES:] + spread[period:, :LANES]
@@ -336,14 +347,25 @@
             out[k] = coarse[first + k]
 
 
-def own_kernel(near, to_z, to_y, real, imag, ahead):
-    to_frequencies_z(lambda x: near[x], real.shape[0], 4, to_z, ahead)
+def own_kernel(near, kr, kd, ks, to_z, to_y, out_real, out_imag, real, imag, ahead):
+    count = real.shape[0]
+    half = kr.shape[0] // 2
+    to_frequencies_z(lambda x: near[x], count, 4, to_z, ahead)
     to_frequencies_y(ahead, 4, to_y, real, imag)
+    along_x(
+        lambda x, rows: real[x - half, rows, :],
+        lambda x, rows: imag[x - half, rows, :],
+        (kr, kd, ks),
+        out_real,
+        out_imag,
+        8,
+        lambda x: half <= x < half + count,
+    )
 
 
 def final_kernel(
-    own_real,
-    own_imag,
+    part_real,
+    part_imag,
     next_a,
     next_b,
     far_a,
@@ -401,7 +423,7 @@
     ended_x, close_x = left_x == 1, left_x <= 2
     ended_y = (lax.axis_index("gy") == lax.axis_size("gy") - 1).astype(jnp.int32)
     up_x, up_far = leads("gx", 1), leads("gx", 2)
-    count, width = own_real.shape[:2]
+    count, width = part_real.shape[:2]
     reach = side_real.shape[0] // 2
     top_rows = left_x * (count // 4) + reach
 
@@ -431,17 +453,19 @@
         ahead[1, rows_at(first, period, len(xs)), :] = low
     to_frequencies_y(ahead, 7, to_y, side_real, side_imag)
 
-    def source(own, side):
-        def read(x, rows):
-            if x < reach:
-                return side[x, rows, :]
-            if x < reach + count:
-                return own[x - reach, rows, :]
-            return side[x - count, rows, :]
-
-        return read
-
-    along_x(source(own_real, side_real), source(own_imag, side_imag), (kr, kd, ks), er, ei, 8)
+    def source(side):
+        return lambda x, rows: side[x if x < reach else x - count, rows, :]
+
+    along_x(
+        source(side_real),
+        source(side_imag),
+        (kr, kd, ks),
+        er,
+        ei,
+        8,
+        lambda x: x < reach or x >= reach + count,
+        (part_real, part_imag),
+    )
     from_frequencies_y(er, ei, 4, from_y, back)
 
     def fine_write(x, value):
@@ -628,12 +652,15 @@
         for level in levels
         for _ in range(3)
     ]
-    tables = [table for level in levels for table in (level.kernel_z, level.kernel_y)]
+    tables = []
+    for level in levels:
+        tables.append(level.kernel_z)
+        tables.append(np.pad(level.kernel_y, ((0, 0), (0, 2 * LANES - level.kernel_y.shape[1]))))
     spectra = call(
         functools.partial(spectra_kernel, 3),
         outs,
         [(F32, (taps, 16, LANES)), (F32, (taps * 16, 2 * LANES))],
-        [kernel_fine, kernel_mid, kernel_top, *tables],
+        [kernel_fine, kernel_mid, kernel_top, np.concatenate(tables, 0)],
         8,
     )
 
@@ -686,9 +713,9 @@
     own = call(
         own_kernel,
         [jax.ShapeDtypeStruct((nx, fine.period_y, LANES), F32)] * 2,
-        [(BF, (2, nx * fine.period_y, 2 * LANES))],
-        [near, fine.to_z, fine.to_y],
-        8,
+        [(F32, (nx, fine.period_y, LANES))] * 2 + [(BF, (2, nx * fine.period_y, 2 * LANES))],
+        [near, *spectra[:3], fine.to_z, fine.to_y],
+        12,
     )
 
     wide_top = ty + 2 * wide

time: 44.9 us -> 40.4 us (0.90); the launches traced: 44 us -> 40 us
  waiting for transfers between devices: 2.93 us -> 0.02 us
  local copies, waits for them, and re-layouts: 5.39 us -> 4.44 us
    ppermute x6, waiting for transfers between devices: 2.93 us -> 0.02 us  [swapped(): outs.append(lax.ppermute(value, axis, pairs))]
    unnamed x54 -> x44, local copies, waits for them, and re-layouts: 4.11 us -> 3.15 us
  transfers between devices with their start and end apart: 6 -> 6, of which waited for: 2 -> 0; matrix products, arithmetic and copies ran while one was open for 0% -> 0% of each run, Pallas kernels for 12% -> 21%
where the time goes in v5:
time: 40.4 us; the launch traced here: 40 us
  Pallas kernels  22.6 us (56%)
  starting transfers between devices  12.6 us (31%)
  local copies, waits for them, and re-layouts  4.44 us (11%)
    pallas_call x4, Pallas kernels, call(): pl.pallas_call(kernel, out_shape=outs, in_specs=[pl.BlockSpec(memory_spac...  22.6 us
    ppermute x6, starting transfers between devices, swapped(): outs.append(lax.ppermute(value, axis, pairs))  12.6 us
    unnamed x44, local copies, waits for them, and re-layouts  3.15 us
    convert_element_type x1, local copies, waits for them, and re-layouts, shards(): lax.dynamic_slice_in_dim(charges, jnp.where(flag, side, 0), side, 1)  1.29 us
  transfers between devices with their start and end apart: 6, of which 0 were waited for; matrix products, arithmetic and copies ran while one was open for 0% of the time, Pallas kernels for 21%

profile of v5, /device:TPU:8, one launch (start us, length us, event | category | flops | bytes accessed | tf_op | source)
XLA Modules:
  0.0 40.0 jit_solution(8305775628257509367)
XLA Ops:
  0.0 1.3 %dynamic-slice_convert_fusion = (bf16[24,32,128]{2,1,0:T(8,128)(2,1)S(1)}, bf16[24,32,128]{2,1,0:T(8,128)(2,1)S(1)}) fusion(f32[24,64,128]{2,1,0:T(8,128)} %own.1, s32[]{:T(128)S(6)} %select_n.10, s32[]{:T(128)S(6)} %select_n.9), kind=kLoop, calls=%fused_computation | loop fusion | bytes 786440 | tf_op jit(solution)/shard_map/convert_element_type | solution.py:671
  1.3 0.7 %collective-permute-start.1 = (bf16[24,32,128]{2,1,0:T(8,128)(2,1)S(1)}, bf16[24,32,128]{2,1,0:T(8,128)(2,1)S(1)}, u32[]{:S(2)}, u32[]{:S(2)}) collective-permute-start(bf16[24,32,128]{2,1,0:T(8,128)(2,1)S(1)} %get-tuple-element.39), channel_id=1, source_target_pairs={{1,2},{2,1},{5,6},{6,5},{9,10},{10,9},{13,14},{14,13},{17,18},{18,... | collective-permute-start | bytes 589832 | tf_op jit(solution)/shard_map/ppermute | solution.py:616
  2.0 0.0 copy-start.13
  2.0 2.9 %collective-permute-start = (bf16[24,32,128]{2,1,0:T(8,128)(2,1)S(1)}, bf16[24,32,128]{2,1,0:T(8,128)(2,1)S(1)}, u32[]{:S(2)}, u32[]{:S(2)}) collective-permute-start(bf16[24,32,128]{2,1,0:T(8,128)(2,1)S(1)} %get-tuple-element.40), channel_id=1, source_target_pairs={{0,1},{2,3},{1,0},{3,2},{4,5},{6,7},{5,4},{7,6},{8,9},{10,11},{9,8... | collective-permute-start | bytes 589832 | tf_op jit(solution)/shard_map/ppermute | solution.py:616
  4.9 0.8 %copy-done.14 = bf16[15,15,15]{2,1,0:T(8,128)(2,1)S(1)} copy-done((bf16[15,15,15]{2,1,0:T(8,128)(2,1)S(1)}, bf16[15,15,15]{2,1,0:T(8,128)(2,1)}, u32[]{:S(2)}) %copy-start.14) | copy-done | bytes 6774
  5.8 0.8 %copy-done.15 = bf16[15,15,15]{2,1,0:T(8,128)(2,1)S(1)} copy-done((bf16[15,15,15]{2,1,0:T(8,128)(2,1)S(1)}, bf16[15,15,15]{2,1,0:T(8,128)(2,1)}, u32[]{:S(2)}) %copy-start.15) | copy-done | bytes 6774
  6.6 0.8 %copy-done.16 = bf16[15,15,15]{2,1,0:T(8,128)(2,1)S(1)} copy-done((bf16[15,15,15]{2,1,0:T(8,128)(2,1)S(1)}, bf16[15,15,15]{2,1,0:T(8,128)(2,1)}, u32[]{:S(2)}) %copy-start.16) | copy-done | bytes 6774
  7.4 2.4 %shard_map.208 = (f32[15,80,128]{2,1,0:T(8,128)S(1)}, f32[15,80,128]{2,1,0:T(8,128)S(1)}, f32[15,80,128]{2,1,0:T(8,128)S(1)}, f32[15,48,128]{2,1,0:T(8,128)S(1)}...) custom-call(bf16[15,15,15]{2,1,0:T(8,128)(2,1)S(1)} %copy-done.14, ...), custom_call_target="tpu_custom_call" | custom-call | tf_op jit(solution)/shard_map/pallas_call | solution.py:582
  9.9 0.0 collective-permute-done.got_a
  9.9 0.0 copy-start.2
  9.9 0.0 copy-start.3
  10.0 1.7 %shard_map.209 = (bf16[24,80,128]{2,1,0:T(8,128)(2,1)S(1)}, bf16[17,32,128]{2,1,0:T(8,128)(2,1)S(1)}, bf16[1104,128]{1,0:T(8,128)(2,1)S(1)}, bf16[1104,128]{1,0:...) custom-call(f32[24,64,128]{2,1,0:T(8,128)S(1)} %copy-done, ...), custom_call_target="tpu_custom_call" | custom-call | tf_op jit(solution)/shard_map/pallas_call | solution.py:582
  11.6 1.6 %collective-permute-start.2 = (bf16[1104,128]{1,0:T(8,128)(2,1)S(1)}, bf16[1104,128]{1,0:T(8,128)(2,1)S(1)}, u32[]{:S(2)}, u32[]{:S(2)}) collective-permute-start(bf16[1104,128]{1,0:T(8,128)(2,1)S(1)} %get-tuple-element.28), channel_id=1, source_target_pairs={{0,4},{8,12},{16,20},{24,28},{4,0},{12,8},{20,16},{28,24},{1,5},{9... | collective-permute-start | bytes 847880 | tf_op jit(solution)/shard_map/ppermute | solution.py:616
  13.2 2.3 %collective-permute-start.3 = (bf16[1104,128]{1,0:T(8,128)(2,1)S(1)}, bf16[1104,128]{1,0:T(8,128)(2,1)S(1)}, u32[]{:S(2)}, u32[]{:S(2)}) collective-permute-start(bf16[1104,128]{1,0:T(8,128)(2,1)S(1)} %get-tuple-element.29), channel_id=1, source_target_pairs={{4,8},{12,16},{20,24},{8,4},{16,12},{24,20},{5,9},{13,17},{21,25},... | collective-permute-start | bytes 847880 | tf_op jit(solution)/shard_map/ppermute | solution.py:616
  15.5 0.1 collective-permute-start.4
  15.6 5.0 %collective-permute-start.5 = (bf16[6,32,128]{2,1,0:T(8,128)(2,1)S(1)}, bf16[6,32,128]{2,1,0:T(8,128)(2,1)S(1)}, u32[]{:S(2)}, u32[]{:S(2)}) collective-permute-start(bf16[6,32,128]{2,1,0:T(8,128)(2,1)S(1)} %get-tuple-element.31), channel_id=1, source_target_pairs={{8,16},{12,20},{16,8},{20,12},{9,17},{13,21},{17,9},{21,13},{10,18... | collective-permute-start | bytes 147464 | tf_op jit(solution)/shard_map/ppermute | solution.py:616
  20.7 0.0 copy-start.4
  20.7 0.0 copy-start.5
  20.7 0.0 copy-start.6
  20.7 0.0 copy-start.7
  20.7 0.0 copy-start.8
  20.7 0.0 copy-start.9
  20.7 0.0 copy-start.10
  20.8 0.0 copy-start.11
  20.8 0.0 copy-start.12
  20.8 0.0 copy-start.17
  20.8 0.0 copy-start.18
  20.8 0.0 copy-start.21
  20.8 6.0 %shard_map.210 = (f32[24,80,128]{2,1,0:T(8,128)S(1)}, f32[24,80,128]{2,1,0:T(8,128)S(1)}) custom-call(bf16[24,80,128]{2,1,0:T(8,128)(2,1)S(1)} %get-tuple-element.23.near, f32[15,80,128]{2,1,0:T(8,128)S(1)} %get-tuple-element.22.ordered.kr, f32[15,80,128]{2,1,0:T(8,128)S(1)} %get-tuple-element.24.kd, f32[15,80,128]{2,1,0:T(8,128)S(1)} %get-tuple-element.25.ks, ...), custom_call_target="tpu_custom_call" | custom-call | tf_op jit(solution)/shard_map/pallas_call | solution.py:582
  26.8 0.0 copy-start.20
  27.0 0.5 %copy-done.20 = bf16[64,96]{1,0:T(8,128)(2,1)S(1)} copy-done((bf16[64,96]{1,0:T(8,128)(2,1)S(1)}, bf16[64,96]{1,0:T(8,128)(2,1)}, u32[]{:S(2)}) %copy-start.20) | copy-done | bytes 12312
  27.5 12.5 %shard_map.211 = f32[24,64,128]{2,1,0:T(8,128)} custom-call(f32[24,80,128]{2,1,0:T(8,128)S(1)} %get-tuple-element.26.part_real, f32[24,80,128]{2,1,0:T(8,128)S(1)} %get-tuple-element.27.part_imag, bf16[1104,128]{1,0:T(8,128)(2,1)S(1)} %collective-permute-done.2.next_a, bf16[1104,128]{1,0:T(8,128)(2,1)S(1)} %collective-permute-done.3.next_b, ...), custom_call_target="tpu_custom_call" | custom-call | tf_op jit(solution)/shard_map/pallas_call | solution.py:582
  (29 shorter events, 0.1 us)
Async XLA Ops:
  0.0 4.9 %copy-start.1 = (bf16[1088,256]{1,0:T(8,128)(2,1)S(1)}, bf16[1088,256]{1,0:T(8,128)(2,1)}, u32[]{:S(2)}) copy-start(bf16[1088,256]{1,0:T(8,128)(2,1)} %constant.52.clone.refs_3_) | copy-start | bytes 1671172
  0.0 9.9 %copy-start = (f32[24,64,128]{2,1,0:T(8,128)S(1)}, f32[24,64,128]{2,1,0:T(8,128)}, u32[]{:S(2)}) copy-start(f32[24,64,128]{2,1,0:T(8,128)} %own.1) | copy-start | bytes 2359300
  1.3 8.6 %collective-permute-start.1 = (bf16[24,32,128]{2,1,0:T(8,128)(2,1)S(1)}, bf16[24,32,128]{2,1,0:T(8,128)(2,1)S(1)}, u32[]{:S(2)}, u32[]{:S(2)}) collective-permute-start(bf16[24,32,128]{2,1,0:T(8,128)(2,1)S(1)} %get-tuple-element.39), channel_id=1, source_target_pairs={{1,2},{2,1},{5,6},{6,5},{9,10},{10,9},{13,14},{14,13},{17,18},{18,... | collective-permute-start | bytes 589832 | tf_op jit(solution)/shard_map/ppermute | solution.py:616
  2.0 7.9 %copy-start.13 = (bf16[256,128]{1,0:T(8,128)(2,1)S(1)}, bf16[256,128]{1,0:T(8,128)(2,1)}, u32[]{:S(2)}) copy-start(bf16[256,128]{1,0:T(8,128)(2,1)} %constant.53.clone.down_z) | copy-start | bytes 196612
  2.0 7.9 %collective-permute-start = (bf16[24,32,128]{2,1,0:T(8,128)(2,1)S(1)}, bf16[24,32,128]{2,1,0:T(8,128)(2,1)S(1)}, u32[]{:S(2)}, u32[]{:S(2)}) collective-permute-start(bf16[24,32,128]{2,1,0:T(8,128)(2,1)S(1)} %get-tuple-element.40), channel_id=1, source_target_pairs={{0,1},{2,3},{1,0},{3,2},{4,5},{6,7},{5,4},{7,6},{8,9},{10,11},{9,8... | collective-permute-start | bytes 589832 | tf_op jit(solution)/shard_map/ppermute | solution.py:616
  4.9 0.8 %copy-start.14 = (bf16[15,15,15]{2,1,0:T(8,128)(2,1)S(1)}, bf16[15,15,15]{2,1,0:T(8,128)(2,1)}, u32[]{:S(2)}) copy-start(bf16[15,15,15]{2,1,0:T(8,128)(2,1)} %refs_0_.1) | copy-start | bytes 20254
  5.8 0.8 %copy-start.15 = (bf16[15,15,15]{2,1,0:T(8,128)(2,1)S(1)}, bf16[15,15,15]{2,1,0:T(8,128)(2,1)}, u32[]{:S(2)}) copy-start(bf16[15,15,15]{2,1,0:T(8,128)(2,1)} %refs_1_.1) | copy-start | bytes 20254
  6.6 0.8 %copy-start.16 = (bf16[15,15,15]{2,1,0:T(8,128)(2,1)S(1)}, bf16[15,15,15]{2,1,0:T(8,128)(2,1)}, u32[]{:S(2)}) copy-start(bf16[15,15,15]{2,1,0:T(8,128)(2,1)} %refs_2_.1) | copy-start | bytes 20254
  7.4 2.5 %copy-start.19 = (bf16[64,240]{1,0:T(8,128)(2,1)S(1)}, bf16[64,240]{1,0:T(8,128)(2,1)}, u32[]{:S(2)}) copy-start(bf16[64,240]{1,0:T(8,128)(2,1)} %constant.54.clone.down_y) | copy-start | bytes 92164
  9.9 10.7 %copy-start.2 = (bf16[256,256]{1,0:T(8,128)(2,1)S(1)}, bf16[256,256]{1,0:T(8,128)(2,1)}, u32[]{:S(2)}) copy-start(bf16[256,256]{1,0:T(8,128)(2,1)} %constant.55.clone.to_z) | copy-start | bytes 393220
  9.9 10.7 %copy-start.3 = (bf16[160,240]{1,0:T(8,128)(2,1)S(1)}, bf16[160,240]{1,0:T(8,128)(2,1)}, u32[]{:S(2)}) copy-start(bf16[160,240]{1,0:T(8,128)(2,1)} %constant.56.clone.to_y) | copy-start | bytes 230404
  11.6 15.2 %collective-permute-start.2 = (bf16[1104,128]{1,0:T(8,128)(2,1)S(1)}, bf16[1104,128]{1,0:T(8,128)(2,1)S(1)}, u32[]{:S(2)}, u32[]{:S(2)}) collective-permute-start(bf16[1104,128]{1,0:T(8,128)(2,1)S(1)} %get-tuple-element.28), channel_id=1, source_target_pairs={{0,4},{8,12},{16,20},{24,28},{4,0},{12,8},{20,16},{28,24},{1,5},{9... | collective-permute-start | bytes 847880 | tf_op jit(solution)/shard_map/ppermute | solution.py:616
  13.2 13.6 %collective-permute-start.3 = (bf16[1104,128]{1,0:T(8,128)(2,1)S(1)}, bf16[1104,128]{1,0:T(8,128)(2,1)S(1)}, u32[]{:S(2)}, u32[]{:S(2)}) collective-permute-start(bf16[1104,128]{1,0:T(8,128)(2,1)S(1)} %get-tuple-element.29), channel_id=1, source_target_pairs={{4,8},{12,16},{20,24},{8,4},{16,12},{24,20},{5,9},{13,17},{21,25},... | collective-permute-start | bytes 847880 | tf_op jit(solution)/shard_map/ppermute | solution.py:616
  15.5 11.3 %collective-permute-start.4 = (bf16[6,32,128]{2,1,0:T(8,128)(2,1)S(1)}, bf16[6,32,128]{2,1,0:T(8,128)(2,1)S(1)}, u32[]{:S(2)}, u32[]{:S(2)}) collective-permute-start(bf16[6,32,128]{2,1,0:T(8,128)(2,1)S(1)} %get-tuple-element.30), channel_id=1, source_target_pairs={{0,8},{4,12},{16,24},{20,28},{8,0},{12,4},{24,16},{28,20},{1,9},{5... | collective-permute-start | bytes 147464 | tf_op jit(solution)/shard_map/ppermute | solution.py:616
  15.6 11.2 %collective-permute-start.5 = (bf16[6,32,128]{2,1,0:T(8,128)(2,1)S(1)}, bf16[6,32,128]{2,1,0:T(8,128)(2,1)S(1)}, u32[]{:S(2)}, u32[]{:S(2)}) collective-permute-start(bf16[6,32,128]{2,1,0:T(8,128)(2,1)S(1)} %get-tuple-element.31), channel_id=1, source_target_pairs={{8,16},{12,20},{16,8},{20,12},{9,17},{13,21},{17,9},{21,13},{10,18... | collective-permute-start | bytes 147464 | tf_op jit(solution)/shard_map/ppermute | solution.py:616
  20.7 6.2 %copy-start.4 = (bf16[768,128]{1,0:T(8,128)(2,1)S(1)}, bf16[768,128]{1,0:T(8,128)(2,1)}, u32[]{:S(2)}) copy-start(bf16[768,128]{1,0:T(8,128)(2,1)} %constant.69.clone.t_from_z) | copy-start | bytes 589828
  20.7 6.2 %copy-start.5 = (bf16[768,32]{1,0:T(8,128)(2,1)S(1)}, bf16[768,32]{1,0:T(8,128)(2,1)}, u32[]{:S(2)}) copy-start(bf16[768,32]{1,0:T(8,128)(2,1)} %constant.65.clone.t_down_z) | copy-start | bytes 147460
  20.7 6.2 %copy-start.6 = (bf16[768,128]{1,0:T(8,128)(2,1)S(1)}, bf16[768,128]{1,0:T(8,128)(2,1)}, u32[]{:S(2)}) copy-start(bf16[768,128]{1,0:T(8,128)(2,1)} %constant.63.clone.m_from_z) | copy-start | bytes 589828
  20.7 6.2 %copy-start.7 = (bf16[768,128]{1,0:T(8,128)(2,1)S(1)}, bf16[768,128]{1,0:T(8,128)(2,1)}, u32[]{:S(2)}) copy-start(bf16[768,128]{1,0:T(8,128)(2,1)} %constant.58.clone.from_z) | copy-start | bytes 589828
  20.7 6.2 %copy-start.8 = (bf16[2,128,144]{2,1,0:T(8,128)(2,1)S(1)}, bf16[2,128,144]{2,1,0:T(8,128)(2,1)}, u32[]{:S(2)}) copy-start(bf16[2,128,144]{2,1,0:T(8,128)(2,1)} %constant.62.clone.m_from_y) | copy-start | bytes 221188
  20.7 6.2 %copy-start.9 = (bf16[256,256]{1,0:T(8,128)(2,1)S(1)}, bf16[256,256]{1,0:T(8,128)(2,1)}, u32[]{:S(2)}) copy-start(bf16[256,256]{1,0:T(8,128)(2,1)} %constant.60.clone.m_high) | copy-start | bytes 393220
  20.7 6.2 %copy-start.10 = (bf16[256,256]{1,0:T(8,128)(2,1)S(1)}, bf16[256,256]{1,0:T(8,128)(2,1)}, u32[]{:S(2)}) copy-start(bf16[256,256]{1,0:T(8,128)(2,1)} %constant.59.clone.m_low) | copy-start | bytes 393220
  20.8 6.2 %copy-start.11 = (bf16[2,128,96]{2,1,0:T(8,128)(2,1)S(1)}, bf16[2,128,96]{2,1,0:T(8,128)(2,1)}, u32[]{:S(2)}) copy-start(bf16[2,128,96]{2,1,0:T(8,128)(2,1)} %constant.68.clone.t_from_y) | copy-start | bytes 147460
  20.8 6.2 %copy-start.12 = (bf16[128,240]{1,0:T(8,128)(2,1)S(1)}, bf16[128,240]{1,0:T(8,128)(2,1)}, u32[]{:S(2)}) copy-start(bf16[128,240]{1,0:T(8,128)(2,1)} %constant.57.clone.from_y) | copy-start | bytes 184324
  20.8 6.2 %copy-start.17 = (bf16[96,144]{1,0:T(8,128)(2,1)S(1)}, bf16[96,144]{1,0:T(8,128)(2,1)}, u32[]{:S(2)}) copy-start(bf16[96,144]{1,0:T(8,128)(2,1)} %constant.61.clone.m_to_y) | copy-start | bytes 82948
  20.8 6.2 %copy-start.18 = (bf16[64,256]{1,0:T(8,128)(2,1)S(1)}, bf16[64,256]{1,0:T(8,128)(2,1)}, u32[]{:S(2)}) copy-start(bf16[64,256]{1,0:T(8,128)(2,1)} %constant.66.clone.t_to_z) | copy-start | bytes 98308
  20.8 6.2 %copy-start.21 = (bf16[64,96]{1,0:T(8,128)(2,1)S(1)}, bf16[64,96]{1,0:T(8,128)(2,1)}, u32[]{:S(2)}) copy-start(bf16[64,96]{1,0:T(8,128)(2,1)} %constant.64.clone.t_down_y) | copy-start | bytes 36868
  26.8 0.7 %copy-start.20 = (bf16[64,96]{1,0:T(8,128)(2,1)S(1)}, bf16[64,96]{1,0:T(8,128)(2,1)}, u32[]{:S(2)}) copy-start(bf16[64,96]{1,0:T(8,128)(2,1)} %constant.67.clone.t_to_y) | copy-start | bytes 36868

commit v6 on v5

--- a/solution.py
+++ b/solution.py
@@ -19,16 +19,14 @@
     return high, low
 
 
-def beside(real, imag):
-    out = np.zeros((real.shape[0], 2 * LANES))
-    out[:, : real.shape[1]] = real
-    out[:, LANES : LANES + imag.shape[1]] = imag
-    return out
-
-
 def three_terms(matrix):
     high, low = two(matrix)
     return np.concatenate([high, high, low], 1)
+
+
+def terms_below(matrix):
+    high, low = two(matrix)
+    return np.concatenate([high, high, low], 0)
 
 
 def up(count):
@@ -49,43 +47,61 @@
 
 
 class Level:
-    def __init__(self, taps, out_x, out_y, shift, period_y, size_z, rows_y, rows_y_end, cols_z):
+    def __init__(self, taps, out_x, out_y, shift, window, size_z, rows_y, rows_y_end, cols_z):
         half = taps // 2
         self.taps, self.out_x, self.in_x = taps, out_x, out_x + taps - 1
-        self.period_y, self.size_z = period_y, size_z
-        period_z = size_z + half + (size_z + half) % 2
-        assert period_y >= shift + out_y + half and shift >= half and period_y % 16 == 0
-        freq_z = np.arange(period_z // 2 + 1)
-        assert len(freq_z) <= LANES
-        freq_y = np.arange(period_y)
+        period_y = out_y + 2 * half + (out_y + 1) % 2
+        period_z = size_z + half
+        self.freq = (period_y + 1) // 2
+        self.main = min(LANES, period_z)
+        self.left = period_z - self.main
+        assert self.freq % 8 == 0 and self.left <= 8 and self.freq <= LANES
+        self.rows = self.freq + (8 if self.left else 0)
         turn_z, turn_y = 2 * np.pi / period_z, 2 * np.pi / period_y
-        angle = turn_z * np.outer(np.arange(size_z), freq_z)
-        table = beside(np.cos(angle), -np.sin(angle))
-        self.to_z = np.concatenate(two(table), 0)
-        self.to_z_packed = [np.concatenate(two(side), 0) for side in both_sides(table)]
-        angle = turn_y * np.outer(freq_y, np.arange(period_y))
-        self.to_y = three_terms(np.concatenate([np.cos(angle), np.sin(angle)], 0))
+        freq_y, freq_z = np.arange(self.freq), np.arange(period_z)
+
+        cells = np.arange(window)
+        needed = (cells >= shift - half) & (cells < shift + out_y + half)
+        angle = turn_y * np.outer(freq_y, cells)
+        self.table_y = np.concatenate([np.cos(angle), -np.sin(angle)], 0) * needed
+        self.to_y = np.concatenate(two(self.table_y), 1)
+        self.table_z = self.columns(turn_z * np.outer(np.arange(size_z), freq_z))
+        self.to_z = terms_below(self.table_z)
+
         offsets = np.arange(taps) - half
-        angle = turn_z * np.outer(offsets, freq_z)
-        table = np.zeros((LANES, 2 * LANES))
-        table[:taps] = beside(np.cos(angle), np.sin(angle))
-        self.kernel_z = np.concatenate(two(table), 0)
-        angle = turn_y * np.outer(freq_y, np.pad(offsets, (0, 1)))
-        self.kernel_y = three_terms(np.concatenate([np.cos(angle), np.sin(angle)], 0))
+        angle = turn_y * np.outer(freq_y, offsets)
+        table = np.zeros((2 * self.freq, 16))
+        table[:, :taps] = np.concatenate([np.cos(angle), np.sin(angle)], 0)
+        self.kernel_y = np.concatenate(two(table), 1)
+        table = self.columns(turn_z * np.outer(offsets, freq_z))
+        table = terms_below(np.pad(table, ((0, 16 - taps), (0, 0))))
+        self.kernel_z = np.pad(table, ((0, LANES - 48), (0, 0)))
+
+        angle = turn_z * np.outer(freq_z, np.arange(size_z))
+        table = np.concatenate([np.cos(angle) @ cols_z.T, np.sin(angle) @ cols_z.T], 1) / period_z
+        lanes = np.zeros((LANES * (2 if self.left else 1), table.shape[1]))
+        lanes[: self.main] = table[: self.main]
+        if self.left:
+            for group in range(self.freq // 8):
+                at = LANES + 8 * group
+                lanes[at : at + self.left] = table[self.main :]
+        self.from_z = terms_below(lanes)
+        weight = np.where(freq_y == 0, 1.0, 2.0) / period_y
         angle = turn_y * np.outer(np.arange(out_y) + shift, freq_y)
-        self.from_y = [
-            three_terms(
-                np.concatenate([rows @ np.cos(angle), rows @ np.sin(angle)], 0) / period_y
-            )
-            for rows in (rows_y, rows_y_end)
-        ]
-        weight = np.where((freq_z == 0) | (2 * freq_z == period_z), 1.0, 2.0)[:, None] / period_z
-        angle = turn_z * np.outer(freq_z, np.arange(size_z))
-        table = np.zeros((2 * LANES, cols_z.shape[0]))
-        table[: len(freq_z)] = (weight * np.cos(angle)) @ cols_z.T
-        table[LANES : LANES + len(freq_z)] = (-weight * np.sin(angle)) @ cols_z.T
-        high, low = two(table)
-        self.from_z = np.concatenate([high, high, low], 0)
+        wave = np.concatenate([weight * np.cos(angle), -weight * np.sin(angle)], 1)
+        self.from_y = [three_terms(rows @ wave) for rows in (rows_y, rows_y_end)]
+
+    def columns(self, angle):
+        out = []
+        for start, stop in ((0, self.main), (self.main, self.main + self.left)):
+            for wave in (np.cos(angle[:, start:stop]), np.sin(angle[:, start:stop])):
+                table = np.zeros((angle.shape[0], LANES))
+                for group in range(1 if start == 0 else self.freq // 8):
+                    table[:, 8 * group : 8 * group + stop - start] = wave
+                out.append(table)
+            if not self.left:
+                break
+        return np.concatenate(out, 1)
 
 
 def down(count, first, length):
@@ -109,9 +125,41 @@
     return out + [value.astype(BF)]
 
 
-def stacked(value):
+def side_by_side(value):
     high, low = split(value, 2)
-    return jnp.concatenate([high, low, high], 0)
+    return jnp.concatenate([high, low, high], 1)
+
+
+def fold(value):
+    groups = value.shape[0] // 8
+    lane = lax.broadcasted_iota(jnp.int32, (8, LANES), 1)
+    out = value[8 * (groups - 1) :]
+    for group in range(groups - 2, -1, -1):
+        out = jnp.where(lane < 8 * (group + 1), value[8 * group : 8 * (group + 1)], out)
+    return out
+
+
+def unfold(value, groups):
+    lane = lax.broadcasted_iota(jnp.int32, (8, LANES), 1)
+    return jnp.concatenate(
+        [
+            jnp.where((lane >= 8 * group) & (lane < 8 * (group + 1)), value, 0.0)
+            for group in range(groups)
+        ],
+        0,
+    )
+
+
+def joined(spread, sign):
+    freq = spread.shape[0] // 2
+    outs = []
+    for at in range(0, spread.shape[1], 2 * LANES):
+        rc, rs = spread[:freq, at : at + LANES], spread[:freq, at + LANES : at + 2 * LANES]
+        ic, js = spread[freq:, at : at + LANES], spread[freq:, at + LANES : at + 2 * LANES]
+        if at:
+            rc, rs, ic, js = fold(rc), fold(rs), fold(ic), fold(js)
+        outs.append((rc + js, ic - rs) if sign > 0 else (rc - js, ic + rs))
+    return [jnp.concatenate([out[k] for out in outs], 0) for k in range(2)]
 
 
 def batches(count, size, body):
@@ -133,66 +181,96 @@
     return pl.ds(first * period if isinstance(first, int) else pl.multiple_of(first * period, 16), count * period)
 
 
-def to_frequencies_z(read, count, size, table, terms):
-    period = terms.shape[1] // count
+def store_terms(terms, first, rows, values):
+    high, low = split(jnp.concatenate(values, 0), 2)
+    terms[0, rows_at(first, rows, len(values)), :] = high
+    terms[1, rows_at(first, rows, len(values)), :] = low
+
+
+def to_frequencies_y(read, count, size, to_y, terms, packed=False):
+    rows = terms.shape[1] // count
 
     def body(xs, first):
-        cells = jnp.concatenate([read(x) for x in xs], 0)
-        size_z = cells.shape[1]
-        if size_z % LANES == 0:
-            value = dot(jnp.concatenate([cells, cells], 1), table[...])
-        else:
-            value = dot(cells, table[:size_z]) + dot(cells, table[size_z:])
-        high, low = split(value, 2)
-        terms[0, rows_at(first, period, len(xs)), :] = high
-        terms[1, rows_at(first, period, len(xs)), :] = low
+        values = []
+        for k in range(0, len(xs), 2):
+            cells = [read(x) for x in xs[k : k + 2]]
+            width = cells[0].shape[1]
+            if width % LANES == 0:
+                cells = [jnp.concatenate(cells, 1)]
+            for part in cells:
+                spread = dot(to_y[...], jnp.concatenate([part, part], 0))
+                for at in range(0, spread.shape[1], width):
+                    value = spread[:, at : at + width]
+                    if packed:
+                        low_lanes = lax.broadcasted_iota(jnp.int32, (rows, LANES), 1) < LANES // 2
+                        value = jnp.where(low_lanes, value[:rows], value[rows:])
+                    values.append(value)
+        store_terms(terms, first, rows, values)
 
     batches(count, size, body)
 
 
-def to_frequencies_y(terms, size, to_y, real, imag):
-    count, period = real.shape[:2]
-
-    def body(xs, first):
-        spreads = []
-        for x in xs:
-            rows = rows_at(x, period, 1)
-            high, low = terms[0, rows, :], terms[1, rows, :]
-            spreads.append(dot(to_y[...], jnp.concatenate([high, low, high], 0)))
-        for x, spread in zip(xs, spreads):
-            real[x] = spread[:period, :LANES] + spread[period:, LANES:]
-            imag[x] = spread[:period, LANES:] - spread[period:, :LANES]
-
-    batches(count, size, body)
-
-
-def from_frequencies_y(real, imag, size, from_y, terms):
+def to_frequencies_z(terms, size, to_z, real, imag):
     count = real.shape[0]
-    rows = from_y.shape[0] // 2
-
-    def body(xs, first):
-        spreads = [
-            dot(from_y[...], stacked(jnp.concatenate([real[x], imag[x]], 1))) for x in xs
-        ]
-        for x, spread in zip(xs, spreads):
-            r = spread[:rows, :LANES] - spread[rows:, LANES:]
-            i = spread[rows:, :LANES] + spread[:rows, LANES:]
-            high, low = split(jnp.concatenate([r, i], 1), 2)
-            terms[0, rows_at(x, rows, 1), :] = high
-            terms[1, rows_at(x, rows, 1), :] = low
-
-    batches(count, size, body)
-
-
-def from_frequencies_z(terms, count, size, from_z, write):
     rows = terms.shape[1] // count
 
     def body(xs, first):
         span = rows_at(first, rows, len(xs))
         high, low = terms[0, span, :], terms[1, span, :]
-        value = dot(jnp.concatenate([high, low, high], 1), from_z[...])
+        width = high.shape[1]
+        if width % LANES == 0:
+            spread = dot(jnp.concatenate([high, low, high], 1), to_z[...])
+        else:
+            spread = dot(high, to_z[:width]) + dot(low, to_z[width : 2 * width])
+            spread = spread + dot(high, to_z[2 * width :])
         for k, x in enumerate(xs):
-            write(x, value[k * rows : (k + 1) * rows])
+            real[x], imag[x] = joined(spread[k * rows : (k + 1) * rows], 1)
+
+    batches(count, size, body)
+
+
+def from_frequencies_z(real, imag, size, from_z, terms):
+    count = real.shape[0]
+    rows = terms.shape[1] // count
+    freq = rows // 2
+
+    def body(xs, first):
+        lines = []
+        for x in xs:
+            for ref in (real, imag):
+                value = ref[x]
+                main = value[:freq]
+                if value.shape[0] > freq:
+                    main = jnp.concatenate([main, unfold(value[freq:], freq // 8)], 1)
+                lines.append(main)
+        spread = dot(side_by_side(jnp.concatenate(lines, 0)), from_z[...])
+        half = spread.shape[1] // 2
+        values = []
+        for k in range(len(xs)):
+            r = spread[k * rows : k * rows + freq]
+            i = spread[k * rows + freq : (k + 1) * rows]
+            values += [r[:, :half] - i[:, half:], r[:, half:] + i[:, :half]]
+        high, low = split(jnp.concatenate(values, 0), 2)
+        terms[0, rows_at(first, rows, len(xs)), :] = high
+        terms[1, rows_at(first, rows, len(xs)), :] = low
+
+    batches(count, size, body)
+
+
+def from_frequencies_y(terms, count, size, from_y, write):
+    rows = terms.shape[1] // count
+
+    def body(xs, first):
+        for k in range(0, len(xs), 2):
+            parts = []
+            for x in xs[k : k + 2]:
+                span = rows_at(x, rows, 1)
+                high, low = terms[0, span, :], terms[1, span, :]
+                parts.append(jnp.concatenate([high, low, high], 0))
+            value = dot(from_y[...], jnp.concatenate(parts, 1))
+            width = parts[0].shape[1]
+            for j, x in enumerate(xs[k : k + 2]):
+                write(x, value[:, j * width : (j + 1) * width])
 
     batches(count, size, body)
 
@@ -249,27 +327,31 @@
     return jnp.concatenate(split(value, 3), 0)
 
 
-def spectra_kernel(levels, *refs):
-    kernels, refs = refs[:levels], refs[levels:]
-    table, outs, (padded, mid) = refs[0], refs[1:-2], refs[-2:]
-    at = 0
-    taps = kernels[0].shape[0]
+def spectra_kernel(sizes, *refs):
+    kernels, table, outs, (padded, lines) = refs[0], refs[1], refs[2:-2], refs[-2:]
+    levels, taps = kernels.shape[:2]
     padded[...] = jnp.zeros(padded.shape, padded.dtype)
+    at_z = 0
     for level in range(levels):
         outs_here = outs[3 * level : 3 * level + 3]
-        period = outs_here[0].shape[1]
-        kernel_z = table[at : at + 2 * LANES, :]
-        kernel_y = table[at + 2 * LANES : at + 2 * LANES + 2 * period, : 3 * padded.shape[1]]
-        at += 2 * LANES + 2 * period
-        padded[:, :taps, :taps] = kernels[level][...].astype(F32)
-        cells = padded[...].astype(BF).reshape(taps * padded.shape[1], LANES)
-        mid[...] = dot(jnp.concatenate([cells, cells], 1), kernel_z)
-
-        def body(xs, first, kernel_y=kernel_y, outs=outs_here, period=period):
-            spreads = [dot(kernel_y, stacked(mid[rows_at(a, 16, 1), :])) for a in xs]
-            for a, spread in zip(xs, spreads):
-                real = spread[:period, :LANES] - spread[period:, LANES:]
-                imag = spread[:period, LANES:] + spread[period:, :LANES]
+        rows, columns, row, lane = sizes[level]
+        kernel_y = table[row : row + rows, lane : lane + 32]
+        kernel_z = table[:, at_z : at_z + columns]
+        at_z += columns
+        for at in (0, 16, 32):
+            padded[:, :taps, at : at + taps] = kernels[level].astype(F32)
+        cells = jnp.concatenate([padded[a].astype(BF) for a in range(taps)], 1)
+        spread = dot(kernel_y, jnp.concatenate([cells, cells], 0))
+        lane = lax.broadcasted_iota(jnp.int32, (rows, LANES), 1)
+        middle = (lane >= 16) & (lane < 32)
+        for a in range(taps):
+            high, low = (term.astype(F32) for term in split(spread[:, a * LANES : (a + 1) * LANES], 2))
+            lines[a * rows : (a + 1) * rows, :] = jnp.where(middle, low, high).astype(BF)
+
+        def body(xs, first, rows=rows, kernel_z=kernel_z, outs=outs_here):
+            spread = dot(lines[rows_at(first, rows, len(xs)), :], kernel_z)
+            for k, a in enumerate(xs):
+                real, imag = joined(spread[k * rows : (k + 1) * rows], -1)
                 outs[0][a] = real
                 outs[1][a] = imag - real
                 outs[2][a] = imag + real
@@ -347,11 +429,15 @@
             out[k] = coarse[first + k]
 
 
-def own_kernel(near, kr, kd, ks, to_z, to_y, out_real, out_imag, real, imag, ahead):
+def own_kernel(near, to_y, to_z, real, imag, ahead):
+    count = real.shape[0]
+    to_frequencies_y(lambda x: near[x], count, 8, to_y, ahead)
+    to_frequencies_z(ahead, 4, to_z, real, imag)
+
+
+def own_sum_kernel(real, imag, kr, kd, ks, out_real, out_imag):
     count = real.shape[0]
     half = kr.shape[0] // 2
-    to_frequencies_z(lambda x: near[x], count, 4, to_z, ahead)
-    to_frequencies_y(ahead, 4, to_y, real, imag)
     along_x(
         lambda x, rows: real[x - half, rows, :],
         lambda x, rows: imag[x - half, rows, :],
@@ -364,6 +450,7 @@
 
 
 def final_kernel(
+    t_columns,
     part_real,
     part_imag,
     next_a,
@@ -374,27 +461,26 @@
     kr,
     kd,
     ks,
+    to_y,
     to_z,
-    to_y,
+    from_z,
     from_y,
-    from_z,
     mr,
     md,
     ms,
-    m_low,
-    m_high,
     m_to_y,
+    m_to_z,
+    m_from_z,
     m_from_y,
-    m_from_z,
     tr,
     td,
     ts,
     t_down_y,
     t_down_z,
+    t_to_y,
     t_to_z,
-    t_to_y,
+    t_from_z,
     t_from_y,
-    t_from_z,
     out,
     side_real,
     side_imag,
@@ -423,7 +509,8 @@
     ended_x, close_x = left_x == 1, left_x <= 2
     ended_y = (lax.axis_index("gy") == lax.axis_size("gy") - 1).astype(jnp.int32)
     up_x, up_far = leads("gx", 1), leads("gx", 2)
-    count, width = part_real.shape[:2]
+    count = part_real.shape[0]
+    width = to_y.shape[1] // 2
     reach = side_real.shape[0] // 2
     top_rows = left_x * (count // 4) + reach
 
@@ -443,15 +530,12 @@
         read, first = (from_left, x) if x < reach else (from_right, x - reach)
         return read(slice(first * width, (first + 1) * width))
 
-    period = width
-    for first in range(0, 2 * reach, 4):
-        xs = list(range(first, min(2 * reach, first + 4)))
-        cells = jnp.concatenate([side_cells(x) for x in xs], 0)
-        value = dot(jnp.concatenate([cells, cells], 1), to_z[...])
-        high, low = split(value, 2)
-        ahead[0, rows_at(first, period, len(xs)), :] = high
-        ahead[1, rows_at(first, period, len(xs)), :] = low
-    to_frequencies_y(ahead, 7, to_y, side_real, side_imag)
+    for first in range(0, 2 * reach, 2):
+        xs = [first, first + 1]
+        cells = jnp.concatenate([side_cells(x) for x in xs], 1)
+        spread = dot(to_y[...], jnp.concatenate([cells, cells], 0))
+        store_terms(ahead, first, to_y.shape[0], [spread[:, :LANES], spread[:, LANES:]])
+    to_frequencies_z(ahead, 7, to_z, side_real, side_imag)
 
     def source(side):
         return lambda x, rows: side[x if x < reach else x - count, rows, :]
@@ -466,12 +550,12 @@
         lambda x: x < reach or x >= reach + count,
         (part_real, part_imag),
     )
-    from_frequencies_y(er, ei, 4, from_y, back)
+    from_frequencies_z(er, ei, 4, from_z, back)
 
     def fine_write(x, value):
         out[x] = value
 
-    from_frequencies_z(back, count, 4, from_z, fine_write)
+    from_frequencies_y(back, count, 8, from_y, fine_write)
 
     half = mid.shape[1]
     last = count // 2
@@ -505,26 +589,13 @@
         mid[k] = row
 
     skip = (mid.shape[0] - m_real.shape[0]) // 2
-    m_width = m_real.shape[1]
-    cut = half - m_width // 2
-
-    def mid_z(xs, first):
-        cells = jnp.concatenate([mid[x + skip] for x in xs], 0)
-        cells = jnp.concatenate([cells, cells], 1)
-        low, high = dot(cells, m_low[...]), dot(cells, m_high[...])
-        parts = []
-        for k in range(len(xs)):
-            parts += [low[k * half + cut : (k + 1) * half], high[k * half : (k + 1) * half - cut]]
-        high, low = split(jnp.concatenate(parts, 0), 2)
-        m_ahead[0, rows_at(first, m_width, len(xs)), :] = high
-        m_ahead[1, rows_at(first, m_width, len(xs)), :] = low
-
-    batches(m_real.shape[0], 9, mid_z)
-    to_frequencies_y(m_ahead, 9, m_to_y, m_real, m_imag)
-
-    t_width = t_real.shape[1]
+    to_frequencies_y(lambda x: mid[x + skip], m_real.shape[0], 9, m_to_y, m_ahead, True)
+    to_frequencies_z(m_ahead, 9, m_to_z, m_real, m_imag)
+
+    t_width = t_cells.shape[1]
+    spare = (t_width - t_columns) // 2
     inside = lax.broadcasted_iota(jnp.int32, (t_width, t_cells.shape[2]), 0)
-    inside = inside < jnp.where(ended_y == 1, t_width - (t_width - last_columns(t_width, m_width)) // 2, t_width)
+    inside = inside < jnp.where(ended_y == 1, t_width - spare, t_width)
 
     def top_cells(xs, first):
         spreads = []
@@ -539,8 +610,8 @@
             t_cells[t] = jnp.where(t < top_rows, row, 0.0).astype(BF)
 
     batches(t_real.shape[0], 7, top_cells)
-    to_frequencies_z(lambda x: t_cells[x], t_real.shape[0], 7, t_to_z, t_ahead)
-    to_frequencies_y(t_ahead, 7, t_to_y, t_real, t_imag)
+    to_frequencies_y(lambda x: t_cells[x], t_real.shape[0], 7, t_to_y, t_ahead)
+    to_frequencies_z(t_ahead, 7, t_to_z, t_real, t_imag)
 
     def plain(ref):
         return lambda x, rows: ref[x, rows, :]
@@ -554,10 +625,10 @@
     def mid_write(x, value):
         m_out[x] = value
 
-    from_frequencies_y(t_er, t_ei, 7, t_from_y.at[ended_y], t_back)
-    from_frequencies_y(m_er, m_ei, 7, m_from_y.at[ended_y], m_back)
-    from_frequencies_z(t_back, t_out.shape[0], 7, t_from_z, top_write)
-    from_frequencies_z(m_back, m_out.shape[0], 7, m_from_z, mid_write)
+    from_frequencies_z(t_er, t_ei, 7, t_from_z, t_back)
+    from_frequencies_z(m_er, m_ei, 7, m_from_z, m_back)
+    from_frequencies_y(t_back, t_out.shape[0], 7, t_from_y.at[ended_y], top_write)
+    from_frequencies_y(m_back, m_out.shape[0], 7, m_from_y.at[ended_y], mid_write)
     keep = jnp.where(ended_x, 0.0, 1.0)
     top = t_out.shape[0] - 1
     t_out[top] = t_out[top] * keep
@@ -571,10 +642,6 @@
         out[2 * i + 1] += 0.5 * (m_out[i] + m_out[i + 1])
 
     rows_loop(count // 2, 2, finish)
-
-
-def last_columns(t_width, m_width):
-    return m_width - t_width
 
 
 def call(kernel, outs, scratch, args, mib, loose=()):
@@ -591,14 +658,14 @@
     )(*args)
 
 
-def level_scratch(level, ny, nz, extra=()):
+def level_scratch(level, ny, nz, lanes, extra=()):
     rows = [
-        (F32, (count, level.period_y, LANES))
+        (F32, (count, level.rows, LANES))
         for count in (level.in_x, level.in_x, level.out_x, level.out_x)
     ]
     terms = [
-        (BF, (2, level.in_x * level.period_y, 2 * LANES)),
-        (BF, (2, level.out_x * ny, 2 * LANES)),
+        (BF, (2, level.in_x * 2 * level.freq, lanes)),
+        (BF, (2, level.out_x * 2 * level.freq, nz)),
     ]
     return [*rows, *extra, *terms, (F32, (level.out_x, ny, nz))]
 
@@ -617,19 +684,20 @@
     return outs
 
 
-def shards(charges, kernel_fine, kernel_mid, kernel_top):
+def block(charges, kernel_fine, kernel_mid, kernel_top):
     nx, ny, nz = charges.shape
     taps = kernel_fine.shape[0]
     half = taps // 2
     wide = half + 1
 
     ident = np.eye(ny)
-    fine = Level(taps, nx, ny, wide, ny + 2 * wide, nz, ident, ident, np.eye(nz))
+    width = ny + 2 * wide
+    fine = Level(taps, nx, ny, wide, width, nz, ident, ident, np.eye(nz))
     my, mz = ny // 2, nz // 2
     to_fine = up(my)
     ended = np.diag([1.0] * my + [0.0])
     mid = Level(
-        taps, nx // 2 + 1, my + 1, wide, my + 2 * wide, mz, to_fine, to_fine @ ended, up_closed(mz)
+        taps, nx // 2 + 1, my + 1, ny // 4, ny, mz, to_fine, to_fine @ ended, up_closed(mz)
     )
     ty, tz = my // 2, mz // 2
     to_mid = np.concatenate([up(ty), np.eye(ty + 1)[-1:]], 0)
@@ -648,19 +716,23 @@
 
     levels = (fine, mid, top)
     outs = [
-        jax.ShapeDtypeStruct((taps, level.period_y, LANES), F32)
+        jax.ShapeDtypeStruct((taps, level.rows, LANES), F32)
         for level in levels
         for _ in range(3)
     ]
-    tables = []
-    for level in levels:
-        tables.append(level.kernel_z)
-        tables.append(np.pad(level.kernel_y, ((0, 0), (0, 2 * LANES - level.kernel_y.shape[1]))))
+    table = np.concatenate([level.kernel_z for level in levels], 1)
+    sizes = []
+    for level, other in ((fine, None), (mid, None), (top, mid)):
+        rows, columns = level.kernel_y.shape[0], level.kernel_z.shape[1]
+        row, lane = 48 + (other.kernel_y.shape[0] if other else 0), 0 if level is fine else LANES
+        assert row + rows <= LANES
+        table[row : row + rows, lane : lane + 32] = level.kernel_y
+        sizes.append((rows, columns, row, lane))
     spectra = call(
-        functools.partial(spectra_kernel, 3),
+        functools.partial(spectra_kernel, sizes),
         outs,
-        [(F32, (taps, 16, LANES)), (F32, (taps * 16, 2 * LANES))],
-        [kernel_fine, kernel_mid, kernel_top, np.concatenate(tables, 0)],
+        [(F32, (taps, 16, LANES)), (BF, (taps * 2 * fine.freq, LANES))],
+        [jnp.stack([kernel_fine, kernel_mid, kernel_top]), table],
         8,
     )
 
@@ -685,10 +757,10 @@
     reach = 2 * half + 1 - mx
     assert 0 < reach <= mx - 1 and 2 * mz == LANES == nz
     shapes = [
-        (nx, fine.period_y, LANES),
+        (nx, width, LANES),
         (lines, packed, LANES),
-        (half * fine.period_y + lines * packed, LANES),
-        (half * fine.period_y + lines * packed, LANES),
+        (half * width + lines * packed, LANES),
+        (half * width + lines * packed, LANES),
         (reach + 3, packed, LANES),
         (reach + 3, packed, LANES),
     ]
@@ -707,16 +779,18 @@
         8,
         loose=(5,),
     )
+    far_a, far_b = swapped(far_a, far_b, "gx", 2)
     next_a, next_b = swapped(next_a, next_b, "gx", 1)
-    far_a, far_b = swapped(far_a, far_b, "gx", 2)
-
+
+    spectrum = [jax.ShapeDtypeStruct((nx, fine.rows, LANES), F32)] * 2
     own = call(
         own_kernel,
-        [jax.ShapeDtypeStruct((nx, fine.period_y, LANES), F32)] * 2,
-        [(F32, (nx, fine.period_y, LANES))] * 2 + [(BF, (2, nx * fine.period_y, 2 * LANES))],
-        [near, *spectra[:3], fine.to_z, fine.to_y],
-        12,
-    )
+        spectrum,
+        [(BF, (2, nx * 2 * fine.freq, nz))],
+        [near, fine.to_y, fine.to_z],
+        10,
+    )
+    own = call(own_sum_kernel, spectrum, [], [*own, *spectra[:3]], 8)
 
     wide_top = ty + 2 * wide
     t_down_y = down(wide_top, 0, 2 * packed)
@@ -725,18 +799,18 @@
         [np.tile(table, (3, 1)) for table in both_sides(down(tz, 0, mz).T)], 0
     )
     return call(
-        final_kernel,
+        functools.partial(final_kernel, ty),
         jax.ShapeDtypeStruct((nx, ny, nz), F32),
         [
-            (F32, (2 * half, fine.period_y, LANES)),
-            (F32, (2 * half, fine.period_y, LANES)),
-            (F32, (nx, fine.period_y, LANES)),
-            (F32, (nx, fine.period_y, LANES)),
-            (BF, (2, 2 * half * fine.period_y, 2 * LANES)),
-            (BF, (2, nx * ny, 2 * LANES)),
+            (F32, (2 * half, fine.rows, LANES)),
+            (F32, (2 * half, fine.rows, LANES)),
+            (F32, (nx, fine.rows, LANES)),
+            (F32, (nx, fine.rows, LANES)),
+            (BF, (2, 2 * half * 2 * fine.freq, nz)),
+            (BF, (2, nx * 2 * fine.freq, nz)),
             (BF, (3 * mx + 1 + 2 * reach, packed, LANES)),
-            *level_scratch(mid, ny, nz),
-            *level_scratch(top, ny, nz, [(BF, (top.in_x, top.period_y, tz))]),
+            *level_scratch(mid, ny, nz, LANES),
+            *level_scratch(top, ny, nz, tz, [(BF, (top.in_x, wide_top, tz))]),
         ],
         [
             *own,
@@ -746,22 +820,22 @@
             far_b,
             coarse,
             *spectra[:3],
+            fine.to_y,
             fine.to_z,
-            fine.to_y,
+            fine.from_z,
             fine.from_y[0],
-            fine.from_z,
             *spectra[3:6],
-            *mid.to_z_packed,
-            mid.to_y,
+            np.concatenate([np.concatenate(two(mid.table_y[:, at : at + packed]), 1) for at in (0, packed)], 0),
+            terms_below(np.tile(mid.table_z, (2, 1))),
+            mid.from_z,
             np.stack(mid.from_y),
-            mid.from_z,
             *spectra[6:],
             np.tile(t_down_y, (1, 3)).astype(BF),
             t_down_z.astype(BF),
+            top.to_y,
             top.to_z,
-            top.to_y,
+            top.from_z,
             np.stack(top.from_y),
-            top.from_z,
         ],
         26,
     )
@@ -770,5 +844,5 @@
 def solution(mesh):
     placed = (P("gx", "gy", None), P(), P(), P())
     return jax.shard_map(
-        shards, mesh=mesh, in_specs=placed, out_specs=P("gx", "gy", None), check_vma=False
-    )
+        block, mesh=mesh, in_specs=placed, out_specs=P("gx", "gy", None), check_vma=False
+    )

time: 40.4 us -> 36.4 us (0.901)
  the two profiles are of different devices: /device:TPU:8 before, /device:TPU:0 now
where the time goes in v6:
time: 36.4 us; the launch traced here: 36.1 us
  Pallas kernels  19.2 us (53%)
  starting transfers between devices  11.4 us (31%)
  waiting for transfers between devices  2.94 us (8%)
  local copies, waits for them, and re-layouts  1.38 us (4%)
  other arithmetic  0.88 us (2%)
    pallas_call x5, Pallas kernels, call(): pl.pallas_call(kernel, out_shape=outs, in_specs=[pl.BlockSpec(memory_spac...  19.2 us
    ppermute x6, starting transfers between devices, swapped(): outs.append(lax.ppermute(value, axis, pairs))  11.4 us
    ppermute x6, waiting for transfers between devices, swapped(): outs.append(lax.ppermute(value, axis, pairs))  2.94 us
    convert_element_type x1, local copies, waits for them, and re-layouts, block(): lax.dynamic_slice_in_dim(charges, jnp.where(flag, side, 0), side, 1)  1.26 us
    another operation x1, other arithmetic, block(): jnp.stack([kernel_fine, kernel_mid, kernel_top])  0.88 us
  transfers between devices with their start and end apart: 6, of which 2 were waited for; matrix products, arithmetic and copies ran while one was open for 2% of the time, Pallas kernels for 20%

profile of v6, /device:TPU:0, one launch (start us, length us, event | category | flops | bytes accessed | tf_op | source)
XLA Modules:
  0.0 36.1 jit_solution(13929612199682953007)
XLA Ops:
  0.0 1.3 %dynamic-slice_convert_fusion = (bf16[24,32,128]{2,1,0:T(8,128)(2,1)S(1)}, bf16[24,32,128]{2,1,0:T(8,128)(2,1)S(1)}) fusion(f32[24,64,128]{2,1,0:T(8,128)} %own.1, s32[]{:T(128)S(6)} %select_n.10, s32[]{:T(128)S(6)} %select_n.9), kind=kLoop, calls=%fused_computation | loop fusion | bytes 786440 | tf_op jit(solution)/shard_map/convert_element_type | solution.py:743
  1.3 0.0 copy-start.3
  1.3 0.8 %collective-permute-start.1 = (bf16[24,32,128]{2,1,0:T(8,128)(2,1)S(1)}, bf16[24,32,128]{2,1,0:T(8,128)(2,1)S(1)}, u32[]{:S(2)}, u32[]{:S(2)}) collective-permute-start(bf16[24,32,128]{2,1,0:T(8,128)(2,1)S(1)} %get-tuple-element.43), channel_id=1, source_target_pairs={{1,2},{2,1},{5,6},{6,5},{9,10},{10,9},{13,14},{14,13},{17,18},{18,... | collective-permute-start | bytes 589832 | tf_op jit(solution)/shard_map/ppermute | solution.py:683
  2.1 4.4 %collective-permute-start = (bf16[24,32,128]{2,1,0:T(8,128)(2,1)S(1)}, bf16[24,32,128]{2,1,0:T(8,128)(2,1)S(1)}, u32[]{:S(2)}, u32[]{:S(2)}) collective-permute-start(bf16[24,32,128]{2,1,0:T(8,128)(2,1)S(1)} %get-tuple-element.44), channel_id=1, source_target_pairs={{0,1},{2,3},{1,0},{3,2},{4,5},{6,7},{5,4},{7,6},{8,9},{10,11},{9,8... | collective-permute-start | bytes 589832 | tf_op jit(solution)/shard_map/ppermute | solution.py:683
  6.5 0.9 %pad_maximum_fusion.refs_0_ = bf16[3,15,15,15]{3,2,1,0:T(8,128)(2,1)S(1)} fusion(bf16[1,15,15,15]{3,2,1,0:T(8,128)(2,1)S(1)} %bitcast.3, bf16[1,15,15,15]{3,2,1,0:T(8,128)(2,1)S(1)} %bitcast.4, bf16[1,15,15,15]{3,2,1,0:T(8,128)(2,1)} %bitcast.5), kind=kLoop, calls=%fused_computation.2 | loop fusion | flops 20250 | bytes 40500 | tf_op jit(solution)/shard_map/stack | solution.py:735
  7.4 0.0 copy-start.10
  7.4 0.0 copy-start.14
  7.4 2.6 %shard_map.199 = (f32[15,48,128]{2,1,0:T(8,128)S(1)}, f32[15,48,128]{2,1,0:T(8,128)S(1)}, f32[15,48,128]{2,1,0:T(8,128)S(1)}, f32[15,24,128]{2,1,0:T(8,128)S(1)}...) custom-call(bf16[3,15,15,15]{3,2,1,0:T(8,128)(2,1)S(1)} %pad_maximum, ...), custom_call_target="tpu_custom_call" | custom-call | tf_op jit(solution)/shard_map/pallas_call | solution.py:649
  10.1 0.0 copy-start.1
  10.1 0.0 copy-start.8
  10.1 1.7 %shard_map.200 = (bf16[24,80,128]{2,1,0:T(8,128)(2,1)S(1)}, bf16[17,32,128]{2,1,0:T(8,128)(2,1)S(1)}, bf16[1104,128]{1,0:T(8,128)(2,1)S(1)}, bf16[1104,128]{1,0:...) custom-call(f32[24,64,128]{2,1,0:T(8,128)S(1)} %copy-done, ...), custom_call_target="tpu_custom_call" | custom-call | tf_op jit(solution)/shard_map/pallas_call | solution.py:649
  11.8 1.5 %collective-permute-start.2 = (bf16[1104,128]{1,0:T(8,128)(2,1)S(1)}, bf16[1104,128]{1,0:T(8,128)(2,1)S(1)}, u32[]{:S(2)}, u32[]{:S(2)}) collective-permute-start(bf16[1104,128]{1,0:T(8,128)(2,1)S(1)} %get-tuple-element.32), channel_id=1, source_target_pairs={{0,4},{8,12},{16,20},{24,28},{4,0},{12,8},{20,16},{28,24},{1,5},{9... | collective-permute-start | bytes 847880 | tf_op jit(solution)/shard_map/ppermute | solution.py:683
  13.4 0.7 %collective-permute-start.3 = (bf16[1104,128]{1,0:T(8,128)(2,1)S(1)}, bf16[1104,128]{1,0:T(8,128)(2,1)S(1)}, u32[]{:S(2)}, u32[]{:S(2)}) collective-permute-start(bf16[1104,128]{1,0:T(8,128)(2,1)S(1)} %get-tuple-element.33), channel_id=1, source_target_pairs={{4,8},{12,16},{20,24},{8,4},{16,12},{24,20},{5,9},{13,17},{21,25},... | collective-permute-start | bytes 847880 | tf_op jit(solution)/shard_map/ppermute | solution.py:683
  14.0 3.3 %collective-permute-start.4 = (bf16[6,32,128]{2,1,0:T(8,128)(2,1)S(1)}, bf16[6,32,128]{2,1,0:T(8,128)(2,1)S(1)}, u32[]{:S(2)}, u32[]{:S(2)}) collective-permute-start(bf16[6,32,128]{2,1,0:T(8,128)(2,1)S(1)} %get-tuple-element.34), channel_id=1, source_target_pairs={{0,8},{4,12},{16,24},{20,28},{8,0},{12,4},{24,16},{28,20},{1,9},{5... | collective-permute-start | bytes 147464 | tf_op jit(solution)/shard_map/ppermute | solution.py:683
  17.3 0.7 %collective-permute-start.5 = (bf16[6,32,128]{2,1,0:T(8,128)(2,1)S(1)}, bf16[6,32,128]{2,1,0:T(8,128)(2,1)S(1)}, u32[]{:S(2)}, u32[]{:S(2)}) collective-permute-start(bf16[6,32,128]{2,1,0:T(8,128)(2,1)S(1)} %get-tuple-element.35), channel_id=1, source_target_pairs={{8,16},{12,20},{16,8},{20,12},{9,17},{13,21},{17,9},{21,13},{10,18... | collective-permute-start | bytes 147464 | tf_op jit(solution)/shard_map/ppermute | solution.py:683
  18.0 2.6 %shard_map.201 = (f32[24,48,128]{2,1,0:T(8,128)S(1)}, f32[24,48,128]{2,1,0:T(8,128)S(1)}) custom-call(bf16[24,80,128]{2,1,0:T(8,128)(2,1)S(1)} %get-tuple-element.25.near, bf16[80,160]{1,0:T(8,128)(2,1)S(1)} %copy-done.8, bf16[384,512]{1,0:T(8,128)(2,1)S(1)} %copy-done.1), custom_call_target="tpu_custom_call" | custom-call | tf_op jit(solution)/shard_map/pallas_call | solution.py:649
  20.6 0.0 copy-start.2
  20.7 0.0 copy-start.4
  20.7 0.0 copy-start.5
  20.7 0.0 copy-start.6
  20.7 0.0 copy-start.7
  20.7 0.0 copy-start.9
  20.7 0.0 copy-start.11
  20.7 0.0 copy-start.12
  20.7 0.0 copy-start.13
  20.8 0.0 copy-start.15
  20.8 0.0 copy-start.17
  20.8 1.9 %shard_map.202 = (f32[24,48,128]{2,1,0:T(8,128)S(1)}, f32[24,48,128]{2,1,0:T(8,128)S(1)}) custom-call(f32[24,48,128]{2,1,0:T(8,128)S(1)} %get-tuple-element.26.real, f32[24,48,128]{2,1,0:T(8,128)S(1)} %get-tuple-element.27.imag, f32[15,48,128]{2,1,0:T(8,128)S(1)} %get-tuple-element.24.ordered.kr, f32[15,48,128]{2,1,0:T(8,128)S(1)} %get-tuple-element.28.kd, ...), custom_call_target="tpu_custom_call" | custom-call | tf_op jit(solution)/shard_map/pallas_call | solution.py:649
  22.7 0.0 copy-start.16
  22.7 2.0 %collective-permute-done.4.far_a = bf16[6,32,128]{2,1,0:T(8,128)(2,1)S(1)} collective-permute-done((bf16[6,32,128]{2,1,0:T(8,128)(2,1)S(1)}, bf16[6,32,128]{2,1,0:T(8,128)(2,1)S(1)}, u32[]{:S(2)}, u32[]{:S(2)}) %collective-permute-start.4) | collective-permute-done | bytes 49184 | tf_op jit(solution)/shard_map/ppermute | solution.py:683
  24.7 0.9 %collective-permute-done.2.next_a = bf16[1104,128]{1,0:T(8,128)(2,1)S(1)} collective-permute-done((bf16[1104,128]{1,0:T(8,128)(2,1)S(1)}, bf16[1104,128]{1,0:T(8,128)(2,1)S(1)}, u32[]{:S(2)}, u32[]{:S(2)}) %collective-permute-start.2) | collective-permute-done | bytes 282656 | tf_op jit(solution)/shard_map/ppermute | solution.py:683
  25.7 10.4 %shard_map.203 = f32[24,64,128]{2,1,0:T(8,128)} custom-call(f32[24,48,128]{2,1,0:T(8,128)S(1)} %get-tuple-element.30.part_real, f32[24,48,128]{2,1,0:T(8,128)S(1)} %get-tuple-element.31.part_imag, bf16[1104,128]{1,0:T(8,128)(2,1)S(1)} %collective-permute-done.2.next_a, bf16[1104,128]{1,0:T(8,128)(2,1)S(1)} %collective-permute-done.3.next_b, ...), custom_call_target="tpu_custom_call" | custom-call | tf_op jit(solution)/shard_map/pallas_call | solution.py:649
  (27 shorter events, 0.1 us)
Async XLA Ops:
  0.0 6.5 %copy-start.18 = (bf16[15,15,15]{2,1,0:T(8,128)(2,1)S(1)}, bf16[15,15,15]{2,1,0:T(8,128)(2,1)}, u32[]{:S(2)}) copy-start(bf16[15,15,15]{2,1,0:T(8,128)(2,1)} %param.24) | copy-start | bytes 20254
  0.0 6.5 %copy-start.19 = (bf16[15,15,15]{2,1,0:T(8,128)(2,1)S(1)}, bf16[15,15,15]{2,1,0:T(8,128)(2,1)}, u32[]{:S(2)}) copy-start(bf16[15,15,15]{2,1,0:T(8,128)(2,1)} %param.23) | copy-start | bytes 20254
  0.0 10.1 %copy-start = (f32[24,64,128]{2,1,0:T(8,128)S(1)}, f32[24,64,128]{2,1,0:T(8,128)}, u32[]{:S(2)}) copy-start(f32[24,64,128]{2,1,0:T(8,128)} %own.1) | copy-start | bytes 2359300
  1.3 6.1 %copy-start.3 = (bf16[128,1024]{1,0:T(8,128)(2,1)S(1)}, bf16[128,1024]{1,0:T(8,128)(2,1)}, u32[]{:S(2)}) copy-start(bf16[128,1024]{1,0:T(8,128)(2,1)} %constant.50.clone.refs_1_) | copy-start | bytes 786436
  1.3 8.8 %collective-permute-start.1 = (bf16[24,32,128]{2,1,0:T(8,128)(2,1)S(1)}, bf16[24,32,128]{2,1,0:T(8,128)(2,1)S(1)}, u32[]{:S(2)}, u32[]{:S(2)}) collective-permute-start(bf16[24,32,128]{2,1,0:T(8,128)(2,1)S(1)} %get-tuple-element.43), channel_id=1, source_target_pairs={{1,2},{2,1},{5,6},{6,5},{9,10},{10,9},{13,14},{14,13},{17,18},{18,... | collective-permute-start | bytes 589832 | tf_op jit(solution)/shard_map/ppermute | solution.py:683
  2.1 8.0 %collective-permute-start = (bf16[24,32,128]{2,1,0:T(8,128)(2,1)S(1)}, bf16[24,32,128]{2,1,0:T(8,128)(2,1)S(1)}, u32[]{:S(2)}, u32[]{:S(2)}) collective-permute-start(bf16[24,32,128]{2,1,0:T(8,128)(2,1)S(1)} %get-tuple-element.44), channel_id=1, source_target_pairs={{0,1},{2,3},{1,0},{3,2},{4,5},{6,7},{5,4},{7,6},{8,9},{10,11},{9,8... | collective-permute-start | bytes 589832 | tf_op jit(solution)/shard_map/ppermute | solution.py:683
  7.4 2.7 %copy-start.10 = (bf16[256,128]{1,0:T(8,128)(2,1)S(1)}, bf16[256,128]{1,0:T(8,128)(2,1)}, u32[]{:S(2)}) copy-start(bf16[256,128]{1,0:T(8,128)(2,1)} %constant.51.clone.down_z) | copy-start | bytes 196612
  7.4 2.7 %copy-start.14 = (bf16[64,240]{1,0:T(8,128)(2,1)S(1)}, bf16[64,240]{1,0:T(8,128)(2,1)}, u32[]{:S(2)}) copy-start(bf16[64,240]{1,0:T(8,128)(2,1)} %constant.52.clone.down_y) | copy-start | bytes 92164
  10.1 7.9 %copy-start.1 = (bf16[384,512]{1,0:T(8,128)(2,1)S(1)}, bf16[384,512]{1,0:T(8,128)(2,1)}, u32[]{:S(2)}) copy-start(bf16[384,512]{1,0:T(8,128)(2,1)} %constant.54.clone.to_z) | copy-start | bytes 1179652
  10.1 7.9 %copy-start.8 = (bf16[80,160]{1,0:T(8,128)(2,1)S(1)}, bf16[80,160]{1,0:T(8,128)(2,1)}, u32[]{:S(2)}) copy-start(bf16[80,160]{1,0:T(8,128)(2,1)} %constant.53.clone.to_y) | copy-start | bytes 76804
  11.8 13.8 %collective-permute-start.2 = (bf16[1104,128]{1,0:T(8,128)(2,1)S(1)}, bf16[1104,128]{1,0:T(8,128)(2,1)S(1)}, u32[]{:S(2)}, u32[]{:S(2)}) collective-permute-start(bf16[1104,128]{1,0:T(8,128)(2,1)S(1)} %get-tuple-element.32), channel_id=1, source_target_pairs={{0,4},{8,12},{16,20},{24,28},{4,0},{12,8},{20,16},{28,24},{1,5},{9... | collective-permute-start | bytes 847880 | tf_op jit(solution)/shard_map/ppermute | solution.py:683
  13.4 12.3 %collective-permute-start.3 = (bf16[1104,128]{1,0:T(8,128)(2,1)S(1)}, bf16[1104,128]{1,0:T(8,128)(2,1)S(1)}, u32[]{:S(2)}, u32[]{:S(2)}) collective-permute-start(bf16[1104,128]{1,0:T(8,128)(2,1)S(1)} %get-tuple-element.33), channel_id=1, source_target_pairs={{4,8},{12,16},{20,24},{8,4},{16,12},{24,20},{5,9},{13,17},{21,25},... | collective-permute-start | bytes 847880 | tf_op jit(solution)/shard_map/ppermute | solution.py:683
  14.0 10.7 %collective-permute-start.4 = (bf16[6,32,128]{2,1,0:T(8,128)(2,1)S(1)}, bf16[6,32,128]{2,1,0:T(8,128)(2,1)S(1)}, u32[]{:S(2)}, u32[]{:S(2)}) collective-permute-start(bf16[6,32,128]{2,1,0:T(8,128)(2,1)S(1)} %get-tuple-element.34), channel_id=1, source_target_pairs={{0,8},{4,12},{16,24},{20,28},{8,0},{12,4},{24,16},{28,20},{1,9},{5... | collective-permute-start | bytes 147464 | tf_op jit(solution)/shard_map/ppermute | solution.py:683
  17.3 7.4 %collective-permute-start.5 = (bf16[6,32,128]{2,1,0:T(8,128)(2,1)S(1)}, bf16[6,32,128]{2,1,0:T(8,128)(2,1)S(1)}, u32[]{:S(2)}, u32[]{:S(2)}) collective-permute-start(bf16[6,32,128]{2,1,0:T(8,128)(2,1)S(1)} %get-tuple-element.35), channel_id=1, source_target_pairs={{8,16},{12,20},{16,8},{20,12},{9,17},{13,21},{17,9},{21,13},{10,18... | collective-permute-start | bytes 147464 | tf_op jit(solution)/shard_map/ppermute | solution.py:683
  20.6 5.0 %copy-start.2 = (bf16[768,256]{1,0:T(8,128)(2,1)S(1)}, bf16[768,256]{1,0:T(8,128)(2,1)}, u32[]{:S(2)}) copy-start(bf16[768,256]{1,0:T(8,128)(2,1)} %constant.55.clone.from_z) | copy-start | bytes 1179652
  20.7 5.0 %copy-start.4 = (bf16[384,256]{1,0:T(8,128)(2,1)S(1)}, bf16[384,256]{1,0:T(8,128)(2,1)}, u32[]{:S(2)}) copy-start(bf16[384,256]{1,0:T(8,128)(2,1)} %constant.65.clone.t_from_z) | copy-start | bytes 589828
  20.7 5.0 %copy-start.5 = (bf16[768,32]{1,0:T(8,128)(2,1)S(1)}, bf16[768,32]{1,0:T(8,128)(2,1)}, u32[]{:S(2)}) copy-start(bf16[768,32]{1,0:T(8,128)(2,1)} %constant.62.clone.t_down_z) | copy-start | bytes 147460
  20.7 5.0 %copy-start.6 = (bf16[384,256]{1,0:T(8,128)(2,1)S(1)}, bf16[384,256]{1,0:T(8,128)(2,1)}, u32[]{:S(2)}) copy-start(bf16[384,256]{1,0:T(8,128)(2,1)} %constant.59.clone.m_from_z) | copy-start | bytes 589828
  20.7 5.0 %copy-start.7 = (bf16[384,256]{1,0:T(8,128)(2,1)S(1)}, bf16[384,256]{1,0:T(8,128)(2,1)}, u32[]{:S(2)}) copy-start(bf16[384,256]{1,0:T(8,128)(2,1)} %constant.58.clone.m_to_z) | copy-start | bytes 589828
  20.7 5.0 %copy-start.9 = (bf16[2,64,144]{2,1,0:T(8,128)(2,1)S(1)}, bf16[2,64,144]{2,1,0:T(8,128)(2,1)}, u32[]{:S(2)}) copy-start(bf16[2,64,144]{2,1,0:T(8,128)(2,1)} %constant.60.clone.m_from_y) | copy-start | bytes 110596
  20.7 5.0 %copy-start.11 = (bf16[96,256]{1,0:T(8,128)(2,1)S(1)}, bf16[96,256]{1,0:T(8,128)(2,1)}, u32[]{:S(2)}) copy-start(bf16[96,256]{1,0:T(8,128)(2,1)} %constant.64.clone.t_to_z) | copy-start | bytes 147460
  20.7 5.0 %copy-start.12 = (bf16[2,64,96]{2,1,0:T(8,128)(2,1)S(1)}, bf16[2,64,96]{2,1,0:T(8,128)(2,1)}, u32[]{:S(2)}) copy-start(bf16[2,64,96]{2,1,0:T(8,128)(2,1)} %constant.66.clone.t_from_y) | copy-start | bytes 73732
  20.7 5.0 %copy-start.13 = (bf16[64,240]{1,0:T(8,128)(2,1)S(1)}, bf16[64,240]{1,0:T(8,128)(2,1)}, u32[]{:S(2)}) copy-start(bf16[64,240]{1,0:T(8,128)(2,1)} %constant.56.clone.from_y) | copy-start | bytes 92164
  20.8 5.0 %copy-start.15 = (bf16[96,64]{1,0:T(8,128)(2,1)S(1)}, bf16[96,64]{1,0:T(8,128)(2,1)}, u32[]{:S(2)}) copy-start(bf16[96,64]{1,0:T(8,128)(2,1)} %constant.57.clone.m_to_y) | copy-start | bytes 36868
  20.8 5.0 %copy-start.17 = (bf16[32,64]{1,0:T(8,128)(2,1)S(1)}, bf16[32,64]{1,0:T(8,128)(2,1)}, u32[]{:S(2)}) copy-start(bf16[32,64]{1,0:T(8,128)(2,1)} %constant.63.clone.t_to_y) | copy-start | bytes 12292
  22.7 3.0 %copy-start.16 = (bf16[64,96]{1,0:T(8,128)(2,1)S(1)}, bf16[64,96]{1,0:T(8,128)(2,1)}, u32[]{:S(2)}) copy-start(bf16[64,96]{1,0:T(8,128)(2,1)} %constant.61.clone.t_down_y) | copy-start | bytes 36868

commit v7 on v6

--- a/solution.py
+++ b/solution.py
@@ -163,17 +163,7 @@
 
 
 def batches(count, size, body):
-    def trip(i, _):
-        first = i * size
-        body([first + k for k in range(size)], first)
-        return 0
-
-    whole = count // size
-    if whole > 1:
-        lax.fori_loop(0, whole, trip, 0)
-    else:
-        whole = 0
-    for first in range(whole * size, count, size):
+    for first in range(0, count, size):
         body(list(range(first, min(count, first + size))), first)
 
 

time: 36.4 us -> 31.1 us (0.85)
  Pallas kernels: 19.2 us -> 12 us
  waiting for transfers between devices: 2.94 us -> 4.87 us
    pallas_call x5, Pallas kernels: 19.2 us -> 12 us  [call(): pl.pallas_call(kernel, out_shape=outs, in_specs=[pl.BlockSpec(memory_spac...]
    ppermute x6, waiting for transfers between devices: 2.94 us -> 4.87 us  [swapped(): outs.append(lax.ppermute(value, axis, pairs))]
  transfers between devices with their start and end apart: 6 -> 6, of which waited for: 2 -> 2; matrix products, arithmetic and copies ran while one was open for 2% -> 3% of each run, Pallas kernels for 20% -> 14%
where the time goes in v7:
time: 31.1 us; the launch traced here: 30.9 us
  Pallas kernels  12 us (39%)
  starting transfers between devices  11.4 us (37%)
  waiting for transfers between devices  4.87 us (16%)
  local copies, waits for them, and re-layouts  1.38 us (4%)
  other arithmetic  0.88 us (3%)
  between operations  0.34 us (1%)
    pallas_call x5, Pallas kernels, call(): pl.pallas_call(kernel, out_shape=outs, in_specs=[pl.BlockSpec(memory_spac...  12 us
    ppermute x6, starting transfers between devices, swapped(): outs.append(lax.ppermute(value, axis, pairs))  11.4 us
    ppermute x6, waiting for transfers between devices, swapped(): outs.append(lax.ppermute(value, axis, pairs))  4.87 us
    convert_element_type x1, local copies, waits for them, and re-layouts, block(): lax.dynamic_slice_in_dim(charges, jnp.where(flag, side, 0), side, 1)  1.26 us
    another operation x1, other arithmetic, block(): jnp.stack([kernel_fine, kernel_mid, kernel_top])  0.88 us
  transfers between devices with their start and end apart: 6, of which 2 were waited for; matrix products, arithmetic and copies ran while one was open for 3% of the time, Pallas kernels for 14%

profile of v7, /device:TPU:0, one launch (start us, length us, event | category | flops | bytes accessed | tf_op | source)
XLA Modules:
  0.0 30.9 jit_solution(7188547229751768574)
XLA Ops:
  0.0 1.3 %dynamic-slice_convert_fusion = (bf16[24,32,128]{2,1,0:T(8,128)(2,1)S(1)}, bf16[24,32,128]{2,1,0:T(8,128)(2,1)S(1)}) fusion(f32[24,64,128]{2,1,0:T(8,128)} %own.1, s32[]{:T(128)S(6)} %select_n.10, s32[]{:T(128)S(6)} %select_n.9), kind=kLoop, calls=%fused_computation | loop fusion | bytes 786440 | tf_op jit(solution)/shard_map/convert_element_type | solution.py:733
  1.3 0.0 copy-start.3
  1.3 0.8 %collective-permute-start.1 = (bf16[24,32,128]{2,1,0:T(8,128)(2,1)S(1)}, bf16[24,32,128]{2,1,0:T(8,128)(2,1)S(1)}, u32[]{:S(2)}, u32[]{:S(2)}) collective-permute-start(bf16[24,32,128]{2,1,0:T(8,128)(2,1)S(1)} %get-tuple-element.43), channel_id=1, source_target_pairs={{1,2},{2,1},{5,6},{6,5},{9,10},{10,9},{13,14},{14,13},{17,18},{18,... | collective-permute-start | bytes 589832 | tf_op jit(solution)/shard_map/ppermute | solution.py:673
  2.1 4.4 %collective-permute-start = (bf16[24,32,128]{2,1,0:T(8,128)(2,1)S(1)}, bf16[24,32,128]{2,1,0:T(8,128)(2,1)S(1)}, u32[]{:S(2)}, u32[]{:S(2)}) collective-permute-start(bf16[24,32,128]{2,1,0:T(8,128)(2,1)S(1)} %get-tuple-element.44), channel_id=1, source_target_pairs={{0,1},{2,3},{1,0},{3,2},{4,5},{6,7},{5,4},{7,6},{8,9},{10,11},{9,8... | collective-permute-start | bytes 589832 | tf_op jit(solution)/shard_map/ppermute | solution.py:673
  6.5 0.9 %pad_maximum_fusion.refs_0_ = bf16[3,15,15,15]{3,2,1,0:T(8,128)(2,1)S(1)} fusion(bf16[1,15,15,15]{3,2,1,0:T(8,128)(2,1)S(1)} %bitcast.3, bf16[1,15,15,15]{3,2,1,0:T(8,128)(2,1)S(1)} %bitcast.4, bf16[1,15,15,15]{3,2,1,0:T(8,128)(2,1)} %bitcast.5), kind=kLoop, calls=%fused_computation.2 | loop fusion | flops 20250 | bytes 40500 | tf_op jit(solution)/shard_map/stack | solution.py:725
  7.4 0.0 copy-start.10
  7.4 0.0 copy-start.14
  7.4 1.1 %shard_map.199 = (f32[15,48,128]{2,1,0:T(8,128)S(1)}, f32[15,48,128]{2,1,0:T(8,128)S(1)}, f32[15,48,128]{2,1,0:T(8,128)S(1)}, f32[15,24,128]{2,1,0:T(8,128)S(1)}...) custom-call(bf16[3,15,15,15]{3,2,1,0:T(8,128)(2,1)S(1)} %pad_maximum, ...), custom_call_target="tpu_custom_call" | custom-call | tf_op jit(solution)/shard_map/pallas_call | solution.py:639
  8.6 0.0 copy-start.1
  8.6 0.0 copy-start.8
  8.6 0.9 %shard_map.200 = (bf16[24,80,128]{2,1,0:T(8,128)(2,1)S(1)}, bf16[17,32,128]{2,1,0:T(8,128)(2,1)S(1)}, bf16[1104,128]{1,0:T(8,128)(2,1)S(1)}, bf16[1104,128]{1,0:...) custom-call(f32[24,64,128]{2,1,0:T(8,128)S(1)} %copy-done, ...), custom_call_target="tpu_custom_call" | custom-call | tf_op jit(solution)/shard_map/pallas_call | solution.py:639
  9.5 1.6 %collective-permute-start.2 = (bf16[1104,128]{1,0:T(8,128)(2,1)S(1)}, bf16[1104,128]{1,0:T(8,128)(2,1)S(1)}, u32[]{:S(2)}, u32[]{:S(2)}) collective-permute-start(bf16[1104,128]{1,0:T(8,128)(2,1)S(1)} %get-tuple-element.32), channel_id=1, source_target_pairs={{0,4},{8,12},{16,20},{24,28},{4,0},{12,8},{20,16},{28,24},{1,5},{9... | collective-permute-start | bytes 847880 | tf_op jit(solution)/shard_map/ppermute | solution.py:673
  11.1 0.7 %collective-permute-start.3 = (bf16[1104,128]{1,0:T(8,128)(2,1)S(1)}, bf16[1104,128]{1,0:T(8,128)(2,1)S(1)}, u32[]{:S(2)}, u32[]{:S(2)}) collective-permute-start(bf16[1104,128]{1,0:T(8,128)(2,1)S(1)} %get-tuple-element.33), channel_id=1, source_target_pairs={{4,8},{12,16},{20,24},{8,4},{16,12},{24,20},{5,9},{13,17},{21,25},... | collective-permute-start | bytes 847880 | tf_op jit(solution)/shard_map/ppermute | solution.py:673
  11.7 3.3 %collective-permute-start.4 = (bf16[6,32,128]{2,1,0:T(8,128)(2,1)S(1)}, bf16[6,32,128]{2,1,0:T(8,128)(2,1)S(1)}, u32[]{:S(2)}, u32[]{:S(2)}) collective-permute-start(bf16[6,32,128]{2,1,0:T(8,128)(2,1)S(1)} %get-tuple-element.34), channel_id=1, source_target_pairs={{0,8},{4,12},{16,24},{20,28},{8,0},{12,4},{24,16},{28,20},{1,9},{5... | collective-permute-start | bytes 147464 | tf_op jit(solution)/shard_map/ppermute | solution.py:673
  15.0 0.7 %collective-permute-start.5 = (bf16[6,32,128]{2,1,0:T(8,128)(2,1)S(1)}, bf16[6,32,128]{2,1,0:T(8,128)(2,1)S(1)}, u32[]{:S(2)}, u32[]{:S(2)}) collective-permute-start(bf16[6,32,128]{2,1,0:T(8,128)(2,1)S(1)} %get-tuple-element.35), channel_id=1, source_target_pairs={{8,16},{12,20},{16,8},{20,12},{9,17},{13,21},{17,9},{21,13},{10,18... | collective-permute-start | bytes 147464 | tf_op jit(solution)/shard_map/ppermute | solution.py:673
  15.7 1.4 %shard_map.201 = (f32[24,48,128]{2,1,0:T(8,128)S(1)}, f32[24,48,128]{2,1,0:T(8,128)S(1)}) custom-call(bf16[24,80,128]{2,1,0:T(8,128)(2,1)S(1)} %get-tuple-element.25.near, bf16[80,160]{1,0:T(8,128)(2,1)S(1)} %copy-done.8, bf16[384,512]{1,0:T(8,128)(2,1)S(1)} %copy-done.1), custom_call_target="tpu_custom_call" | custom-call | tf_op jit(solution)/shard_map/pallas_call | solution.py:639
  17.1 0.0 copy-start.2
  17.1 0.0 copy-start.4
  17.1 0.0 copy-start.5
  17.1 0.0 copy-start.6
  17.2 0.0 copy-start.7
  17.2 0.0 copy-start.9
  17.2 0.0 copy-start.11
  17.2 0.0 copy-start.12
  17.2 0.0 copy-start.13
  17.2 0.0 copy-start.15
  17.2 0.0 copy-start.17
  17.2 1.9 %shard_map.202 = (f32[24,48,128]{2,1,0:T(8,128)S(1)}, f32[24,48,128]{2,1,0:T(8,128)S(1)}) custom-call(f32[24,48,128]{2,1,0:T(8,128)S(1)} %get-tuple-element.26.real, f32[24,48,128]{2,1,0:T(8,128)S(1)} %get-tuple-element.27.imag, f32[15,48,128]{2,1,0:T(8,128)S(1)} %get-tuple-element.24.ordered.kr, f32[15,48,128]{2,1,0:T(8,128)S(1)} %get-tuple-element.28.kd, ...), custom_call_target="tpu_custom_call" | custom-call | tf_op jit(solution)/shard_map/pallas_call | solution.py:639
  19.1 0.0 copy-start.16
  19.2 4.4 %collective-permute-done.4.far_a = bf16[6,32,128]{2,1,0:T(8,128)(2,1)S(1)} collective-permute-done((bf16[6,32,128]{2,1,0:T(8,128)(2,1)S(1)}, bf16[6,32,128]{2,1,0:T(8,128)(2,1)S(1)}, u32[]{:S(2)}, u32[]{:S(2)}) %collective-permute-start.4) | collective-permute-done | bytes 49184 | tf_op jit(solution)/shard_map/ppermute | solution.py:673
  23.6 0.4 %collective-permute-done.2.next_a = bf16[1104,128]{1,0:T(8,128)(2,1)S(1)} collective-permute-done((bf16[1104,128]{1,0:T(8,128)(2,1)S(1)}, bf16[1104,128]{1,0:T(8,128)(2,1)S(1)}, u32[]{:S(2)}, u32[]{:S(2)}) %collective-permute-start.2) | collective-permute-done | bytes 282656 | tf_op jit(solution)/shard_map/ppermute | solution.py:673
  24.1 6.7 %shard_map.203 = f32[24,64,128]{2,1,0:T(8,128)} custom-call(f32[24,48,128]{2,1,0:T(8,128)S(1)} %get-tuple-element.30.part_real, f32[24,48,128]{2,1,0:T(8,128)S(1)} %get-tuple-element.31.part_imag, bf16[1104,128]{1,0:T(8,128)(2,1)S(1)} %collective-permute-done.2.next_a, bf16[1104,128]{1,0:T(8,128)(2,1)S(1)} %collective-permute-done.3.next_b, ...), custom_call_target="tpu_custom_call" | custom-call | tf_op jit(solution)/shard_map/pallas_call | solution.py:639
  (27 shorter events, 0.1 us)
Async XLA Ops:
  0.0 6.5 %copy-start.18 = (bf16[15,15,15]{2,1,0:T(8,128)(2,1)S(1)}, bf16[15,15,15]{2,1,0:T(8,128)(2,1)}, u32[]{:S(2)}) copy-start(bf16[15,15,15]{2,1,0:T(8,128)(2,1)} %param.24) | copy-start | bytes 20254
  0.0 6.5 %copy-start.19 = (bf16[15,15,15]{2,1,0:T(8,128)(2,1)S(1)}, bf16[15,15,15]{2,1,0:T(8,128)(2,1)}, u32[]{:S(2)}) copy-start(bf16[15,15,15]{2,1,0:T(8,128)(2,1)} %param.23) | copy-start | bytes 20254
  0.0 8.6 %copy-start = (f32[24,64,128]{2,1,0:T(8,128)S(1)}, f32[24,64,128]{2,1,0:T(8,128)}, u32[]{:S(2)}) copy-start(f32[24,64,128]{2,1,0:T(8,128)} %own.1) | copy-start | bytes 2359300
  1.3 6.1 %copy-start.3 = (bf16[128,1024]{1,0:T(8,128)(2,1)S(1)}, bf16[128,1024]{1,0:T(8,128)(2,1)}, u32[]{:S(2)}) copy-start(bf16[128,1024]{1,0:T(8,128)(2,1)} %constant.50.clone.refs_1_) | copy-start | bytes 786436
  1.3 7.3 %collective-permute-start.1 = (bf16[24,32,128]{2,1,0:T(8,128)(2,1)S(1)}, bf16[24,32,128]{2,1,0:T(8,128)(2,1)S(1)}, u32[]{:S(2)}, u32[]{:S(2)}) collective-permute-start(bf16[24,32,128]{2,1,0:T(8,128)(2,1)S(1)} %get-tuple-element.43), channel_id=1, source_target_pairs={{1,2},{2,1},{5,6},{6,5},{9,10},{10,9},{13,14},{14,13},{17,18},{18,... | collective-permute-start | bytes 589832 | tf_op jit(solution)/shard_map/ppermute | solution.py:673
  2.1 6.5 %collective-permute-start = (bf16[24,32,128]{2,1,0:T(8,128)(2,1)S(1)}, bf16[24,32,128]{2,1,0:T(8,128)(2,1)S(1)}, u32[]{:S(2)}, u32[]{:S(2)}) collective-permute-start(bf16[24,32,128]{2,1,0:T(8,128)(2,1)S(1)} %get-tuple-element.44), channel_id=1, source_target_pairs={{0,1},{2,3},{1,0},{3,2},{4,5},{6,7},{5,4},{7,6},{8,9},{10,11},{9,8... | collective-permute-start | bytes 589832 | tf_op jit(solution)/shard_map/ppermute | solution.py:673
  7.4 1.2 %copy-start.10 = (bf16[256,128]{1,0:T(8,128)(2,1)S(1)}, bf16[256,128]{1,0:T(8,128)(2,1)}, u32[]{:S(2)}) copy-start(bf16[256,128]{1,0:T(8,128)(2,1)} %constant.51.clone.down_z) | copy-start | bytes 196612
  7.4 1.2 %copy-start.14 = (bf16[64,240]{1,0:T(8,128)(2,1)S(1)}, bf16[64,240]{1,0:T(8,128)(2,1)}, u32[]{:S(2)}) copy-start(bf16[64,240]{1,0:T(8,128)(2,1)} %constant.52.clone.down_y) | copy-start | bytes 92164
  8.6 7.1 %copy-start.1 = (bf16[384,512]{1,0:T(8,128)(2,1)S(1)}, bf16[384,512]{1,0:T(8,128)(2,1)}, u32[]{:S(2)}) copy-start(bf16[384,512]{1,0:T(8,128)(2,1)} %constant.54.clone.to_z) | copy-start | bytes 1179652
  8.6 7.1 %copy-start.8 = (bf16[80,160]{1,0:T(8,128)(2,1)S(1)}, bf16[80,160]{1,0:T(8,128)(2,1)}, u32[]{:S(2)}) copy-start(bf16[80,160]{1,0:T(8,128)(2,1)} %constant.53.clone.to_y) | copy-start | bytes 76804
  9.5 14.5 %collective-permute-start.2 = (bf16[1104,128]{1,0:T(8,128)(2,1)S(1)}, bf16[1104,128]{1,0:T(8,128)(2,1)S(1)}, u32[]{:S(2)}, u32[]{:S(2)}) collective-permute-start(bf16[1104,128]{1,0:T(8,128)(2,1)S(1)} %get-tuple-element.32), channel_id=1, source_target_pairs={{0,4},{8,12},{16,20},{24,28},{4,0},{12,8},{20,16},{28,24},{1,5},{9... | collective-permute-start | bytes 847880 | tf_op jit(solution)/shard_map/ppermute | solution.py:673
  11.1 13.0 %collective-permute-start.3 = (bf16[1104,128]{1,0:T(8,128)(2,1)S(1)}, bf16[1104,128]{1,0:T(8,128)(2,1)S(1)}, u32[]{:S(2)}, u32[]{:S(2)}) collective-permute-start(bf16[1104,128]{1,0:T(8,128)(2,1)S(1)} %get-tuple-element.33), channel_id=1, source_target_pairs={{4,8},{12,16},{20,24},{8,4},{16,12},{24,20},{5,9},{13,17},{21,25},... | collective-permute-start | bytes 847880 | tf_op jit(solution)/shard_map/ppermute | solution.py:673
  11.7 11.8 %collective-permute-start.4 = (bf16[6,32,128]{2,1,0:T(8,128)(2,1)S(1)}, bf16[6,32,128]{2,1,0:T(8,128)(2,1)S(1)}, u32[]{:S(2)}, u32[]{:S(2)}) collective-permute-start(bf16[6,32,128]{2,1,0:T(8,128)(2,1)S(1)} %get-tuple-element.34), channel_id=1, source_target_pairs={{0,8},{4,12},{16,24},{20,28},{8,0},{12,4},{24,16},{28,20},{1,9},{5... | collective-permute-start | bytes 147464 | tf_op jit(solution)/shard_map/ppermute | solution.py:673
  15.0 8.6 %collective-permute-start.5 = (bf16[6,32,128]{2,1,0:T(8,128)(2,1)S(1)}, bf16[6,32,128]{2,1,0:T(8,128)(2,1)S(1)}, u32[]{:S(2)}, u32[]{:S(2)}) collective-permute-start(bf16[6,32,128]{2,1,0:T(8,128)(2,1)S(1)} %get-tuple-element.35), channel_id=1, source_target_pairs={{8,16},{12,20},{16,8},{20,12},{9,17},{13,21},{17,9},{21,13},{10,18... | collective-permute-start | bytes 147464 | tf_op jit(solution)/shard_map/ppermute | solution.py:673
  17.1 6.9 %copy-start.2 = (bf16[768,256]{1,0:T(8,128)(2,1)S(1)}, bf16[768,256]{1,0:T(8,128)(2,1)}, u32[]{:S(2)}) copy-start(bf16[768,256]{1,0:T(8,128)(2,1)} %constant.55.clone.from_z) | copy-start | bytes 1179652
  17.1 6.9 %copy-start.4 = (bf16[384,256]{1,0:T(8,128)(2,1)S(1)}, bf16[384,256]{1,0:T(8,128)(2,1)}, u32[]{:S(2)}) copy-start(bf16[384,256]{1,0:T(8,128)(2,1)} %constant.65.clone.t_from_z) | copy-start | bytes 589828
  17.1 6.9 %copy-start.5 = (bf16[768,32]{1,0:T(8,128)(2,1)S(1)}, bf16[768,32]{1,0:T(8,128)(2,1)}, u32[]{:S(2)}) copy-start(bf16[768,32]{1,0:T(8,128)(2,1)} %constant.62.clone.t_down_z) | copy-start | bytes 147460
  17.1 6.9 %copy-start.6 = (bf16[384,256]{1,0:T(8,128)(2,1)S(1)}, bf16[384,256]{1,0:T(8,128)(2,1)}, u32[]{:S(2)}) copy-start(bf16[384,256]{1,0:T(8,128)(2,1)} %constant.59.clone.m_from_z) | copy-start | bytes 589828
  17.2 6.9 %copy-start.7 = (bf16[384,256]{1,0:T(8,128)(2,1)S(1)}, bf16[384,256]{1,0:T(8,128)(2,1)}, u32[]{:S(2)}) copy-start(bf16[384,256]{1,0:T(8,128)(2,1)} %constant.58.clone.m_to_z) | copy-start | bytes 589828
  17.2 6.9 %copy-start.9 = (bf16[2,64,144]{2,1,0:T(8,128)(2,1)S(1)}, bf16[2,64,144]{2,1,0:T(8,128)(2,1)}, u32[]{:S(2)}) copy-start(bf16[2,64,144]{2,1,0:T(8,128)(2,1)} %constant.60.clone.m_from_y) | copy-start | bytes 110596
  17.2 6.9 %copy-start.11 = (bf16[96,256]{1,0:T(8,128)(2,1)S(1)}, bf16[96,256]{1,0:T(8,128)(2,1)}, u32[]{:S(2)}) copy-start(bf16[96,256]{1,0:T(8,128)(2,1)} %constant.64.clone.t_to_z) | copy-start | bytes 147460
  17.2 6.9 %copy-start.12 = (bf16[2,64,96]{2,1,0:T(8,128)(2,1)S(1)}, bf16[2,64,96]{2,1,0:T(8,128)(2,1)}, u32[]{:S(2)}) copy-start(bf16[2,64,96]{2,1,0:T(8,128)(2,1)} %constant.66.clone.t_from_y) | copy-start | bytes 73732
  17.2 6.9 %copy-start.13 = (bf16[64,240]{1,0:T(8,128)(2,1)S(1)}, bf16[64,240]{1,0:T(8,128)(2,1)}, u32[]{:S(2)}) copy-start(bf16[64,240]{1,0:T(8,128)(2,1)} %constant.56.clone.from_y) | copy-start | bytes 92164
  17.2 6.9 %copy-start.15 = (bf16[96,64]{1,0:T(8,128)(2,1)S(1)}, bf16[96,64]{1,0:T(8,128)(2,1)}, u32[]{:S(2)}) copy-start(bf16[96,64]{1,0:T(8,128)(2,1)} %constant.57.clone.m_to_y) | copy-start | bytes 36868
  17.2 6.9 %copy-start.17 = (bf16[32,64]{1,0:T(8,128)(2,1)S(1)}, bf16[32,64]{1,0:T(8,128)(2,1)}, u32[]{:S(2)}) copy-start(bf16[32,64]{1,0:T(8,128)(2,1)} %constant.63.clone.t_to_y) | copy-start | bytes 12292
  19.1 5.0 %copy-start.16 = (bf16[64,96]{1,0:T(8,128)(2,1)S(1)}, bf16[64,96]{1,0:T(8,128)(2,1)}, u32[]{:S(2)}) copy-start(bf16[64,96]{1,0:T(8,128)(2,1)} %constant.61.clone.t_down_y) | copy-start | bytes 36868

commit v8 on v7

--- a/solution.py
+++ b/solution.py
@@ -11,6 +11,9 @@
 BF = jnp.bfloat16
 F32 = jnp.float32
 LANES = 128
+BLOCK = 8
+PARTS = 2
+TERMS = 3
 
 
 def two(matrix):
@@ -265,38 +268,36 @@
     batches(count, size, body)
 
 
-def along_x(real, imag, spectrum, out_real, out_imag, block, taken=None, before=None):
+def along_x(real, imag, spectrum, out_real, out_imag, block, outputs=None, taken=None, before=None):
     kernel_r, kernel_d, kernel_s = spectrum
     taps, period = kernel_r.shape[:2]
-    out_x = out_real.shape[0]
+    outputs = outputs or list(range(out_real.shape[0]))
     taken = taken or (lambda x: True)
 
     def body(part, _):
         rows = pl.ds(pl.multiple_of(8 * part, 8), 8)
-        for start in range(0, out_x, block):
-            count = min(block, out_x - start)
-            sums = [[None] * 3 for _ in range(count)]
+        for start in range(0, len(outputs), block):
+            wanted = outputs[start : start + block]
+            sums = [[None] * 3 for _ in wanted]
             seen = {}
             for a in range(taps):
-                used = [i for i in range(count) if taken(start + i + a)]
+                used = [i for i, out in enumerate(wanted) if taken(out + a)]
                 if used:
                     weights = kernel_r[a, rows, :], kernel_d[a, rows, :], kernel_s[a, rows, :]
                 for i in used:
-                    x = start + i + a
+                    x = wanted[i] + a
                     if x not in seen:
                         r, m = real(x, rows), imag(x, rows)
                         seen[x] = r + m, r, m
                     for k in range(3):
                         term = weights[k] * seen[x][k]
                         sums[i][k] = term if sums[i][k] is None else sums[i][k] + term
-            for i in range(count):
-                values = []
-                if sums[i][0] is not None:
-                    values.append((sums[i][0] - sums[i][2], sums[i][0] + sums[i][1]))
+            for i, out in enumerate(wanted):
+                value = sums[i][0] - sums[i][2], sums[i][0] + sums[i][1]
                 if before is not None:
-                    values.append((before[0][start + i, rows, :], before[1][start + i, rows, :]))
-                out_real[start + i, rows, :] = sum(value[0] for value in values)
-                out_imag[start + i, rows, :] = sum(value[1] for value in values)
+                    value = value[0] + before[0][out, rows, :], value[1] + before[1][out, rows, :]
+                out_real[start + i, rows, :] = value[0]
+                out_imag[start + i, rows, :] = value[1]
         return 0
 
     lax.fori_loop(0, period // 8, body, 0)
@@ -314,7 +315,7 @@
 
 
 def all_terms(value):
-    return jnp.concatenate(split(value, 3), 0)
+    return jnp.concatenate(split(value, TERMS), 0)
 
 
 def spectra_kernel(sizes, *refs):
@@ -397,13 +398,13 @@
         row = jnp.where(high_lanes, total[half:], total[:half])
         row = jnp.where(outside, 0.0, row)
         if i == 0:
-            for k, term in enumerate(split(row, 3)):
+            for k, term in enumerate(split(row, PARTS)):
                 coarse[k] = term
         elif i == last:
-            for k, term in enumerate(split(row, 3)):
-                coarse[last + 2 + k] = term
+            for k, term in enumerate(split(row, PARTS)):
+                coarse[last + PARTS - 1 + k] = term
         else:
-            coarse[i + 2] = row.astype(BF)
+            coarse[i + PARTS - 1] = row.astype(BF)
     lines = next_a.shape[0] - coarse.shape[0] * half
     tail = count - lines // width
     far_tail = coarse.shape[0] - far_a.shape[0]
@@ -425,7 +426,7 @@
     to_frequencies_z(ahead, 4, to_z, real, imag)
 
 
-def own_sum_kernel(real, imag, kr, kd, ks, out_real, out_imag):
+def own_sum_kernel(real, imag, kr, kd, ks, from_z, from_y, out_real, out_imag, whole, back):
     count = real.shape[0]
     half = kr.shape[0] // 2
     along_x(
@@ -434,15 +435,24 @@
         (kr, kd, ks),
         out_real,
         out_imag,
-        8,
+        BLOCK,
+        None,
         lambda x: half <= x < half + count,
     )
+    inner = slice(half, count - half)
+
+    def write(x, value):
+        whole[x] = value
+
+    from_frequencies_z(out_real.at[inner], out_imag.at[inner], 4, from_z, back)
+    from_frequencies_y(back, whole.shape[0], 8, from_y, write)
 
 
 def final_kernel(
     t_columns,
     part_real,
     part_imag,
+    whole,
     next_a,
     next_b,
     far_a,
@@ -530,22 +540,26 @@
     def source(side):
         return lambda x, rows: side[x if x < reach else x - count, rows, :]
 
+    edges = list(range(reach)) + list(range(count - reach, count))
     along_x(
         source(side_real),
         source(side_imag),
         (kr, kd, ks),
         er,
         ei,
-        8,
+        reach,
+        edges,
         lambda x: x < reach or x >= reach + count,
         (part_real, part_imag),
     )
     from_frequencies_z(er, ei, 4, from_z, back)
 
     def fine_write(x, value):
-        out[x] = value
-
-    from_frequencies_y(back, count, 8, from_y, fine_write)
+        out[edges[x]] = value
+
+    from_frequencies_y(back, len(edges), 8, from_y, fine_write)
+    for x in range(whole.shape[0]):
+        out[reach + x] = whole[x]
 
     half = mid.shape[1]
     last = count // 2
@@ -558,23 +572,23 @@
         return from_right(slice(lines + k * half, lines + (k + 1) * half))
 
     def added(first, second, dropped=None):
-        value = sum(first(2 - k).astype(F32) for k in range(3))
-        value = value + sum(second(last + 4 - k).astype(F32) for k in range(3))
+        value = sum(first(PARTS - 1 - k).astype(F32) for k in range(PARTS))
+        value = value + sum(second(last + 2 * PARTS - 2 - k).astype(F32) for k in range(PARTS))
         if dropped is not None:
             value = jnp.where(dropped, 0.0, value)
         return value.astype(BF)
 
-    spare = far_a.shape[0] - 3
+    spare = far_a.shape[0] - PARTS
     far_first = coarse.shape[0] - far_a.shape[0]
     rows = [far_left(k) for k in range(spare)]
     rows += [added(left_row, lambda k: far_left(k - far_first))]
-    rows += [left_row(k) for k in range(3, last + 2)]
+    rows += [left_row(k) for k in range(PARTS, last - 1 + PARTS)]
     rows += [added(lambda k: coarse[k], left_row)]
-    rows += [coarse[k] for k in range(3, last + 2)]
+    rows += [coarse[k] for k in range(PARTS, last - 1 + PARTS)]
     rows += [added(right_row, lambda k: coarse[k], ended_x)]
-    rows += [right_row(k) for k in range(3, last + 2)]
+    rows += [right_row(k) for k in range(PARTS, last - 1 + PARTS)]
     rows += [added(far_right, right_row, close_x)]
-    rows += [far_right(k) for k in range(3, 3 + spare)]
+    rows += [far_right(k) for k in range(PARTS, PARTS + spare)]
     for k, row in enumerate(rows):
         mid[k] = row
 
@@ -594,7 +608,7 @@
             spreads.append(dot(t_down_y[...], all_terms(total)))
         low = jnp.concatenate([spread[:t_width] for spread in spreads], 0)
         high = jnp.concatenate([spread[t_width:] for spread in spreads], 0)
-        value = dot(jnp.concatenate(split(low, 3) + split(high, 3), 1), t_down_z[...])
+        value = dot(jnp.concatenate(split(low, TERMS) + split(high, TERMS), 1), t_down_z[...])
         for k, t in enumerate(xs):
             row = jnp.where(inside, value[k * t_width : (k + 1) * t_width], 0.0)
             t_cells[t] = jnp.where(t < top_rows, row, 0.0).astype(BF)
@@ -743,7 +757,7 @@
     shift = ny + 2 * side - window
     down_y = np.concatenate([down(packed, 0, window), down(packed, 2 * packed - shift, window)], 0)
     mx = nx // 2
-    lines = mx - 1 + 6
+    lines = mx - 1 + 2 * PARTS
     reach = 2 * half + 1 - mx
     assert 0 < reach <= mx - 1 and 2 * mz == LANES == nz
     shapes = [
@@ -751,8 +765,8 @@
         (lines, packed, LANES),
         (half * width + lines * packed, LANES),
         (half * width + lines * packed, LANES),
-        (reach + 3, packed, LANES),
-        (reach + 3, packed, LANES),
+        (reach + PARTS, packed, LANES),
+        (reach + PARTS, packed, LANES),
     ]
     near, coarse, next_a, next_b, far_a, far_b = call(
         pack_kernel,
@@ -763,7 +777,7 @@
             got_a,
             got_b,
             down_z.astype(BF),
-            np.tile(down_y, (1, 3)).astype(BF),
+            np.tile(down_y, (1, TERMS)).astype(BF),
             spectra[0],
         ],
         8,
@@ -780,13 +794,20 @@
         [near, fine.to_y, fine.to_z],
         10,
     )
-    own = call(own_sum_kernel, spectrum, [], [*own, *spectra[:3]], 8)
+    inner = nx - 2 * half
+    own = call(
+        own_sum_kernel,
+        [*spectrum, jax.ShapeDtypeStruct((inner, ny, nz), F32)],
+        [(BF, (2, inner * 2 * fine.freq, nz))],
+        [*own, *spectra[:3], fine.from_z, fine.from_y[0]],
+        10,
+    )
 
     wide_top = ty + 2 * wide
     t_down_y = down(wide_top, 0, 2 * packed)
     t_down_y = np.concatenate([t_down_y[:, :packed], t_down_y[:, packed:]], 0)
     t_down_z = np.concatenate(
-        [np.tile(table, (3, 1)) for table in both_sides(down(tz, 0, mz).T)], 0
+        [np.tile(table, (TERMS, 1)) for table in both_sides(down(tz, 0, mz).T)], 0
     )
     return call(
         functools.partial(final_kernel, ty),
@@ -794,10 +815,10 @@
         [
             (F32, (2 * half, fine.rows, LANES)),
             (F32, (2 * half, fine.rows, LANES)),
-            (F32, (nx, fine.rows, LANES)),
-            (F32, (nx, fine.rows, LANES)),
+            (F32, (2 * half, fine.rows, LANES)),
+            (F32, (2 * half, fine.rows, LANES)),
             (BF, (2, 2 * half * 2 * fine.freq, nz)),
-            (BF, (2, nx * 2 * fine.freq, nz)),
+            (BF, (2, 2 * half * 2 * fine.freq, nz)),
             (BF, (3 * mx + 1 + 2 * reach, packed, LANES)),
             *level_scratch(mid, ny, nz, LANES),
             *level_scratch(top, ny, nz, tz, [(BF, (top.in_x, wide_top, tz))]),
@@ -820,7 +841,7 @@
             mid.from_z,
             np.stack(mid.from_y),
             *spectra[6:],
-            np.tile(t_down_y, (1, 3)).astype(BF),
+            np.tile(t_down_y, (1, TERMS)).astype(BF),
             t_down_z.astype(BF),
             top.to_y,
             top.to_z,

time: 31.1 us -> 30.1 us (0.968)
  waiting for transfers between devices: 4.87 us -> 3.5 us
  Pallas kernels: 12 us -> 12.4 us
    ppermute x6, waiting for transfers between devices: 4.87 us -> 3.5 us  [swapped(): outs.append(lax.ppermute(value, axis, pairs))]
    pallas_call x5, Pallas kernels: 12 us -> 12.4 us  [call(): pl.pallas_call(kernel, out_shape=outs, in_specs=[pl.BlockSpec(memory_spac...]
  transfers between devices with their start and end apart: 6 -> 6, of which waited for: 2 -> 2; matrix products, arithmetic and copies ran while one was open for 3% -> 3% of each run, Pallas kernels for 14% -> 17%
where the time goes in v8:
time: 30.1 us; the launch traced here: 29.9 us
  Pallas kernels  12.4 us (41%)
  starting transfers between devices  11.4 us (38%)
  waiting for transfers between devices  3.5 us (12%)
  local copies, waits for them, and re-layouts  1.38 us (5%)
  other arithmetic  0.88 us (3%)
  between operations  0.32 us (1%)
    pallas_call x5, Pallas kernels, call(): pl.pallas_call(kernel, out_shape=outs, in_specs=[pl.BlockSpec(memory_spac...  12.4 us
    ppermute x6, starting transfers between devices, swapped(): outs.append(lax.ppermute(value, axis, pairs))  11.4 us
    ppermute x6, waiting for transfers between devices, swapped(): outs.append(lax.ppermute(value, axis, pairs))  3.5 us
    convert_element_type x1, local copies, waits for them, and re-layouts, block(): lax.dynamic_slice_in_dim(charges, jnp.where(flag, side, 0), side, 1)  1.26 us
    another operation x1, other arithmetic, block(): jnp.stack([kernel_fine, kernel_mid, kernel_top])  0.88 us
  transfers between devices with their start and end apart: 6, of which 2 were waited for; matrix products, arithmetic and copies ran while one was open for 3% of the time, Pallas kernels for 17%

profile of v8, /device:TPU:0, one launch (start us, length us, event | category | flops | bytes accessed | tf_op | source)
XLA Modules:
  0.0 29.9 jit_solution(3987137595003544613)
XLA Ops:
  0.0 1.3 %dynamic-slice_convert_fusion = (bf16[24,32,128]{2,1,0:T(8,128)(2,1)S(1)}, bf16[24,32,128]{2,1,0:T(8,128)(2,1)S(1)}) fusion(f32[24,64,128]{2,1,0:T(8,128)} %own.1, s32[]{:T(128)S(6)} %select_n.10, s32[]{:T(128)S(6)} %select_n.9), kind=kLoop, calls=%fused_computation | loop fusion | bytes 786440 | tf_op jit(solution)/shard_map/convert_element_type | solution.py:747
  1.3 0.0 copy-start.3
  1.3 0.8 %collective-permute-start.1 = (bf16[24,32,128]{2,1,0:T(8,128)(2,1)S(1)}, bf16[24,32,128]{2,1,0:T(8,128)(2,1)S(1)}, u32[]{:S(2)}, u32[]{:S(2)}) collective-permute-start(bf16[24,32,128]{2,1,0:T(8,128)(2,1)S(1)} %get-tuple-element.45), channel_id=1, source_target_pairs={{1,2},{2,1},{5,6},{6,5},{9,10},{10,9},{13,14},{14,13},{17,18},{18,... | collective-permute-start | bytes 589832 | tf_op jit(solution)/shard_map/ppermute | solution.py:687
  2.1 4.4 %collective-permute-start = (bf16[24,32,128]{2,1,0:T(8,128)(2,1)S(1)}, bf16[24,32,128]{2,1,0:T(8,128)(2,1)S(1)}, u32[]{:S(2)}, u32[]{:S(2)}) collective-permute-start(bf16[24,32,128]{2,1,0:T(8,128)(2,1)S(1)} %get-tuple-element.46), channel_id=1, source_target_pairs={{0,1},{2,3},{1,0},{3,2},{4,5},{6,7},{5,4},{7,6},{8,9},{10,11},{9,8... | collective-permute-start | bytes 589832 | tf_op jit(solution)/shard_map/ppermute | solution.py:687
  6.5 0.9 %pad_maximum_fusion.refs_0_ = bf16[3,15,15,15]{3,2,1,0:T(8,128)(2,1)S(1)} fusion(bf16[1,15,15,15]{3,2,1,0:T(8,128)(2,1)S(1)} %bitcast.3, bf16[1,15,15,15]{3,2,1,0:T(8,128)(2,1)S(1)} %bitcast.4, bf16[1,15,15,15]{3,2,1,0:T(8,128)(2,1)} %bitcast.5), kind=kLoop, calls=%fused_computation.2 | loop fusion | flops 20250 | bytes 40500 | tf_op jit(solution)/shard_map/stack | solution.py:739
  7.4 0.0 copy-start.11
  7.4 0.0 copy-start.14
  7.4 1.1 %shard_map.199 = (f32[15,48,128]{2,1,0:T(8,128)S(1)}, f32[15,48,128]{2,1,0:T(8,128)S(1)}, f32[15,48,128]{2,1,0:T(8,128)S(1)}, f32[15,24,128]{2,1,0:T(8,128)S(1)}...) custom-call(bf16[3,15,15,15]{3,2,1,0:T(8,128)(2,1)S(1)} %pad_maximum, ...), custom_call_target="tpu_custom_call" | custom-call | tf_op jit(solution)/shard_map/pallas_call | solution.py:653
  8.6 0.0 collective-permute-done.got_a
  8.6 0.0 copy-start.1
  8.6 0.0 copy-start.8
  8.6 0.9 %shard_map.200 = (bf16[24,80,128]{2,1,0:T(8,128)(2,1)S(1)}, bf16[15,32,128]{2,1,0:T(8,128)(2,1)S(1)}, bf16[1040,128]{1,0:T(8,128)(2,1)S(1)}, bf16[1040,128]{1,0:...) custom-call(f32[24,64,128]{2,1,0:T(8,128)S(1)} %copy-done, ...), custom_call_target="tpu_custom_call" | custom-call | tf_op jit(solution)/shard_map/pallas_call | solution.py:653
  9.5 1.6 %collective-permute-start.2 = (bf16[1040,128]{1,0:T(8,128)(2,1)S(1)}, bf16[1040,128]{1,0:T(8,128)(2,1)S(1)}, u32[]{:S(2)}, u32[]{:S(2)}) collective-permute-start(bf16[1040,128]{1,0:T(8,128)(2,1)S(1)} %get-tuple-element.34), channel_id=1, source_target_pairs={{0,4},{8,12},{16,20},{24,28},{4,0},{12,8},{20,16},{28,24},{1,5},{9... | collective-permute-start | bytes 798728 | tf_op jit(solution)/shard_map/ppermute | solution.py:687
  11.1 0.7 %collective-permute-start.3 = (bf16[1040,128]{1,0:T(8,128)(2,1)S(1)}, bf16[1040,128]{1,0:T(8,128)(2,1)S(1)}, u32[]{:S(2)}, u32[]{:S(2)}) collective-permute-start(bf16[1040,128]{1,0:T(8,128)(2,1)S(1)} %get-tuple-element.35), channel_id=1, source_target_pairs={{4,8},{12,16},{20,24},{8,4},{16,12},{24,20},{5,9},{13,17},{21,25},... | collective-permute-start | bytes 798728 | tf_op jit(solution)/shard_map/ppermute | solution.py:687
  11.7 3.3 %collective-permute-start.4 = (bf16[5,32,128]{2,1,0:T(8,128)(2,1)S(1)}, bf16[5,32,128]{2,1,0:T(8,128)(2,1)S(1)}, u32[]{:S(2)}, u32[]{:S(2)}) collective-permute-start(bf16[5,32,128]{2,1,0:T(8,128)(2,1)S(1)} %get-tuple-element.36), channel_id=1, source_target_pairs={{0,8},{4,12},{16,24},{20,28},{8,0},{12,4},{24,16},{28,20},{1,9},{5... | collective-permute-start | bytes 122888 | tf_op jit(solution)/shard_map/ppermute | solution.py:687
  15.0 0.7 %collective-permute-start.5 = (bf16[5,32,128]{2,1,0:T(8,128)(2,1)S(1)}, bf16[5,32,128]{2,1,0:T(8,128)(2,1)S(1)}, u32[]{:S(2)}, u32[]{:S(2)}) collective-permute-start(bf16[5,32,128]{2,1,0:T(8,128)(2,1)S(1)} %get-tuple-element.37), channel_id=1, source_target_pairs={{8,16},{12,20},{16,8},{20,12},{9,17},{13,21},{17,9},{21,13},{10,18... | collective-permute-start | bytes 122888 | tf_op jit(solution)/shard_map/ppermute | solution.py:687
  15.7 0.0 copy-start.2
  15.7 0.0 copy-start.9
  15.7 1.4 %shard_map.201 = (f32[24,48,128]{2,1,0:T(8,128)S(1)}, f32[24,48,128]{2,1,0:T(8,128)S(1)}) custom-call(bf16[24,80,128]{2,1,0:T(8,128)(2,1)S(1)} %get-tuple-element.26.near, bf16[80,160]{1,0:T(8,128)(2,1)S(1)} %copy-done.8, bf16[384,512]{1,0:T(8,128)(2,1)S(1)} %copy-done.1), custom_call_target="tpu_custom_call" | custom-call | tf_op jit(solution)/shard_map/pallas_call | solution.py:653
  17.1 0.0 copy-start.4
  17.2 0.0 copy-start.5
  17.2 0.0 copy-start.6
  17.2 0.0 copy-start.7
  17.2 0.0 copy-start.10
  17.2 0.0 copy-start.12
  17.2 0.0 copy-start.13
  17.2 0.0 copy-start.15
  17.2 0.0 copy-start.17
  17.3 2.6 %shard_map.202 = (f32[24,48,128]{2,1,0:T(8,128)S(1)}, f32[24,48,128]{2,1,0:T(8,128)S(1)}, f32[10,64,128]{2,1,0:T(8,128)S(1)}) custom-call(f32[24,48,128]{2,1,0:T(8,128)S(1)} %get-tuple-element.27.real, f32[24,48,128]{2,1,0:T(8,128)S(1)} %get-tuple-element.28.imag, f32[15,48,128]{2,1,0:T(8,128)S(1)} %get-tuple-element.25.ordered.kr, ...), custom_call_target="tpu_custom_call" | custom-call | tf_op jit(solution)/shard_map/pallas_call | solution.py:653
  19.8 3.2 %collective-permute-done.4.far_a = bf16[5,32,128]{2,1,0:T(8,128)(2,1)S(1)} collective-permute-done((bf16[5,32,128]{2,1,0:T(8,128)(2,1)S(1)}, bf16[5,32,128]{2,1,0:T(8,128)(2,1)S(1)}, u32[]{:S(2)}, u32[]{:S(2)}) %collective-permute-start.4) | collective-permute-done | bytes 40992 | tf_op jit(solution)/shard_map/ppermute | solution.py:687
  23.0 0.3 collective-permute-done.2.next_a
  23.4 6.5 %shard_map.203 = f32[24,64,128]{2,1,0:T(8,128)} custom-call(f32[24,48,128]{2,1,0:T(8,128)S(1)} %get-tuple-element.31.part_real, f32[24,48,128]{2,1,0:T(8,128)S(1)} %get-tuple-element.32.part_imag, f32[10,64,128]{2,1,0:T(8,128)S(1)} %get-tuple-element.33.whole, bf16[1040,128]{1,0:T(8,128)(2,1)S(1)} %collective-permute-done.2.next_a, ...), custom_call_target="tpu_custom_call" | custom-call | tf_op jit(solution)/shard_map/pallas_call | solution.py:653
  (27 shorter events, 0.1 us)
Async XLA Ops:
  0.0 6.5 %copy-start.18 = (bf16[15,15,15]{2,1,0:T(8,128)(2,1)S(1)}, bf16[15,15,15]{2,1,0:T(8,128)(2,1)}, u32[]{:S(2)}) copy-start(bf16[15,15,15]{2,1,0:T(8,128)(2,1)} %param.24) | copy-start | bytes 20254
  0.0 6.5 %copy-start.19 = (bf16[15,15,15]{2,1,0:T(8,128)(2,1)S(1)}, bf16[15,15,15]{2,1,0:T(8,128)(2,1)}, u32[]{:S(2)}) copy-start(bf16[15,15,15]{2,1,0:T(8,128)(2,1)} %param.23) | copy-start | bytes 20254
  0.0 8.6 %copy-start = (f32[24,64,128]{2,1,0:T(8,128)S(1)}, f32[24,64,128]{2,1,0:T(8,128)}, u32[]{:S(2)}) copy-start(f32[24,64,128]{2,1,0:T(8,128)} %own.1) | copy-start | bytes 2359300
  1.3 6.1 %copy-start.3 = (bf16[128,1024]{1,0:T(8,128)(2,1)S(1)}, bf16[128,1024]{1,0:T(8,128)(2,1)}, u32[]{:S(2)}) copy-start(bf16[128,1024]{1,0:T(8,128)(2,1)} %constant.50.clone.refs_1_) | copy-start | bytes 786436
  1.3 7.3 %collective-permute-start.1 = (bf16[24,32,128]{2,1,0:T(8,128)(2,1)S(1)}, bf16[24,32,128]{2,1,0:T(8,128)(2,1)S(1)}, u32[]{:S(2)}, u32[]{:S(2)}) collective-permute-start(bf16[24,32,128]{2,1,0:T(8,128)(2,1)S(1)} %get-tuple-element.45), channel_id=1, source_target_pairs={{1,2},{2,1},{5,6},{6,5},{9,10},{10,9},{13,14},{14,13},{17,18},{18,... | collective-permute-start | bytes 589832 | tf_op jit(solution)/shard_map/ppermute | solution.py:687
  2.1 6.5 %collective-permute-start = (bf16[24,32,128]{2,1,0:T(8,128)(2,1)S(1)}, bf16[24,32,128]{2,1,0:T(8,128)(2,1)S(1)}, u32[]{:S(2)}, u32[]{:S(2)}) collective-permute-start(bf16[24,32,128]{2,1,0:T(8,128)(2,1)S(1)} %get-tuple-element.46), channel_id=1, source_target_pairs={{0,1},{2,3},{1,0},{3,2},{4,5},{6,7},{5,4},{7,6},{8,9},{10,11},{9,8... | collective-permute-start | bytes 589832 | tf_op jit(solution)/shard_map/ppermute | solution.py:687
  7.4 1.2 %copy-start.11 = (bf16[256,128]{1,0:T(8,128)(2,1)S(1)}, bf16[256,128]{1,0:T(8,128)(2,1)}, u32[]{:S(2)}) copy-start(bf16[256,128]{1,0:T(8,128)(2,1)} %constant.51.clone.down_z) | copy-start | bytes 196612
  7.4 1.2 %copy-start.14 = (bf16[64,240]{1,0:T(8,128)(2,1)S(1)}, bf16[64,240]{1,0:T(8,128)(2,1)}, u32[]{:S(2)}) copy-start(bf16[64,240]{1,0:T(8,128)(2,1)} %constant.52.clone.down_y) | copy-start | bytes 92164
  8.6 7.1 %copy-start.1 = (bf16[384,512]{1,0:T(8,128)(2,1)S(1)}, bf16[384,512]{1,0:T(8,128)(2,1)}, u32[]{:S(2)}) copy-start(bf16[384,512]{1,0:T(8,128)(2,1)} %constant.54.clone.to_z) | copy-start | bytes 1179652
  8.6 7.1 %copy-start.8 = (bf16[80,160]{1,0:T(8,128)(2,1)S(1)}, bf16[80,160]{1,0:T(8,128)(2,1)}, u32[]{:S(2)}) copy-start(bf16[80,160]{1,0:T(8,128)(2,1)} %constant.53.clone.to_y) | copy-start | bytes 76804
  9.5 13.8 %collective-permute-start.2 = (bf16[1040,128]{1,0:T(8,128)(2,1)S(1)}, bf16[1040,128]{1,0:T(8,128)(2,1)S(1)}, u32[]{:S(2)}, u32[]{:S(2)}) collective-permute-start(bf16[1040,128]{1,0:T(8,128)(2,1)S(1)} %get-tuple-element.34), channel_id=1, source_target_pairs={{0,4},{8,12},{16,20},{24,28},{4,0},{12,8},{20,16},{28,24},{1,5},{9... | collective-permute-start | bytes 798728 | tf_op jit(solution)/shard_map/ppermute | solution.py:687
  11.1 12.3 %collective-permute-start.3 = (bf16[1040,128]{1,0:T(8,128)(2,1)S(1)}, bf16[1040,128]{1,0:T(8,128)(2,1)S(1)}, u32[]{:S(2)}, u32[]{:S(2)}) collective-permute-start(bf16[1040,128]{1,0:T(8,128)(2,1)S(1)} %get-tuple-element.35), channel_id=1, source_target_pairs={{4,8},{12,16},{20,24},{8,4},{16,12},{24,20},{5,9},{13,17},{21,25},... | collective-permute-start | bytes 798728 | tf_op jit(solution)/shard_map/ppermute | solution.py:687
  11.7 11.3 %collective-permute-start.4 = (bf16[5,32,128]{2,1,0:T(8,128)(2,1)S(1)}, bf16[5,32,128]{2,1,0:T(8,128)(2,1)S(1)}, u32[]{:S(2)}, u32[]{:S(2)}) collective-permute-start(bf16[5,32,128]{2,1,0:T(8,128)(2,1)S(1)} %get-tuple-element.36), channel_id=1, source_target_pairs={{0,8},{4,12},{16,24},{20,28},{8,0},{12,4},{24,16},{28,20},{1,9},{5... | collective-permute-start | bytes 122888 | tf_op jit(solution)/shard_map/ppermute | solution.py:687
  15.0 8.0 %collective-permute-start.5 = (bf16[5,32,128]{2,1,0:T(8,128)(2,1)S(1)}, bf16[5,32,128]{2,1,0:T(8,128)(2,1)S(1)}, u32[]{:S(2)}, u32[]{:S(2)}) collective-permute-start(bf16[5,32,128]{2,1,0:T(8,128)(2,1)S(1)} %get-tuple-element.37), channel_id=1, source_target_pairs={{8,16},{12,20},{16,8},{20,12},{9,17},{13,21},{17,9},{21,13},{10,18... | collective-permute-start | bytes 122888 | tf_op jit(solution)/shard_map/ppermute | solution.py:687
  15.7 1.4 %copy-start.2 = (bf16[768,256]{1,0:T(8,128)(2,1)S(1)}, bf16[768,256]{1,0:T(8,128)(2,1)}, u32[]{:S(2)}) copy-start(bf16[768,256]{1,0:T(8,128)(2,1)} %constant.55.clone.from_z) | copy-start | bytes 1179652
  15.7 1.4 %copy-start.9 = (bf16[64,240]{1,0:T(8,128)(2,1)S(1)}, bf16[64,240]{1,0:T(8,128)(2,1)}, u32[]{:S(2)}) copy-start(bf16[64,240]{1,0:T(8,128)(2,1)} %constant.56.clone.from_y) | copy-start | bytes 92164
  17.1 6.2 %copy-start.4 = (bf16[384,256]{1,0:T(8,128)(2,1)S(1)}, bf16[384,256]{1,0:T(8,128)(2,1)}, u32[]{:S(2)}) copy-start(bf16[384,256]{1,0:T(8,128)(2,1)} %constant.65.clone.t_from_z) | copy-start | bytes 589828
  17.2 6.2 %copy-start.5 = (bf16[768,32]{1,0:T(8,128)(2,1)S(1)}, bf16[768,32]{1,0:T(8,128)(2,1)}, u32[]{:S(2)}) copy-start(bf16[768,32]{1,0:T(8,128)(2,1)} %constant.62.clone.t_down_z) | copy-start | bytes 147460
  17.2 6.2 %copy-start.6 = (bf16[384,256]{1,0:T(8,128)(2,1)S(1)}, bf16[384,256]{1,0:T(8,128)(2,1)}, u32[]{:S(2)}) copy-start(bf16[384,256]{1,0:T(8,128)(2,1)} %constant.59.clone.m_from_z) | copy-start | bytes 589828
  17.2 6.2 %copy-start.7 = (bf16[384,256]{1,0:T(8,128)(2,1)S(1)}, bf16[384,256]{1,0:T(8,128)(2,1)}, u32[]{:S(2)}) copy-start(bf16[384,256]{1,0:T(8,128)(2,1)} %constant.58.clone.m_to_z) | copy-start | bytes 589828
  17.2 6.2 %copy-start.10 = (bf16[2,64,144]{2,1,0:T(8,128)(2,1)S(1)}, bf16[2,64,144]{2,1,0:T(8,128)(2,1)}, u32[]{:S(2)}) copy-start(bf16[2,64,144]{2,1,0:T(8,128)(2,1)} %constant.60.clone.m_from_y) | copy-start | bytes 110596
  17.2 6.1 %copy-start.12 = (bf16[96,256]{1,0:T(8,128)(2,1)S(1)}, bf16[96,256]{1,0:T(8,128)(2,1)}, u32[]{:S(2)}) copy-start(bf16[96,256]{1,0:T(8,128)(2,1)} %constant.64.clone.t_to_z) | copy-start | bytes 147460
  17.2 6.1 %copy-start.13 = (bf16[2,64,96]{2,1,0:T(8,128)(2,1)S(1)}, bf16[2,64,96]{2,1,0:T(8,128)(2,1)}, u32[]{:S(2)}) copy-start(bf16[2,64,96]{2,1,0:T(8,128)(2,1)} %constant.66.clone.t_from_y) | copy-start | bytes 73732
  17.2 6.1 %copy-start.15 = (bf16[96,64]{1,0:T(8,128)(2,1)S(1)}, bf16[96,64]{1,0:T(8,128)(2,1)}, u32[]{:S(2)}) copy-start(bf16[96,64]{1,0:T(8,128)(2,1)} %constant.57.clone.m_to_y) | copy-start | bytes 36868
  17.2 6.1 %copy-start.17 = (bf16[32,64]{1,0:T(8,128)(2,1)S(1)}, bf16[32,64]{1,0:T(8,128)(2,1)}, u32[]{:S(2)}) copy-start(bf16[32,64]{1,0:T(8,128)(2,1)} %constant.63.clone.t_to_y) | copy-start | bytes 12292
  19.8 3.6 %copy-start.16 = (bf16[64,96]{1,0:T(8,128)(2,1)S(1)}, bf16[64,96]{1,0:T(8,128)(2,1)}, u32[]{:S(2)}) copy-start(bf16[64,96]{1,0:T(8,128)(2,1)} %constant.61.clone.t_down_y) | copy-start | bytes 36868

commit v9 on v8

--- a/solution.py
+++ b/solution.py
@@ -274,8 +274,8 @@
     outputs = outputs or list(range(out_real.shape[0]))
     taken = taken or (lambda x: True)
 
-    def body(part, _):
-        rows = pl.ds(pl.multiple_of(8 * part, 8), 8)
+    def body(part):
+        rows = slice(8 * part, 8 * part + 8)
         for start in range(0, len(outputs), block):
             wanted = outputs[start : start + block]
             sums = [[None] * 3 for _ in wanted]
@@ -298,9 +298,9 @@
                     value = value[0] + before[0][out, rows, :], value[1] + before[1][out, rows, :]
                 out_real[start + i, rows, :] = value[0]
                 out_imag[start + i, rows, :] = value[1]
-        return 0
-
-    lax.fori_loop(0, period // 8, body, 0)
+
+    for part in range(period // 8):
+        body(part)
 
 
 def rows_loop(count, step, body):
@@ -426,7 +426,30 @@
     to_frequencies_z(ahead, 4, to_z, real, imag)
 
 
-def own_sum_kernel(real, imag, kr, kd, ks, from_z, from_y, out_real, out_imag, whole, back):
+def own_sum_kernel(
+    real,
+    imag,
+    coarse,
+    kr,
+    kd,
+    ks,
+    from_z,
+    from_y,
+    mr,
+    md,
+    ms,
+    m_to_y,
+    m_to_z,
+    out_real,
+    out_imag,
+    whole,
+    m_part_real,
+    m_part_imag,
+    back,
+    m_real,
+    m_imag,
+    m_ahead,
+):
     count = real.shape[0]
     half = kr.shape[0] // 2
     along_x(
@@ -439,6 +462,20 @@
         None,
         lambda x: half <= x < half + count,
     )
+    lines = m_real.shape[0]
+    first = half + 1
+    to_frequencies_y(lambda k: coarse[k + PARTS], lines, 6, m_to_y, m_ahead, True)
+    to_frequencies_z(m_ahead, 6, m_to_z, m_real, m_imag)
+    along_x(
+        lambda x, rows: m_real[x - first, rows, :],
+        lambda x, rows: m_imag[x - first, rows, :],
+        (mr, md, ms),
+        m_part_real,
+        m_part_imag,
+        7,
+        None,
+        lambda x: first <= x < first + lines,
+    )
     inner = slice(half, count - half)
 
     def write(x, value):
@@ -453,6 +490,8 @@
     part_real,
     part_imag,
     whole,
+    m_part_real,
+    m_part_imag,
     next_a,
     next_b,
     far_a,
@@ -592,9 +631,12 @@
     for k, row in enumerate(rows):
         mid[k] = row
 
-    skip = (mid.shape[0] - m_real.shape[0]) // 2
-    to_frequencies_y(lambda x: mid[x + skip], m_real.shape[0], 9, m_to_y, m_ahead, True)
-    to_frequencies_z(m_ahead, 9, m_to_z, m_real, m_imag)
+    own_lines = last - 1
+    m_rows = m_real.shape[0] + own_lines
+    skip = (mid.shape[0] - m_rows) // 2
+    sides = [x for x in range(m_rows) if not reach < x <= reach + own_lines]
+    to_frequencies_y(lambda k: mid[sides[k] + skip], len(sides), 8, m_to_y, m_ahead, True)
+    to_frequencies_z(m_ahead, 8, m_to_z, m_real, m_imag)
 
     t_width = t_cells.shape[1]
     spare = (t_width - t_columns) // 2
@@ -620,7 +662,17 @@
     def plain(ref):
         return lambda x, rows: ref[x, rows, :]
 
-    along_x(plain(m_real), plain(m_imag), (mr, md, ms), m_er, m_ei, 7)
+    along_x(
+        lambda x, rows: m_real[sides.index(x), rows, :],
+        lambda x, rows: m_imag[sides.index(x), rows, :],
+        (mr, md, ms),
+        m_er,
+        m_ei,
+        7,
+        None,
+        lambda x: x in sides,
+        (m_part_real, m_part_imag),
+    )
     along_x(plain(t_real), plain(t_imag), (tr, td, ts), t_er, t_ei, 7)
 
     def top_write(x, value):
@@ -662,13 +714,13 @@
     )(*args)
 
 
-def level_scratch(level, ny, nz, lanes, extra=()):
+def level_scratch(level, in_x, ny, nz, lanes, extra=()):
     rows = [
         (F32, (count, level.rows, LANES))
-        for count in (level.in_x, level.in_x, level.out_x, level.out_x)
+        for count in (in_x, in_x, level.out_x, level.out_x)
     ]
     terms = [
-        (BF, (2, level.in_x * 2 * level.freq, lanes)),
+        (BF, (2, in_x * 2 * level.freq, lanes)),
         (BF, (2, level.out_x * 2 * level.freq, nz)),
     ]
     return [*rows, *extra, *terms, (F32, (level.out_x, ny, nz))]
@@ -786,6 +838,9 @@
     far_a, far_b = swapped(far_a, far_b, "gx", 2)
     next_a, next_b = swapped(next_a, next_b, "gx", 1)
 
+    parts = [np.concatenate(two(mid.table_y[:, at : at + packed]), 1) for at in (0, packed)]
+    mid_to_y = np.concatenate(parts, 0)
+    mid_to_z = terms_below(np.tile(mid.table_z, (2, 1)))
     spectrum = [jax.ShapeDtypeStruct((nx, fine.rows, LANES), F32)] * 2
     own = call(
         own_kernel,
@@ -797,9 +852,26 @@
     inner = nx - 2 * half
     own = call(
         own_sum_kernel,
-        [*spectrum, jax.ShapeDtypeStruct((inner, ny, nz), F32)],
-        [(BF, (2, inner * 2 * fine.freq, nz))],
-        [*own, *spectra[:3], fine.from_z, fine.from_y[0]],
+        [
+            *spectrum,
+            jax.ShapeDtypeStruct((inner, ny, nz), F32),
+            *[jax.ShapeDtypeStruct((mid.out_x, mid.rows, LANES), F32)] * 2,
+        ],
+        [
+            (BF, (2, inner * 2 * fine.freq, nz)),
+            *[(F32, (mx - 1, mid.rows, LANES))] * 2,
+            (BF, (2, (mx - 1) * 2 * mid.freq, LANES)),
+        ],
+        [
+            *own,
+            coarse,
+            *spectra[:3],
+            fine.from_z,
+            fine.from_y[0],
+            *spectra[3:6],
+            mid_to_y,
+            mid_to_z,
+        ],
         10,
     )
 
@@ -820,8 +892,8 @@
             (BF, (2, 2 * half * 2 * fine.freq, nz)),
             (BF, (2, 2 * half * 2 * fine.freq, nz)),
             (BF, (3 * mx + 1 + 2 * reach, packed, LANES)),
-            *level_scratch(mid, ny, nz, LANES),
-            *level_scratch(top, ny, nz, tz, [(BF, (top.in_x, wide_top, tz))]),
+            *level_scratch(mid, mid.in_x - mx + 1, ny, nz, LANES),
+            *level_scratch(top, top.in_x, ny, nz, tz, [(BF, (top.in_x, wide_top, tz))]),
         ],
         [
             *own,
@@ -836,8 +908,8 @@
             fine.from_z,
             fine.from_y[0],
             *spectra[3:6],
-            np.concatenate([np.concatenate(two(mid.table_y[:, at : at + packed]), 1) for at in (0, packed)], 0),
-            terms_below(np.tile(mid.table_z, (2, 1))),
+            mid_to_y,
+            mid_to_z,
             mid.from_z,
             np.stack(mid.from_y),
             *spectra[6:],

time: 30.1 us -> 29.2 us (0.970)
  the two profiles are of different devices: /device:TPU:0 before, /device:TPU:12 now
where the time goes in v9:
time: 29.2 us; the launch traced here: 28.9 us
  Pallas kernels  11.7 us (40%)
  starting transfers between devices  11.1 us (38%)
  waiting for transfers between devices  2.93 us (10%)
  local copies, waits for them, and re-layouts  1.97 us (7%)
  other arithmetic  0.88 us (3%)
  between operations  0.38 us (1%)
    pallas_call x5, Pallas kernels, call(): pl.pallas_call(kernel, out_shape=outs, in_specs=[pl.BlockSpec(memory_spac...  11.7 us
    ppermute x6, starting transfers between devices, swapped(): outs.append(lax.ppermute(value, axis, pairs))  11.1 us
    ppermute x6, waiting for transfers between devices, swapped(): outs.append(lax.ppermute(value, axis, pairs))  2.93 us
    convert_element_type x1, local copies, waits for them, and re-layouts, block(): lax.dynamic_slice_in_dim(charges, jnp.where(flag, side, 0), side, 1)  1.27 us
    another operation x1, other arithmetic, block(): jnp.stack([kernel_fine, kernel_mid, kernel_top])  0.88 us
    unnamed x40, local copies, waits for them, and re-layouts  0.7 us
  transfers between devices with their start and end apart: 6, of which 1 were waited for; matrix products, arithmetic and copies ran while one was open for 3% of the time, Pallas kernels for 19%

profile of v9, /device:TPU:12, one launch (start us, length us, event | category | flops | bytes accessed | tf_op | source)
XLA Modules:
  0.0 28.9 jit_solution(7893577023436839816)
XLA Ops:
  0.0 1.3 %dynamic-slice_convert_fusion = (bf16[24,32,128]{2,1,0:T(8,128)(2,1)S(1)}, bf16[24,32,128]{2,1,0:T(8,128)(2,1)S(1)}) fusion(f32[24,64,128]{2,1,0:T(8,128)} %own.1, s32[]{:T(128)S(6)} %select_n.10, s32[]{:T(128)S(6)} %select_n.9), kind=kLoop, calls=%fused_computation | loop fusion | bytes 786440 | tf_op jit(solution)/shard_map/convert_element_type | solution.py:799
  1.3 0.0 copy-start.4
  1.3 2.1 %collective-permute-start.1 = (bf16[24,32,128]{2,1,0:T(8,128)(2,1)S(1)}, bf16[24,32,128]{2,1,0:T(8,128)(2,1)S(1)}, u32[]{:S(2)}, u32[]{:S(2)}) collective-permute-start(bf16[24,32,128]{2,1,0:T(8,128)(2,1)S(1)} %get-tuple-element.49), channel_id=1, source_target_pairs={{1,2},{2,1},{5,6},{6,5},{9,10},{10,9},{13,14},{14,13},{17,18},{18,... | collective-permute-start | bytes 589832 | tf_op jit(solution)/shard_map/ppermute | solution.py:739
  3.4 0.1 collective-permute-start
  3.4 0.9 %pad_maximum_fusion.refs_0_ = bf16[3,15,15,15]{3,2,1,0:T(8,128)(2,1)S(1)} fusion(bf16[1,15,15,15]{3,2,1,0:T(8,128)(2,1)S(1)} %bitcast.3, bf16[1,15,15,15]{3,2,1,0:T(8,128)(2,1)S(1)} %bitcast.4, bf16[1,15,15,15]{3,2,1,0:T(8,128)(2,1)} %bitcast.5), kind=kLoop, calls=%fused_computation.2 | loop fusion | flops 20250 | bytes 40500 | tf_op jit(solution)/shard_map/stack | solution.py:791
  4.3 0.0 copy-start.12
  4.4 0.0 copy-start.15
  4.4 1.1 %shard_map.199 = (f32[15,48,128]{2,1,0:T(8,128)S(1)}, f32[15,48,128]{2,1,0:T(8,128)S(1)}, f32[15,48,128]{2,1,0:T(8,128)S(1)}, f32[15,24,128]{2,1,0:T(8,128)S(1)}...) custom-call(bf16[3,15,15,15]{3,2,1,0:T(8,128)(2,1)S(1)} %pad_maximum, ...), custom_call_target="tpu_custom_call" | custom-call | tf_op jit(solution)/shard_map/pallas_call | solution.py:705
  5.5 2.9 %collective-permute-done.1.got_b = bf16[24,32,128]{2,1,0:T(8,128)(2,1)S(1)} collective-permute-done((bf16[24,32,128]{2,1,0:T(8,128)(2,1)S(1)}, bf16[24,32,128]{2,1,0:T(8,128)(2,1)S(1)}, u32[]{:S(2)}, u32[]{:S(2)}) %collective-permute-start.1) | collective-permute-done | bytes 196640 | tf_op jit(solution)/shard_map/ppermute | solution.py:739
  8.4 0.0 copy-start.1
  8.4 0.0 copy-start.8
  8.5 0.8 %shard_map.200 = (bf16[24,80,128]{2,1,0:T(8,128)(2,1)S(1)}, bf16[15,32,128]{2,1,0:T(8,128)(2,1)S(1)}, bf16[1040,128]{1,0:T(8,128)(2,1)S(1)}, bf16[1040,128]{1,0:...) custom-call(f32[24,64,128]{2,1,0:T(8,128)S(1)} %copy-done, ...), custom_call_target="tpu_custom_call" | custom-call | tf_op jit(solution)/shard_map/pallas_call | solution.py:705
  9.3 1.6 %collective-permute-start.2 = (bf16[1040,128]{1,0:T(8,128)(2,1)S(1)}, bf16[1040,128]{1,0:T(8,128)(2,1)S(1)}, u32[]{:S(2)}, u32[]{:S(2)}) collective-permute-start(bf16[1040,128]{1,0:T(8,128)(2,1)S(1)} %get-tuple-element.42), channel_id=1, source_target_pairs={{0,4},{8,12},{16,20},{24,28},{4,0},{12,8},{20,16},{28,24},{1,5},{9... | collective-permute-start | bytes 798728 | tf_op jit(solution)/shard_map/ppermute | solution.py:739
  10.9 2.3 %collective-permute-start.3 = (bf16[1040,128]{1,0:T(8,128)(2,1)S(1)}, bf16[1040,128]{1,0:T(8,128)(2,1)S(1)}, u32[]{:S(2)}, u32[]{:S(2)}) collective-permute-start(bf16[1040,128]{1,0:T(8,128)(2,1)S(1)} %get-tuple-element.43), channel_id=1, source_target_pairs={{4,8},{12,16},{20,24},{8,4},{16,12},{24,20},{5,9},{13,17},{21,25},... | collective-permute-start | bytes 798728 | tf_op jit(solution)/shard_map/ppermute | solution.py:739
  13.2 0.1 collective-permute-start.4
  13.3 5.0 %collective-permute-start.5 = (bf16[5,32,128]{2,1,0:T(8,128)(2,1)S(1)}, bf16[5,32,128]{2,1,0:T(8,128)(2,1)S(1)}, u32[]{:S(2)}, u32[]{:S(2)}) collective-permute-start(bf16[5,32,128]{2,1,0:T(8,128)(2,1)S(1)} %get-tuple-element.45), channel_id=1, source_target_pairs={{8,16},{12,20},{16,8},{20,12},{9,17},{13,21},{17,9},{21,13},{10,18... | collective-permute-start | bytes 122888 | tf_op jit(solution)/shard_map/ppermute | solution.py:739
  18.3 0.0 copy-start.2
  18.3 0.0 copy-start.3
  18.4 0.0 copy-start.9
  18.4 0.0 copy-start.10
  18.4 1.4 %shard_map.201 = (f32[24,48,128]{2,1,0:T(8,128)S(1)}, f32[24,48,128]{2,1,0:T(8,128)S(1)}) custom-call(bf16[24,80,128]{2,1,0:T(8,128)(2,1)S(1)} %get-tuple-element.28.near, bf16[80,160]{1,0:T(8,128)(2,1)S(1)} %copy-done.8, bf16[384,512]{1,0:T(8,128)(2,1)S(1)} %copy-done.1), custom_call_target="tpu_custom_call" | custom-call | tf_op jit(solution)/shard_map/pallas_call | solution.py:705
  19.8 0.0 copy-start.5
  19.8 0.0 copy-start.6
  19.8 0.0 copy-start.7
  19.9 0.0 copy-start.11
  19.9 0.0 copy-start.13
  19.9 0.0 copy-start.14
  19.9 0.0 copy-start.16
  19.9 3.1 %shard_map.202 = (f32[24,48,128]{2,1,0:T(8,128)S(1)}, f32[24,48,128]{2,1,0:T(8,128)S(1)}, f32[10,64,128]{2,1,0:T(8,128)S(1)}, f32[13,24,128]{2,1,0:T(8,128)S(1)}, f32[13,24,128]{2,1,0:T(8,128)S(1)}) custom-call(f32[24,48,128]{2,1,0:T(8,128)S(1)} %get-tuple-element.29.real, f32[24,48,128]{2,1,0:T(8,128)S(1)} %get-tuple-element.30.imag, ...), custom_call_target="tpu_custom_call" | custom-call | tf_op jit(solution)/shard_map/pallas_call | solution.py:705
  23.0 0.0 copy-start.17
  23.1 0.6 %copy-done.17 = bf16[32,64]{1,0:T(8,128)(2,1)S(1)} copy-done((bf16[32,64]{1,0:T(8,128)(2,1)S(1)}, bf16[32,64]{1,0:T(8,128)(2,1)}, u32[]{:S(2)}) %copy-start.17) | copy-done | bytes 4120
  23.7 5.2 %shard_map.203 = f32[24,64,128]{2,1,0:T(8,128)} custom-call(f32[24,48,128]{2,1,0:T(8,128)S(1)} %get-tuple-element.37.part_real, f32[24,48,128]{2,1,0:T(8,128)S(1)} %get-tuple-element.38.part_imag, f32[10,64,128]{2,1,0:T(8,128)S(1)} %get-tuple-element.39.whole, f32[13,24,128]{2,1,0:T(8,128)S(1)} %get-tuple-element.40.m_part_real, ...), custom_call_target="tpu_custom_call" | custom-call | tf_op jit(solution)/shard_map/pallas_call | solution.py:705
  (27 shorter events, 0.1 us)
Async XLA Ops:
  0.0 3.4 %copy-start.18 = (bf16[15,15,15]{2,1,0:T(8,128)(2,1)S(1)}, bf16[15,15,15]{2,1,0:T(8,128)(2,1)}, u32[]{:S(2)}) copy-start(bf16[15,15,15]{2,1,0:T(8,128)(2,1)} %param.24) | copy-start | bytes 20254
  0.0 3.4 %copy-start.19 = (bf16[15,15,15]{2,1,0:T(8,128)(2,1)S(1)}, bf16[15,15,15]{2,1,0:T(8,128)(2,1)}, u32[]{:S(2)}) copy-start(bf16[15,15,15]{2,1,0:T(8,128)(2,1)} %param.23) | copy-start | bytes 20254
  0.0 8.4 %copy-start = (f32[24,64,128]{2,1,0:T(8,128)S(1)}, f32[24,64,128]{2,1,0:T(8,128)}, u32[]{:S(2)}) copy-start(f32[24,64,128]{2,1,0:T(8,128)} %own.1) | copy-start | bytes 2359300
  1.3 3.1 %copy-start.4 = (bf16[128,1024]{1,0:T(8,128)(2,1)S(1)}, bf16[128,1024]{1,0:T(8,128)(2,1)}, u32[]{:S(2)}) copy-start(bf16[128,1024]{1,0:T(8,128)(2,1)} %constant.50.clone.refs_1_) | copy-start | bytes 786436
  1.3 7.1 %collective-permute-start.1 = (bf16[24,32,128]{2,1,0:T(8,128)(2,1)S(1)}, bf16[24,32,128]{2,1,0:T(8,128)(2,1)S(1)}, u32[]{:S(2)}, u32[]{:S(2)}) collective-permute-start(bf16[24,32,128]{2,1,0:T(8,128)(2,1)S(1)} %get-tuple-element.49), channel_id=1, source_target_pairs={{1,2},{2,1},{5,6},{6,5},{9,10},{10,9},{13,14},{14,13},{17,18},{18,... | collective-permute-start | bytes 589832 | tf_op jit(solution)/shard_map/ppermute | solution.py:739
  3.4 5.1 %collective-permute-start = (bf16[24,32,128]{2,1,0:T(8,128)(2,1)S(1)}, bf16[24,32,128]{2,1,0:T(8,128)(2,1)S(1)}, u32[]{:S(2)}, u32[]{:S(2)}) collective-permute-start(bf16[24,32,128]{2,1,0:T(8,128)(2,1)S(1)} %get-tuple-element.50), channel_id=1, source_target_pairs={{0,1},{2,3},{1,0},{3,2},{4,5},{6,7},{5,4},{7,6},{8,9},{10,11},{9,8... | collective-permute-start | bytes 589832 | tf_op jit(solution)/shard_map/ppermute | solution.py:739
  4.3 4.1 %copy-start.12 = (bf16[256,128]{1,0:T(8,128)(2,1)S(1)}, bf16[256,128]{1,0:T(8,128)(2,1)}, u32[]{:S(2)}) copy-start(bf16[256,128]{1,0:T(8,128)(2,1)} %constant.51.clone.down_z) | copy-start | bytes 196612
  4.4 4.1 %copy-start.15 = (bf16[64,240]{1,0:T(8,128)(2,1)S(1)}, bf16[64,240]{1,0:T(8,128)(2,1)}, u32[]{:S(2)}) copy-start(bf16[64,240]{1,0:T(8,128)(2,1)} %constant.52.clone.down_y) | copy-start | bytes 92164
  8.4 9.9 %copy-start.1 = (bf16[384,512]{1,0:T(8,128)(2,1)S(1)}, bf16[384,512]{1,0:T(8,128)(2,1)}, u32[]{:S(2)}) copy-start(bf16[384,512]{1,0:T(8,128)(2,1)} %constant.54.clone.to_z) | copy-start | bytes 1179652
  8.4 9.9 %copy-start.8 = (bf16[80,160]{1,0:T(8,128)(2,1)S(1)}, bf16[80,160]{1,0:T(8,128)(2,1)}, u32[]{:S(2)}) copy-start(bf16[80,160]{1,0:T(8,128)(2,1)} %constant.53.clone.to_y) | copy-start | bytes 76804
  9.3 13.7 %collective-permute-start.2 = (bf16[1040,128]{1,0:T(8,128)(2,1)S(1)}, bf16[1040,128]{1,0:T(8,128)(2,1)S(1)}, u32[]{:S(2)}, u32[]{:S(2)}) collective-permute-start(bf16[1040,128]{1,0:T(8,128)(2,1)S(1)} %get-tuple-element.42), channel_id=1, source_target_pairs={{0,4},{8,12},{16,20},{24,28},{4,0},{12,8},{20,16},{28,24},{1,5},{9... | collective-permute-start | bytes 798728 | tf_op jit(solution)/shard_map/ppermute | solution.py:739
  10.9 12.2 %collective-permute-start.3 = (bf16[1040,128]{1,0:T(8,128)(2,1)S(1)}, bf16[1040,128]{1,0:T(8,128)(2,1)S(1)}, u32[]{:S(2)}, u32[]{:S(2)}) collective-permute-start(bf16[1040,128]{1,0:T(8,128)(2,1)S(1)} %get-tuple-element.43), channel_id=1, source_target_pairs={{4,8},{12,16},{20,24},{8,4},{16,12},{24,20},{5,9},{13,17},{21,25},... | collective-permute-start | bytes 798728 | tf_op jit(solution)/shard_map/ppermute | solution.py:739
  13.2 9.8 %collective-permute-start.4 = (bf16[5,32,128]{2,1,0:T(8,128)(2,1)S(1)}, bf16[5,32,128]{2,1,0:T(8,128)(2,1)S(1)}, u32[]{:S(2)}, u32[]{:S(2)}) collective-permute-start(bf16[5,32,128]{2,1,0:T(8,128)(2,1)S(1)} %get-tuple-element.44), channel_id=1, source_target_pairs={{0,8},{4,12},{16,24},{20,28},{8,0},{12,4},{24,16},{28,20},{1,9},{5... | collective-permute-start | bytes 122888 | tf_op jit(solution)/shard_map/ppermute | solution.py:739
  13.3 9.8 %collective-permute-start.5 = (bf16[5,32,128]{2,1,0:T(8,128)(2,1)S(1)}, bf16[5,32,128]{2,1,0:T(8,128)(2,1)S(1)}, u32[]{:S(2)}, u32[]{:S(2)}) collective-permute-start(bf16[5,32,128]{2,1,0:T(8,128)(2,1)S(1)} %get-tuple-element.45), channel_id=1, source_target_pairs={{8,16},{12,20},{16,8},{20,12},{9,17},{13,21},{17,9},{21,13},{10,18... | collective-permute-start | bytes 122888 | tf_op jit(solution)/shard_map/ppermute | solution.py:739
  18.3 1.4 %copy-start.2 = (bf16[768,256]{1,0:T(8,128)(2,1)S(1)}, bf16[768,256]{1,0:T(8,128)(2,1)}, u32[]{:S(2)}) copy-start(bf16[768,256]{1,0:T(8,128)(2,1)} %constant.55.clone.from_z) | copy-start | bytes 1179652
  18.3 1.4 %copy-start.3 = (bf16[384,256]{1,0:T(8,128)(2,1)S(1)}, bf16[384,256]{1,0:T(8,128)(2,1)}, u32[]{:S(2)}) copy-start(bf16[384,256]{1,0:T(8,128)(2,1)} %constant.58.clone.m_to_z) | copy-start | bytes 589828
  18.4 1.4 %copy-start.9 = (bf16[64,240]{1,0:T(8,128)(2,1)S(1)}, bf16[64,240]{1,0:T(8,128)(2,1)}, u32[]{:S(2)}) copy-start(bf16[64,240]{1,0:T(8,128)(2,1)} %constant.56.clone.from_y) | copy-start | bytes 92164
  18.4 1.4 %copy-start.10 = (bf16[96,64]{1,0:T(8,128)(2,1)S(1)}, bf16[96,64]{1,0:T(8,128)(2,1)}, u32[]{:S(2)}) copy-start(bf16[96,64]{1,0:T(8,128)(2,1)} %constant.57.clone.m_to_y) | copy-start | bytes 36868
  19.8 3.2 %copy-start.5 = (bf16[384,256]{1,0:T(8,128)(2,1)S(1)}, bf16[384,256]{1,0:T(8,128)(2,1)}, u32[]{:S(2)}) copy-start(bf16[384,256]{1,0:T(8,128)(2,1)} %constant.65.clone.t_from_z) | copy-start | bytes 589828
  19.8 3.2 %copy-start.6 = (bf16[768,32]{1,0:T(8,128)(2,1)S(1)}, bf16[768,32]{1,0:T(8,128)(2,1)}, u32[]{:S(2)}) copy-start(bf16[768,32]{1,0:T(8,128)(2,1)} %constant.62.clone.t_down_z) | copy-start | bytes 147460
  19.8 3.2 %copy-start.7 = (bf16[384,256]{1,0:T(8,128)(2,1)S(1)}, bf16[384,256]{1,0:T(8,128)(2,1)}, u32[]{:S(2)}) copy-start(bf16[384,256]{1,0:T(8,128)(2,1)} %constant.59.clone.m_from_z) | copy-start | bytes 589828
  19.9 3.2 %copy-start.11 = (bf16[2,64,144]{2,1,0:T(8,128)(2,1)S(1)}, bf16[2,64,144]{2,1,0:T(8,128)(2,1)}, u32[]{:S(2)}) copy-start(bf16[2,64,144]{2,1,0:T(8,128)(2,1)} %constant.60.clone.m_from_y) | copy-start | bytes 110596
  19.9 3.2 %copy-start.13 = (bf16[96,256]{1,0:T(8,128)(2,1)S(1)}, bf16[96,256]{1,0:T(8,128)(2,1)}, u32[]{:S(2)}) copy-start(bf16[96,256]{1,0:T(8,128)(2,1)} %constant.64.clone.t_to_z) | copy-start | bytes 147460
  19.9 3.2 %copy-start.14 = (bf16[2,64,96]{2,1,0:T(8,128)(2,1)S(1)}, bf16[2,64,96]{2,1,0:T(8,128)(2,1)}, u32[]{:S(2)}) copy-start(bf16[2,64,96]{2,1,0:T(8,128)(2,1)} %constant.66.clone.t_from_y) | copy-start | bytes 73732
  19.9 3.2 %copy-start.16 = (bf16[64,96]{1,0:T(8,128)(2,1)S(1)}, bf16[64,96]{1,0:T(8,128)(2,1)}, u32[]{:S(2)}) copy-start(bf16[64,96]{1,0:T(8,128)(2,1)} %constant.61.clone.t_down_y) | copy-start | bytes 36868
  23.0 0.7 %copy-start.17 = (bf16[32,64]{1,0:T(8,128)(2,1)S(1)}, bf16[32,64]{1,0:T(8,128)(2,1)}, u32[]{:S(2)}) copy-start(bf16[32,64]{1,0:T(8,128)(2,1)} %constant.63.clone.t_to_y) | copy-start | bytes 12292

commit v10 on v9

--- a/solution.py
+++ b/solution.py
@@ -13,7 +13,7 @@
 LANES = 128
 BLOCK = 8
 PARTS = 2
-TERMS = 3
+TERMS = 2
 
 
 def two(matrix):
@@ -301,17 +301,6 @@
 
     for part in range(period // 8):
         body(part)
-
-
-def rows_loop(count, step, body):
-    def trip(i, _):
-        for k in range(step):
-            body(i * step + k)
-        return 0
-
-    lax.fori_loop(0, count // step, trip, 0)
-    for x in range(count - count % step, count):
-        body(x)
 
 
 def all_terms(value):
@@ -697,7 +686,8 @@
         out[2 * i] += m_out[i]
         out[2 * i + 1] += 0.5 * (m_out[i] + m_out[i + 1])
 
-    rows_loop(count // 2, 2, finish)
+    for i in range(count // 2):
+        finish(i)
 
 
 def call(kernel, outs, scratch, args, mib, loose=()):

time: 29.2 us -> 28.9 us (0.990)
  Pallas kernels: 11.7 us -> 11.3 us
    pallas_call x5, Pallas kernels: 11.7 us -> 11.3 us  [call(): pl.pallas_call(kernel, out_shape=outs, in_specs=[pl.BlockSpec(memory_spac...]
where the time goes in v10:
time: 28.9 us; the launch traced here: 28.6 us
  Pallas kernels  11.3 us (39%)
  starting transfers between devices  11.1 us (38%)
  waiting for transfers between devices  2.93 us (10%)
  local copies, waits for them, and re-layouts  1.97 us (7%)
  other arithmetic  0.88 us (3%)
  between operations  0.38 us (1%)
    pallas_call x5, Pallas kernels, call(): pl.pallas_call(kernel, out_shape=outs, in_specs=[pl.BlockSpec(memory_spac...  11.3 us
    ppermute x6, starting transfers between devices, swapped(): outs.append(lax.ppermute(value, axis, pairs))  11.1 us
    ppermute x6, waiting for transfers between devices, swapped(): outs.append(lax.ppermute(value, axis, pairs))  2.93 us
    convert_element_type x1, local copies, waits for them, and re-layouts, block(): lax.dynamic_slice_in_dim(charges, jnp.where(flag, side, 0), side, 1)  1.27 us
    another operation x1, other arithmetic, block(): jnp.stack([kernel_fine, kernel_mid, kernel_top])  0.88 us
    unnamed x40, local copies, waits for them, and re-layouts  0.7 us
  transfers between devices with their start and end apart: 6, of which 1 were waited for; matrix products, arithmetic and copies ran while one was open for 3% of the time, Pallas kernels for 19%

profile of v10, /device:TPU:12, one launch (start us, length us, event | category | flops | bytes accessed | tf_op | source)
XLA Modules:
  0.0 28.6 jit_solution(1850586410949346686)
XLA Ops:
  0.0 1.3 %dynamic-slice_convert_fusion = (bf16[24,32,128]{2,1,0:T(8,128)(2,1)S(1)}, bf16[24,32,128]{2,1,0:T(8,128)(2,1)S(1)}) fusion(f32[24,64,128]{2,1,0:T(8,128)} %own.1, s32[]{:T(128)S(6)} %select_n.10, s32[]{:T(128)S(6)} %select_n.9), kind=kLoop, calls=%fused_computation | loop fusion | bytes 786440 | tf_op jit(solution)/shard_map/convert_element_type | solution.py:789
  1.3 0.0 copy-start.4
  1.3 2.1 %collective-permute-start.1 = (bf16[24,32,128]{2,1,0:T(8,128)(2,1)S(1)}, bf16[24,32,128]{2,1,0:T(8,128)(2,1)S(1)}, u32[]{:S(2)}, u32[]{:S(2)}) collective-permute-start(bf16[24,32,128]{2,1,0:T(8,128)(2,1)S(1)} %get-tuple-element.49), channel_id=1, source_target_pairs={{1,2},{2,1},{5,6},{6,5},{9,10},{10,9},{13,14},{14,13},{17,18},{18,... | collective-permute-start | bytes 589832 | tf_op jit(solution)/shard_map/ppermute | solution.py:729
  3.4 0.1 collective-permute-start
  3.4 0.9 %pad_maximum_fusion.refs_0_ = bf16[3,15,15,15]{3,2,1,0:T(8,128)(2,1)S(1)} fusion(bf16[1,15,15,15]{3,2,1,0:T(8,128)(2,1)S(1)} %bitcast.3, bf16[1,15,15,15]{3,2,1,0:T(8,128)(2,1)S(1)} %bitcast.4, bf16[1,15,15,15]{3,2,1,0:T(8,128)(2,1)} %bitcast.5), kind=kLoop, calls=%fused_computation.2 | loop fusion | flops 20250 | bytes 40500 | tf_op jit(solution)/shard_map/stack | solution.py:781
  4.3 0.0 copy-start.12
  4.4 0.0 copy-start.15
  4.4 1.1 %shard_map.199 = (f32[15,48,128]{2,1,0:T(8,128)S(1)}, f32[15,48,128]{2,1,0:T(8,128)S(1)}, f32[15,48,128]{2,1,0:T(8,128)S(1)}, f32[15,24,128]{2,1,0:T(8,128)S(1)}...) custom-call(bf16[3,15,15,15]{3,2,1,0:T(8,128)(2,1)S(1)} %pad_maximum, ...), custom_call_target="tpu_custom_call" | custom-call | tf_op jit(solution)/shard_map/pallas_call | solution.py:695
  5.5 2.9 %collective-permute-done.1.got_b = bf16[24,32,128]{2,1,0:T(8,128)(2,1)S(1)} collective-permute-done((bf16[24,32,128]{2,1,0:T(8,128)(2,1)S(1)}, bf16[24,32,128]{2,1,0:T(8,128)(2,1)S(1)}, u32[]{:S(2)}, u32[]{:S(2)}) %collective-permute-start.1) | collective-permute-done | bytes 196640 | tf_op jit(solution)/shard_map/ppermute | solution.py:729
  8.4 0.0 copy-start.1
  8.4 0.0 copy-start.7
  8.5 0.8 %shard_map.200 = (bf16[24,80,128]{2,1,0:T(8,128)(2,1)S(1)}, bf16[15,32,128]{2,1,0:T(8,128)(2,1)S(1)}, bf16[1040,128]{1,0:T(8,128)(2,1)S(1)}, bf16[1040,128]{1,0:...) custom-call(f32[24,64,128]{2,1,0:T(8,128)S(1)} %copy-done, ...), custom_call_target="tpu_custom_call" | custom-call | tf_op jit(solution)/shard_map/pallas_call | solution.py:695
  9.2 1.6 %collective-permute-start.2 = (bf16[1040,128]{1,0:T(8,128)(2,1)S(1)}, bf16[1040,128]{1,0:T(8,128)(2,1)S(1)}, u32[]{:S(2)}, u32[]{:S(2)}) collective-permute-start(bf16[1040,128]{1,0:T(8,128)(2,1)S(1)} %get-tuple-element.42), channel_id=1, source_target_pairs={{0,4},{8,12},{16,20},{24,28},{4,0},{12,8},{20,16},{28,24},{1,5},{9... | collective-permute-start | bytes 798728 | tf_op jit(solution)/shard_map/ppermute | solution.py:729
  10.8 2.3 %collective-permute-start.3 = (bf16[1040,128]{1,0:T(8,128)(2,1)S(1)}, bf16[1040,128]{1,0:T(8,128)(2,1)S(1)}, u32[]{:S(2)}, u32[]{:S(2)}) collective-permute-start(bf16[1040,128]{1,0:T(8,128)(2,1)S(1)} %get-tuple-element.43), channel_id=1, source_target_pairs={{4,8},{12,16},{20,24},{8,4},{16,12},{24,20},{5,9},{13,17},{21,25},... | collective-permute-start | bytes 798728 | tf_op jit(solution)/shard_map/ppermute | solution.py:729
  13.1 0.1 collective-permute-start.4
  13.2 5.0 %collective-permute-start.5 = (bf16[5,32,128]{2,1,0:T(8,128)(2,1)S(1)}, bf16[5,32,128]{2,1,0:T(8,128)(2,1)S(1)}, u32[]{:S(2)}, u32[]{:S(2)}) collective-permute-start(bf16[5,32,128]{2,1,0:T(8,128)(2,1)S(1)} %get-tuple-element.45), channel_id=1, source_target_pairs={{8,16},{12,20},{16,8},{20,12},{9,17},{13,21},{17,9},{21,13},{10,18... | collective-permute-start | bytes 122888 | tf_op jit(solution)/shard_map/ppermute | solution.py:729
  18.3 0.0 copy-start.2
  18.3 0.0 copy-start.3
  18.3 0.0 copy-start.8
  18.3 0.0 copy-start.10
  18.3 1.4 %shard_map.201 = (f32[24,48,128]{2,1,0:T(8,128)S(1)}, f32[24,48,128]{2,1,0:T(8,128)S(1)}) custom-call(bf16[24,80,128]{2,1,0:T(8,128)(2,1)S(1)} %get-tuple-element.28.near, bf16[80,160]{1,0:T(8,128)(2,1)S(1)} %copy-done.7, bf16[384,512]{1,0:T(8,128)(2,1)S(1)} %copy-done.1), custom_call_target="tpu_custom_call" | custom-call | tf_op jit(solution)/shard_map/pallas_call | solution.py:695
  19.7 0.0 copy-start.5
  19.7 0.0 copy-start.6
  19.8 0.0 copy-start.9
  19.8 0.0 copy-start.11
  19.8 0.0 copy-start.13
  19.8 0.0 copy-start.14
  19.8 0.0 copy-start.16
  19.8 3.1 %shard_map.202 = (f32[24,48,128]{2,1,0:T(8,128)S(1)}, f32[24,48,128]{2,1,0:T(8,128)S(1)}, f32[10,64,128]{2,1,0:T(8,128)S(1)}, f32[13,24,128]{2,1,0:T(8,128)S(1)}, f32[13,24,128]{2,1,0:T(8,128)S(1)}) custom-call(f32[24,48,128]{2,1,0:T(8,128)S(1)} %get-tuple-element.29.real, f32[24,48,128]{2,1,0:T(8,128)S(1)} %get-tuple-element.30.imag, ...), custom_call_target="tpu_custom_call" | custom-call | tf_op jit(solution)/shard_map/pallas_call | solution.py:695
  22.9 0.0 copy-start.17
  23.0 0.6 %copy-done.17 = bf16[32,64]{1,0:T(8,128)(2,1)S(1)} copy-done((bf16[32,64]{1,0:T(8,128)(2,1)S(1)}, bf16[32,64]{1,0:T(8,128)(2,1)}, u32[]{:S(2)}) %copy-start.17) | copy-done | bytes 4120
  23.6 5.0 %shard_map.203 = f32[24,64,128]{2,1,0:T(8,128)} custom-call(f32[24,48,128]{2,1,0:T(8,128)S(1)} %get-tuple-element.37.part_real, f32[24,48,128]{2,1,0:T(8,128)S(1)} %get-tuple-element.38.part_imag, f32[10,64,128]{2,1,0:T(8,128)S(1)} %get-tuple-element.39.whole, f32[13,24,128]{2,1,0:T(8,128)S(1)} %get-tuple-element.40.m_part_real, ...), custom_call_target="tpu_custom_call" | custom-call | tf_op jit(solution)/shard_map/pallas_call | solution.py:695
  (27 shorter events, 0.1 us)
Async XLA Ops:
  0.0 3.4 %copy-start.18 = (bf16[15,15,15]{2,1,0:T(8,128)(2,1)S(1)}, bf16[15,15,15]{2,1,0:T(8,128)(2,1)}, u32[]{:S(2)}) copy-start(bf16[15,15,15]{2,1,0:T(8,128)(2,1)} %param.24) | copy-start | bytes 20254
  0.0 3.4 %copy-start.19 = (bf16[15,15,15]{2,1,0:T(8,128)(2,1)S(1)}, bf16[15,15,15]{2,1,0:T(8,128)(2,1)}, u32[]{:S(2)}) copy-start(bf16[15,15,15]{2,1,0:T(8,128)(2,1)} %param.23) | copy-start | bytes 20254
  0.0 8.4 %copy-start = (f32[24,64,128]{2,1,0:T(8,128)S(1)}, f32[24,64,128]{2,1,0:T(8,128)}, u32[]{:S(2)}) copy-start(f32[24,64,128]{2,1,0:T(8,128)} %own.1) | copy-start | bytes 2359300
  1.3 3.1 %copy-start.4 = (bf16[128,1024]{1,0:T(8,128)(2,1)S(1)}, bf16[128,1024]{1,0:T(8,128)(2,1)}, u32[]{:S(2)}) copy-start(bf16[128,1024]{1,0:T(8,128)(2,1)} %constant.50.clone.refs_1_) | copy-start | bytes 786436
  1.3 7.1 %collective-permute-start.1 = (bf16[24,32,128]{2,1,0:T(8,128)(2,1)S(1)}, bf16[24,32,128]{2,1,0:T(8,128)(2,1)S(1)}, u32[]{:S(2)}, u32[]{:S(2)}) collective-permute-start(bf16[24,32,128]{2,1,0:T(8,128)(2,1)S(1)} %get-tuple-element.49), channel_id=1, source_target_pairs={{1,2},{2,1},{5,6},{6,5},{9,10},{10,9},{13,14},{14,13},{17,18},{18,... | collective-permute-start | bytes 589832 | tf_op jit(solution)/shard_map/ppermute | solution.py:729
  3.4 5.1 %collective-permute-start = (bf16[24,32,128]{2,1,0:T(8,128)(2,1)S(1)}, bf16[24,32,128]{2,1,0:T(8,128)(2,1)S(1)}, u32[]{:S(2)}, u32[]{:S(2)}) collective-permute-start(bf16[24,32,128]{2,1,0:T(8,128)(2,1)S(1)} %get-tuple-element.50), channel_id=1, source_target_pairs={{0,1},{2,3},{1,0},{3,2},{4,5},{6,7},{5,4},{7,6},{8,9},{10,11},{9,8... | collective-permute-start | bytes 589832 | tf_op jit(solution)/shard_map/ppermute | solution.py:729
  4.3 4.1 %copy-start.12 = (bf16[256,128]{1,0:T(8,128)(2,1)S(1)}, bf16[256,128]{1,0:T(8,128)(2,1)}, u32[]{:S(2)}) copy-start(bf16[256,128]{1,0:T(8,128)(2,1)} %constant.51.clone.down_z) | copy-start | bytes 196612
  4.4 4.1 %copy-start.15 = (bf16[64,160]{1,0:T(8,128)(2,1)S(1)}, bf16[64,160]{1,0:T(8,128)(2,1)}, u32[]{:S(2)}) copy-start(bf16[64,160]{1,0:T(8,128)(2,1)} %constant.52.clone.down_y) | copy-start | bytes 61444
  8.4 9.8 %copy-start.1 = (bf16[384,512]{1,0:T(8,128)(2,1)S(1)}, bf16[384,512]{1,0:T(8,128)(2,1)}, u32[]{:S(2)}) copy-start(bf16[384,512]{1,0:T(8,128)(2,1)} %constant.54.clone.to_z) | copy-start | bytes 1179652
  8.4 9.8 %copy-start.7 = (bf16[80,160]{1,0:T(8,128)(2,1)S(1)}, bf16[80,160]{1,0:T(8,128)(2,1)}, u32[]{:S(2)}) copy-start(bf16[80,160]{1,0:T(8,128)(2,1)} %constant.53.clone.to_y) | copy-start | bytes 76804
  9.2 13.7 %collective-permute-start.2 = (bf16[1040,128]{1,0:T(8,128)(2,1)S(1)}, bf16[1040,128]{1,0:T(8,128)(2,1)S(1)}, u32[]{:S(2)}, u32[]{:S(2)}) collective-permute-start(bf16[1040,128]{1,0:T(8,128)(2,1)S(1)} %get-tuple-element.42), channel_id=1, source_target_pairs={{0,4},{8,12},{16,20},{24,28},{4,0},{12,8},{20,16},{28,24},{1,5},{9... | collective-permute-start | bytes 798728 | tf_op jit(solution)/shard_map/ppermute | solution.py:729
  10.8 12.2 %collective-permute-start.3 = (bf16[1040,128]{1,0:T(8,128)(2,1)S(1)}, bf16[1040,128]{1,0:T(8,128)(2,1)S(1)}, u32[]{:S(2)}, u32[]{:S(2)}) collective-permute-start(bf16[1040,128]{1,0:T(8,128)(2,1)S(1)} %get-tuple-element.43), channel_id=1, source_target_pairs={{4,8},{12,16},{20,24},{8,4},{16,12},{24,20},{5,9},{13,17},{21,25},... | collective-permute-start | bytes 798728 | tf_op jit(solution)/shard_map/ppermute | solution.py:729
  13.1 9.8 %collective-permute-start.4 = (bf16[5,32,128]{2,1,0:T(8,128)(2,1)S(1)}, bf16[5,32,128]{2,1,0:T(8,128)(2,1)S(1)}, u32[]{:S(2)}, u32[]{:S(2)}) collective-permute-start(bf16[5,32,128]{2,1,0:T(8,128)(2,1)S(1)} %get-tuple-element.44), channel_id=1, source_target_pairs={{0,8},{4,12},{16,24},{20,28},{8,0},{12,4},{24,16},{28,20},{1,9},{5... | collective-permute-start | bytes 122888 | tf_op jit(solution)/shard_map/ppermute | solution.py:729
  13.2 9.7 %collective-permute-start.5 = (bf16[5,32,128]{2,1,0:T(8,128)(2,1)S(1)}, bf16[5,32,128]{2,1,0:T(8,128)(2,1)S(1)}, u32[]{:S(2)}, u32[]{:S(2)}) collective-permute-start(bf16[5,32,128]{2,1,0:T(8,128)(2,1)S(1)} %get-tuple-element.45), channel_id=1, source_target_pairs={{8,16},{12,20},{16,8},{20,12},{9,17},{13,21},{17,9},{21,13},{10,18... | collective-permute-start | bytes 122888 | tf_op jit(solution)/shard_map/ppermute | solution.py:729
  18.3 1.4 %copy-start.2 = (bf16[768,256]{1,0:T(8,128)(2,1)S(1)}, bf16[768,256]{1,0:T(8,128)(2,1)}, u32[]{:S(2)}) copy-start(bf16[768,256]{1,0:T(8,128)(2,1)} %constant.55.clone.from_z) | copy-start | bytes 1179652
  18.3 1.4 %copy-start.3 = (bf16[384,256]{1,0:T(8,128)(2,1)S(1)}, bf16[384,256]{1,0:T(8,128)(2,1)}, u32[]{:S(2)}) copy-start(bf16[384,256]{1,0:T(8,128)(2,1)} %constant.58.clone.m_to_z) | copy-start | bytes 589828
  18.3 1.4 %copy-start.8 = (bf16[64,240]{1,0:T(8,128)(2,1)S(1)}, bf16[64,240]{1,0:T(8,128)(2,1)}, u32[]{:S(2)}) copy-start(bf16[64,240]{1,0:T(8,128)(2,1)} %constant.56.clone.from_y) | copy-start | bytes 92164
  18.3 1.4 %copy-start.10 = (bf16[96,64]{1,0:T(8,128)(2,1)S(1)}, bf16[96,64]{1,0:T(8,128)(2,1)}, u32[]{:S(2)}) copy-start(bf16[96,64]{1,0:T(8,128)(2,1)} %constant.57.clone.m_to_y) | copy-start | bytes 36868
  19.7 3.2 %copy-start.5 = (bf16[384,256]{1,0:T(8,128)(2,1)S(1)}, bf16[384,256]{1,0:T(8,128)(2,1)}, u32[]{:S(2)}) copy-start(bf16[384,256]{1,0:T(8,128)(2,1)} %constant.65.clone.t_from_z) | copy-start | bytes 589828
  19.7 3.2 %copy-start.6 = (bf16[384,256]{1,0:T(8,128)(2,1)S(1)}, bf16[384,256]{1,0:T(8,128)(2,1)}, u32[]{:S(2)}) copy-start(bf16[384,256]{1,0:T(8,128)(2,1)} %constant.59.clone.m_from_z) | copy-start | bytes 589828
  19.8 3.2 %copy-start.9 = (bf16[512,32]{1,0:T(8,128)(2,1)S(1)}, bf16[512,32]{1,0:T(8,128)(2,1)}, u32[]{:S(2)}) copy-start(bf16[512,32]{1,0:T(8,128)(2,1)} %constant.62.clone.t_down_z) | copy-start | bytes 98308
  19.8 3.2 %copy-start.11 = (bf16[2,64,144]{2,1,0:T(8,128)(2,1)S(1)}, bf16[2,64,144]{2,1,0:T(8,128)(2,1)}, u32[]{:S(2)}) copy-start(bf16[2,64,144]{2,1,0:T(8,128)(2,1)} %constant.60.clone.m_from_y) | copy-start | bytes 110596
  19.8 3.2 %copy-start.13 = (bf16[96,256]{1,0:T(8,128)(2,1)S(1)}, bf16[96,256]{1,0:T(8,128)(2,1)}, u32[]{:S(2)}) copy-start(bf16[96,256]{1,0:T(8,128)(2,1)} %constant.64.clone.t_to_z) | copy-start | bytes 147460
  19.8 3.2 %copy-start.14 = (bf16[2,64,96]{2,1,0:T(8,128)(2,1)S(1)}, bf16[2,64,96]{2,1,0:T(8,128)(2,1)}, u32[]{:S(2)}) copy-start(bf16[2,64,96]{2,1,0:T(8,128)(2,1)} %constant.66.clone.t_from_y) | copy-start | bytes 73732
  19.8 3.2 %copy-start.16 = (bf16[64,64]{1,0:T(8,128)(2,1)S(1)}, bf16[64,64]{1,0:T(8,128)(2,1)}, u32[]{:S(2)}) copy-start(bf16[64,64]{1,0:T(8,128)(2,1)} %constant.61.clone.t_down_y) | copy-start | bytes 24580
  22.9 0.7 %copy-start.17 = (bf16[32,64]{1,0:T(8,128)(2,1)S(1)}, bf16[32,64]{1,0:T(8,128)(2,1)}, u32[]{:S(2)}) copy-start(bf16[32,64]{1,0:T(8,128)(2,1)} %constant.63.clone.t_to_y) | copy-start | bytes 12292
